TPU v7x, 32 devices: a whole 2x2x4 slice. The times are simulated.
32 devices in a mesh: ulysses: 2 (over y), blk: 16 (over z, x, core).
Axes of the slice: x: 2, y: 2, z: 4, core: 2. Of those that a mesh axis runs over, the one named last changes fastest.
Arguments:
- query_first: bfloat16 [32, 64, 2, 128], P('blk', None, 'ulysses'), may hold values from -6 to 6
- query_second: bfloat16 [32, 64, 2, 128], P('blk', None, 'ulysses'), may hold values from -6 to 6
- key_first: bfloat16 [32, 64, 2, 128], P('blk', None, 'ulysses'), may hold values from -6 to 6
- key_second: bfloat16 [32, 64, 2, 128], P('blk', None, 'ulysses'), may hold values from -6 to 6
- values: bfloat16 [32, 64, 2, 256], P('blk', None, 'ulysses'), may hold values from -6 to 6
- out_first: bfloat16 [32, 64, 2, 256], P('blk', None, 'ulysses'), may hold values from -6 to 6, as said below
- out_second: bfloat16 [32, 64, 2, 256], P('blk', None, 'ulysses'), may hold values from -6 to 6, as said below
- log_totals: float32 [2, 2, 32, 64], P('ulysses', None, 'blk'), as said below
- lambdas: float32 [2], P('ulysses'), may hold values from 0.1 to 0.8
- norm_gain: float32 [2, 256], P('ulysses'), may hold values from 0.1 to 1.9
- cotangent: bfloat16 [32, 64, 2, 256], P('blk', 'ulysses'), may hold values from -6 to 6
- block_of: int32 [32], replicated, may hold values from 0 to 31, as said below
Outputs:
- grad_query_first: bfloat16 [32, 64, 2, 128], P('blk', None, 'ulysses')
- grad_query_second: bfloat16 [32, 64, 2, 128], P('blk', None, 'ulysses')
- grad_key_first: bfloat16 [32, 64, 2, 128], P('blk', None, 'ulysses')
- grad_key_second: bfloat16 [32, 64, 2, 128], P('blk', None, 'ulysses')
- grad_values: bfloat16 [32, 64, 2, 256], P('blk', None, 'ulysses')
Inputs may be any that keep to these rules, and one draw needn't show every extreme that they name: `block_of`: slots 2d and 2d + 1 hold blocks c_d and 31 - c_d, where c_0 to c_last form a permutation of 0 to 15. `out_first`: the causal softmax average of values under the first pair's scaled scores, normalised over visible keys, rounded to bfloat16. `out_second`: likewise for the second pair. log_totals[h, 0] and log_totals[h, 1] are the logarithms of the sums over visible keys of exp of the first and second pair's scaled scores.
All inputs are finite; a program needn't handle non-finite values.
Results may differ from a plain program's by a relative error of at most 0.0085.
Values may be sent and summed in bfloat16 or wider, within the bound.
No kernel may reach another device: no remote copies, remote signals or barrier semaphores. Data moves between devices by JAX's collectives and lax.ppermute only.
A program may use at most 64 MiB of HBM per device.

v0:
```python
import functools
import math

import jax
import jax.numpy as jnp
from jax import lax
from jax.experimental import pallas as pl
from jax.experimental.pallas import tpu as pltpu
from jax.sharding import PartitionSpec as P


norm_eps = 1e-05
VMEM = pltpu.VMEM
SMEM = pltpu.SMEM
f32 = jnp.float32
bf16 = jnp.bfloat16


def span(bits):
    masks = [0]
    for bit in bits:
        masks = masks + [mask ^ bit for mask in masks]
    return masks


def group_bits(shards):
    width = shards.bit_length() - 1
    bits = [1 << place for place in range(width)]
    middle = bits[1:-1]
    take = (width + 1) // 2
    key_bits = middle[:take]
    query_bits = [bit for bit in bits[::-1] if bit not in key_bits]
    return query_bits, key_bits


def send(member, mask, shards):
    return lax.ppermute(member, "blk", [(place, place ^ mask) for place in range(shards)])


def in_vmem(count):
    return [pl.BlockSpec(memory_space=VMEM)] * count


def in_smem(count):
    return [pl.BlockSpec(memory_space=SMEM)] * count


def three_parts(exact):
    high = exact.astype(bf16)
    rest = exact - high.astype(f32)
    middle = rest.astype(bf16)
    low = (rest - middle.astype(f32)).astype(bf16)
    return high, middle, low


def grad_out_kernel(place, lam, own_ref, other_ref, one_ref, two_ref, gain_ref, log_ref, pack_ref):
    rows, width = one_ref.shape
    first = place[0] == 0
    own = jnp.where(first, own_ref[:, :, 0, :].astype(f32), own_ref[:, :, 1, :].astype(f32))
    other = jnp.where(first, other_ref[:, :, 0, :].astype(f32), other_ref[:, :, 1, :].astype(f32))
    upper = jnp.where(first, own, other)
    lower = jnp.where(first, other, own)
    grad_y = jnp.concatenate([upper, lower], axis=1).reshape(rows, width)
    one = one_ref[...].astype(f32)
    two = two_ref[...].astype(f32)
    combined = one - lam[0] * two
    inv_rms = lax.rsqrt(jnp.mean(combined * combined, axis=1, keepdims=True) + norm_eps)
    gained = gain_ref[...] * grad_y
    centre = jnp.mean(combined * gained, axis=1, keepdims=True)
    grad_out = (inv_rms * (gained - combined * inv_rms * inv_rms * centre)).astype(bf16)
    pack_ref[:rows, :] = grad_out
    wide = grad_out.astype(f32)

    def as_row(column):
        return jnp.transpose(jnp.broadcast_to(column, (rows, rows)))[:1, :]

    dot_one = as_row(jnp.sum(wide * one, axis=1, keepdims=True))
    dot_two = as_row(jnp.sum(wide * two, axis=1, keepdims=True))
    wide_logs = jnp.concatenate(
        [log_ref[side, slot : slot + 1, :] for side in range(2) for slot in range(log_ref.shape[1])], axis=1
    )
    wide_dots = jnp.concatenate([dot_one, dot_two], axis=1)
    parts = three_parts(wide_logs) + three_parts(wide_dots)
    filler = jnp.zeros((pack_ref.shape[0] - rows - len(parts), width), f32)
    pack_ref[rows:, :] = jnp.concatenate([part.astype(f32) for part in parts] + [filler], axis=0).astype(
        bf16
    )


def tile_kernel(scale, block_len, q_masks, k_masks, keep, table, me, lam, *refs):
    nq, nk = len(q_masks), len(k_masks)
    q_refs, refs = refs[:nq], refs[nq:]
    do_refs, refs = refs[:nq], refs[nq:]
    k_refs, refs = refs[:nk], refs[nk:]
    dq_keep, dq_send, dkv_own = refs[:3]
    dkv_out = refs[3:]
    rows = q_refs[0].shape[0]
    kw = q_refs[0].shape[1] // 2
    lam0 = lam[0]

    def places(mask, axis):
        shard = jnp.bitwise_xor(me[0], mask)
        low = table[2 * shard] * block_len
        high = (table[2 * shard + 1] - 1) * block_len
        shape = (rows, 1) if axis == 0 else (1, rows)
        offset = lax.broadcasted_iota(jnp.int32, shape, axis)
        return offset + jnp.where(offset < block_len, low, high)

    contract = (((1,), (1,)), ((), ()))
    along_keys = (((0,), (0,)), ((), ()))
    q_one = jnp.concatenate([ref[:, :kw] for ref in q_refs], axis=0)
    q_two = jnp.concatenate([ref[:, kw:] for ref in q_refs], axis=0)
    grad = jnp.concatenate([ref[:rows, :] for ref in do_refs], axis=0)
    q_pos = jnp.concatenate([places(mask, 1) for mask in q_masks], axis=1)

    def stat(row, side):
        pieces = []
        for ref in do_refs:
            block = ref[rows:, side * rows : (side + 1) * rows].astype(f32)
            pieces.append(block[row : row + 1] + block[row + 1 : row + 2] + block[row + 2 : row + 3])
        return jnp.concatenate(pieces, axis=1)

    log_one, log_two = stat(0, 0), stat(0, 1)
    dot_one, dot_two = stat(3, 0), stat(3, 1)
    dq_one = None
    dq_two = None
    for j, mask in enumerate(k_masks):
        k_one, k_two, val = k_refs[j][:, :kw], k_refs[j][:, kw : 2 * kw], k_refs[j][:, 2 * kw :]
        visible = places(mask, 0) <= q_pos
        s_one = lax.dot_general(k_one, q_one, contract, preferred_element_type=f32)
        s_two = lax.dot_general(k_two, q_two, contract, preferred_element_type=f32)
        d_attn = lax.dot_general(val, grad, contract, preferred_element_type=f32)
        p_one = jnp.exp(jnp.where(visible, s_one * scale - log_one, -jnp.inf))
        p_two = lam0 * jnp.exp(jnp.where(visible, s_two * scale - log_two, -jnp.inf))
        g_one = (p_one * (d_attn - dot_one)).astype(bf16)
        g_two = (p_two * (dot_two - d_attn)).astype(bf16)
        mix = (p_one - p_two).astype(bf16)
        dkv = dkv_own if mask == 0 else dkv_out[j - 1]
        dkv[:, :kw] = jnp.dot(g_one, q_one, preferred_element_type=f32).astype(dkv.dtype)
        dkv[:, kw : 2 * kw] = jnp.dot(g_two, q_two, preferred_element_type=f32).astype(dkv.dtype)
        dkv[:, 2 * kw :] = jnp.dot(mix, grad, preferred_element_type=f32).astype(dkv.dtype)
        one = lax.dot_general(g_one, k_one, along_keys, preferred_element_type=f32)
        two = lax.dot_general(g_two, k_two, along_keys, preferred_element_type=f32)
        dq_one = one if dq_one is None else dq_one + one
        dq_two = two if dq_two is None else dq_two + two
    kept = 0
    sent = 0
    for i, mask in enumerate(q_masks):
        part = slice(i * rows, (i + 1) * rows)
        if mask in keep:
            dq_keep[kept * rows : (kept + 1) * rows, :kw] = dq_one[part]
            dq_keep[kept * rows : (kept + 1) * rows, kw:] = dq_two[part]
            kept += 1
        else:
            dq_send[sent * rows : (sent + 1) * rows, :kw] = dq_one[part].astype(bf16)
            dq_send[sent * rows : (sent + 1) * rows, kw:] = dq_two[part].astype(bf16)
            sent += 1


def final_kernel(scale, count, dq_ref, dq_in, own_ref, *refs):
    dkv_in, outs = refs[:count], refs[count:]
    kw = outs[0].shape[1]
    dq = (dq_ref[...] + dq_in[...].astype(f32)) * scale
    outs[0][...] = dq[:, :kw].astype(bf16)
    outs[1][...] = dq[:, kw:].astype(bf16)
    total = own_ref[...]
    for ref in dkv_in:
        total = total + ref[...].astype(f32)
    outs[2][...] = (total[:, :kw] * scale).astype(bf16)
    outs[3][...] = (total[:, kw : 2 * kw] * scale).astype(bf16)
    outs[4][...] = total[:, 2 * kw :].astype(bf16)


def one_device(
    shards,
    ranks,
    query_first,
    query_second,
    key_first,
    key_second,
    values,
    out_first,
    out_second,
    log_totals,
    lambdas,
    norm_gain,
    cotangent,
    block_of,
):
    slot_count, block_len, heads_here, value_width = values.shape
    key_width = query_first.shape[3]
    rows = slot_count * block_len
    scale = 1.0 / math.sqrt(key_width)
    assert heads_here == 1 and slot_count == 2 and shards == 1 << (shards.bit_length() - 1)
    q_bits, k_bits = group_bits(shards)
    me = lax.axis_index("blk")
    rank = lax.axis_index("ulysses")
    me_one = me.reshape(1).astype(jnp.int32)

    def flat(member):
        return member.reshape(rows, member.shape[3])

    if ranks == 2:
        own_half = cotangent
        other_half = lax.ppermute(cotangent, "ulysses", [(0, 1), (1, 0)])
        place = rank.reshape(1).astype(jnp.int32)
    else:
        whole = lax.all_to_all(cotangent, "ulysses", split_axis=2, concat_axis=1, tiled=True)
        whole = jnp.concatenate([whole, whole], axis=2)
        own_half, other_half = whole[:, : block_len // 2], whole[:, block_len // 2 :]
        place = jnp.zeros((1,), jnp.int32)

    key_pack = jnp.concatenate([flat(key_first), flat(key_second), flat(values)], axis=1)
    query_pack = jnp.concatenate([flat(query_first), flat(query_second)], axis=1)
    k_masks = span(k_bits)
    keys = {0: key_pack}
    for mask in k_masks[:0:-1]:
        keys[mask] = send(key_pack, mask, shards)

    def spread(member):
        held = {0: member}
        for bit in q_bits:
            for mask in list(held):
                held[mask ^ bit] = send(held[mask], bit, shards)
        return held

    queries = spread(query_pack)
    pack_rows = rows + 16
    grad_pack = pl.pallas_call(
        grad_out_kernel,
        out_shape=jax.ShapeDtypeStruct((pack_rows, value_width), bf16),
        in_specs=in_smem(2) + in_vmem(6),
        out_specs=pl.BlockSpec(memory_space=VMEM),
        compiler_params=pltpu.CompilerParams(vmem_limit_bytes=4 << 20),
        name="grad_out",
    )(
        place,
        lambdas,
        own_half,
        other_half,
        flat(out_first),
        flat(out_second),
        norm_gain,
        log_totals.reshape(2, slot_count, block_len),
    )
    grads = spread(grad_pack)

    q_masks = span(q_bits)
    last = q_bits[-1]
    keep = [mask for mask in q_masks if not mask & last]
    half_count = len(q_masks) // 2
    nk = len(k_masks)
    width = 2 * key_width + value_width
    results = pl.pallas_call(
        functools.partial(tile_kernel, scale, block_len, q_masks, k_masks, keep),
        out_shape=[
            jax.ShapeDtypeStruct((half_count * rows, 2 * key_width), f32),
            jax.ShapeDtypeStruct((half_count * rows, 2 * key_width), bf16),
            jax.ShapeDtypeStruct((rows, width), f32),
        ]
        + [jax.ShapeDtypeStruct((rows, width), bf16)] * (nk - 1),
        in_specs=in_smem(3) + in_vmem(2 * len(q_masks) + nk),
        out_specs=in_vmem(2 + nk),
        compiler_params=pltpu.CompilerParams(vmem_limit_bytes=16 << 20),
        name="tile",
    )(
        block_of,
        me_one,
        lambdas,
        *[queries[mask] for mask in q_masks],
        *[grads[mask] for mask in q_masks],
        *[keys[mask] for mask in k_masks],
    )
    dq_keep, dq_send, dkv_own = results[:3]
    dkv_parts = results[3:]
    dkv_in = [None] * (nk - 1)
    for j in range(nk - 1, 0, -1):
        dkv_in[j - 1] = send(dkv_parts[j - 1], k_masks[j], shards)
    arrived = send(dq_send, last, shards)
    kept = dq_keep + arrived.astype(f32)
    for bit in q_bits[-2::-1]:
        size = kept.shape[0] // 2
        if bit == q_bits[0]:
            dq_in = send(kept[size:].astype(bf16), bit, shards)
            kept = kept[:size]
        else:
            kept = kept[:size] + send(kept[size:].astype(bf16), bit, shards).astype(f32)
    outs = pl.pallas_call(
        functools.partial(final_kernel, scale, nk - 1),
        out_shape=[jax.ShapeDtypeStruct((rows, key_width), bf16)] * 4
        + [jax.ShapeDtypeStruct((rows, value_width), bf16)],
        in_specs=in_vmem(3 + nk - 1),
        out_specs=in_vmem(5),
        compiler_params=pltpu.CompilerParams(vmem_limit_bytes=4 << 20),
        name="final",
    )(kept, dq_in, dkv_own, *dkv_in)
    return tuple(
        out.reshape(slot_count, block_len, heads_here, out.shape[1]) for out in outs
    )


def solution(mesh):
    rows_spec = P("blk", None, "ulysses", None)
    in_specs = (rows_spec,) * 7 + (
        P("ulysses", None, "blk", None),
        P("ulysses"),
        P("ulysses", None),
        P("blk", "ulysses", None, None),
        P(),
    )
    shards = mesh.shape["blk"]
    body = functools.partial(one_device, shards, mesh.shape["ulysses"])
    return jax.shard_map(
        body, mesh=mesh, in_specs=in_specs, out_specs=(rows_spec,) * 5, check_vma=False
    )
```

profile of v0, /device:TPU:0, one launch (start us, length us, event | category | flops | bytes accessed | tf_op | source)
XLA Modules:
  0.0 36.0 jit_solution(1646215626222447999)
XLA Ops:
  0.6 3.1 %collective-permute-start.3 = (bf16[2,32,2,256]{3,2,1,0:T(2,128)(2,1)}, bf16[2,32,2,256]{3,2,1,0:T(2,128)(2,1)S(1)}, u32[]{:S(2)}, u32[]{:S(2)}) collective-permute-start(bf16[2,32,2,256]{3,2,1,0:T(2,128)(2,1)} %own_ref.1), channel_id=1, source_target_pairs={{0,16},{16,0},{1,17},{17,1},{2,18},{18,2},{3,19},{19,3},{4,20},{20... | collective-permute-start | bytes 196616 | tf_op jit(solution)/shard_map/ppermute | solution.py:205
  3.7 0.0 copy-start
  3.7 0.0 copy-start.1
  3.7 0.8 %pad_maximum_fusion.1.refs_0_ = bf16[128,256]{1,0:T(8,128)(2,1)S(1)} fusion(bf16[128,128]{1,0:T(8,128)(2,1)} %bitcast.29, bf16[128,128]{1,0:T(8,128)(2,1)} %bitcast.30), kind=kLoop, calls=%fused_computation.3 | loop fusion | flops 131072 | bytes 131072 | tf_op jit(solution)/shard_map/concatenate | solution.py:214
  4.5 2.6 %collective-permute-start = (bf16[128,256]{1,0:T(8,128)(2,1)S(1)}, bf16[128,256]{1,0:T(8,128)(2,1)S(1)}, u32[]{:S(2)}, u32[]{:S(2)}) collective-permute-start(bf16[128,256]{1,0:T(8,128)(2,1)S(1)} %pad_maximum_fusion.1.refs_0_), channel_id=1, source_target_pairs={{0,8},{1,9},{2,10},{3,11},{4,12},{5,13},{6,14},{7,15},{8,0},{9,1},... | collective-permute-start | bytes 196616 | tf_op jit(solution)/shard_map/ppermute | solution.py:37
  7.2 0.0 collective-permute-start.1
  7.8 0.0 collective-permute-done.3.other_ref
  7.8 0.0 copy-start.3
  7.8 0.0 copy-start.4
  7.9 0.0 copy-done
  7.9 0.0 copy-done.1
  7.9 0.6 %copy-done.3 = f32[1,2,2,64]{3,2,1,0:T(2,128)S(1)} copy-done((f32[1,2,2,64]{3,2,1,0:T(2,128)S(1)}, f32[1,2,2,64]{3,2,1,0:T(2,128)}, u32[]{:S(2)}) %copy-start.3) | copy-done | bytes 1048
  8.5 0.0 copy-done.4
  8.5 0.0 copy-start.2
  8.5 0.8 %copy-done.2 = bf16[2,64,1,256]{3,1,2,0:T(8,128)(2,1)S(1)} copy-done((bf16[2,64,1,256]{3,1,2,0:T(8,128)(2,1)S(1)}, bf16[2,64,1,256]{3,1,2,0:T(8,128)(2,1)}, u32[]{:S(2)}) %copy-start.2) | copy-done | bytes 65560
  9.4 0.0 copy-start.6
  9.4 0.0 copy-start.7
  9.4 0.0 copy-start.8
  9.4 0.4 %grad_out.1.refs_4_ = bf16[144,256]{1,0:T(8,128)(2,1)S(1)} custom-call(s32[1]{0:T(128)} %bitcast.3.place, f32[1]{0:T(128)S(6)} %copy.22.lam, bf16[2,32,2,256]{3,2,1,0:T(2,128)(2,1)S(1)} %copy-done, bf16[2,32,2,256]{3,2,1,0:T(2,128)(2,1)S(1)} %collective-permute-done.3.other_ref, bf16[128,256]{1,0:T(8,128)(2,1)S(1)} %bitcast.25, ...), custom_call_target="tpu_custom_call" | custom-call | tf_op jit(solution)/shard_map/grad_out/pallas_call | solution.py:229
  9.8 1.5 %collective-permute-start.4 = (bf16[144,256]{1,0:T(8,128)(2,1)S(1)}, bf16[144,256]{1,0:T(8,128)(2,1)S(1)}, u32[]{:S(2)}, u32[]{:S(2)}) collective-permute-start(bf16[144,256]{1,0:T(8,128)(2,1)S(1)} %grad_out.1.refs_4_), channel_id=1, source_target_pairs={{0,8},{1,9},{2,10},{3,11},{4,12},{5,13},{6,14},{7,15},{8,0},{9,1},... | collective-permute-start | bytes 221192 | tf_op jit(solution)/shard_map/ppermute | solution.py:37
  11.2 0.0 collective-permute-done.refs_1_
  11.2 0.0 collective-permute-start.2
  11.2 0.0 copy-done.6
  11.2 0.0 copy-done.7
  11.2 0.0 copy-done.8
  11.3 2.6 %collective-permute-start.9 = (bf16[128,512]{1,0:T(8,128)(2,1)S(1)}, bf16[128,512]{1,0:T(8,128)(2,1)S(1)}, u32[]{:S(2)}, u32[]{:S(2)}) collective-permute-start(bf16[128,512]{1,0:T(8,128)(2,1)S(1)} %pad_maximum_fusion.refs_8_), channel_id=1, source_target_pairs={{0,6},{1,7},{2,4},{3,5},{4,2},{5,3},{6,0},{7,1},{8,14},{9,15},{10,... | collective-permute-start | bytes 393224 | tf_op jit(solution)/shard_map/ppermute | solution.py:37
  13.8 0.4 %collective-permute-start.8 = (bf16[128,512]{1,0:T(8,128)(2,1)S(1)}, bf16[128,512]{1,0:T(8,128)(2,1)S(1)}, u32[]{:S(2)}, u32[]{:S(2)}) collective-permute-start(bf16[128,512]{1,0:T(8,128)(2,1)S(1)} %pad_maximum_fusion.refs_8_), channel_id=1, source_target_pairs={{0,4},{1,5},{2,6},{3,7},{4,0},{5,1},{6,2},{7,3},{8,12},{9,13},{10,... | collective-permute-start | bytes 393224 | tf_op jit(solution)/shard_map/ppermute | solution.py:37
  14.3 0.0 collective-permute-done.1.refs_2_
  14.3 0.5 %collective-permute-start.7 = (bf16[128,512]{1,0:T(8,128)(2,1)S(1)}, bf16[128,512]{1,0:T(8,128)(2,1)S(1)}, u32[]{:S(2)}, u32[]{:S(2)}) collective-permute-start(bf16[128,512]{1,0:T(8,128)(2,1)S(1)} %pad_maximum_fusion.refs_8_), channel_id=1, source_target_pairs={{0,2},{1,3},{2,0},{3,1},{4,6},{5,7},{6,4},{7,5},{8,10},{9,11},{10,... | collective-permute-start | bytes 393224 | tf_op jit(solution)/shard_map/ppermute | solution.py:37
  14.8 0.0 collective-permute-done.2.refs_3_
  14.8 0.0 collective-permute-start.5
  14.8 2.2 %collective-permute-done.4.refs_5_ = bf16[144,256]{1,0:T(8,128)(2,1)S(1)} collective-permute-done((bf16[144,256]{1,0:T(8,128)(2,1)S(1)}, bf16[144,256]{1,0:T(8,128)(2,1)S(1)}, u32[]{:S(2)}, u32[]{:S(2)}) %collective-permute-start.4) | collective-permute-done | bytes 73760 | tf_op jit(solution)/shard_map/ppermute | solution.py:37
  17.1 0.0 collective-permute-start.6
  17.1 0.0 copy-start.5
  17.1 2.1 %collective-permute-done.9.refs_11_ = bf16[128,512]{1,0:T(8,128)(2,1)S(1)} collective-permute-done((bf16[128,512]{1,0:T(8,128)(2,1)S(1)}, bf16[128,512]{1,0:T(8,128)(2,1)S(1)}, u32[]{:S(2)}, u32[]{:S(2)}) %collective-permute-start.9) | collective-permute-done | bytes 131104 | tf_op jit(solution)/shard_map/ppermute | solution.py:37
  19.2 2.3 %collective-permute-done.8.refs_10_ = bf16[128,512]{1,0:T(8,128)(2,1)S(1)} collective-permute-done((bf16[128,512]{1,0:T(8,128)(2,1)S(1)}, bf16[128,512]{1,0:T(8,128)(2,1)S(1)}, u32[]{:S(2)}, u32[]{:S(2)}) %collective-permute-start.8) | collective-permute-done | bytes 131104 | tf_op jit(solution)/shard_map/ppermute | solution.py:37
  21.4 0.0 collective-permute-done.7.refs_9_
  21.5 0.0 collective-permute-done.5.refs_6_
  21.5 0.0 collective-permute-done.6.refs_7_
  21.5 0.0 copy-done.5
  21.5 2.4 %tile.1 = (f32[256,256]{1,0:T(8,128)S(1)}, bf16[256,256]{1,0:T(8,128)(2,1)S(1)}, f32[128,512]{1,0:T(8,128)S(1)}, bf16[128,512]{1,0:T(8,128)(2,1)S(1)}, bf16[128,...) custom-call(s32[32]{0:T(128)S(1)} %copy-done.5, s32[1]{0:T(128)} %bitcast.me, f32[1]{0:T(128)S(6)} %copy.22.lam, ...), custom_call_target="tpu_custom_call" | custom-call | tf_op jit(solution)/shard_map/tile/pallas_call | solution.py:254
  23.9 0.1 collective-permute-start.10
  24.0 1.1 %collective-permute-start.12 = (bf16[128,512]{1,0:T(8,128)(2,1)S(1)}, bf16[128,512]{1,0:T(8,128)(2,1)S(1)}, u32[]{:S(2)}, u32[]{:S(2)}) collective-permute-start(bf16[128,512]{1,0:T(8,128)(2,1)S(1)} %get-tuple-element.19), channel_id=1, source_target_pairs={{0,2},{1,3},{2,0},{3,1},{4,6},{5,7},{6,4},{7,5},{8,10},{9,11},{10,... | collective-permute-start | bytes 393224 | tf_op jit(solution)/shard_map/ppermute | solution.py:37
  25.1 1.5 %collective-permute-start.13 = (bf16[128,512]{1,0:T(8,128)(2,1)S(1)}, bf16[128,512]{1,0:T(8,128)(2,1)S(1)}, u32[]{:S(2)}, u32[]{:S(2)}) collective-permute-start(bf16[128,512]{1,0:T(8,128)(2,1)S(1)} %get-tuple-element.20), channel_id=1, source_target_pairs={{0,4},{1,5},{2,6},{3,7},{4,0},{5,1},{6,2},{7,3},{8,12},{9,13},{10,... | collective-permute-start | bytes 393224 | tf_op jit(solution)/shard_map/ppermute | solution.py:37
  26.6 1.0 %collective-permute-start.14 = (bf16[128,512]{1,0:T(8,128)(2,1)S(1)}, bf16[128,512]{1,0:T(8,128)(2,1)S(1)}, u32[]{:S(2)}, u32[]{:S(2)}) collective-permute-start(bf16[128,512]{1,0:T(8,128)(2,1)S(1)} %get-tuple-element.21), channel_id=1, source_target_pairs={{0,6},{1,7},{2,4},{3,5},{4,2},{5,3},{6,0},{7,1},{8,14},{9,15},{10,... | collective-permute-start | bytes 393224 | tf_op jit(solution)/shard_map/ppermute | solution.py:37
  27.5 0.0 collective-permute-done.10
  27.6 2.1 %collective-permute-start.11 = (bf16[128,256]{1,0:T(8,128)(2,1)S(1)}, bf16[128,256]{1,0:T(8,128)(2,1)S(1)}, u32[]{:S(2)}, u32[]{:S(2)}) collective-permute-start(bf16[128,256]{1,0:T(8,128)(2,1)S(1)} %slice.12), channel_id=1, source_target_pairs={{0,8},{1,9},{2,10},{3,11},{4,12},{5,13},{6,14},{7,15},{8,0},{9,1},... | collective-permute-start | bytes 196616 | tf_op jit(solution)/shard_map/ppermute | solution.py:37
  29.7 0.2 collective-permute-done.12.refs_0_
  29.9 2.3 %collective-permute-done.13.refs_1_ = bf16[128,512]{1,0:T(8,128)(2,1)S(1)} collective-permute-done((bf16[128,512]{1,0:T(8,128)(2,1)S(1)}, bf16[128,512]{1,0:T(8,128)(2,1)S(1)}, u32[]{:S(2)}, u32[]{:S(2)}) %collective-permute-start.13) | collective-permute-done | bytes 131104 | tf_op jit(solution)/shard_map/ppermute | solution.py:37
  32.2 3.1 %collective-permute-done.14.refs_2_ = bf16[128,512]{1,0:T(8,128)(2,1)S(1)} collective-permute-done((bf16[128,512]{1,0:T(8,128)(2,1)S(1)}, bf16[128,512]{1,0:T(8,128)(2,1)S(1)}, u32[]{:S(2)}, u32[]{:S(2)}) %collective-permute-start.14) | collective-permute-done | bytes 131104 | tf_op jit(solution)/shard_map/ppermute | solution.py:37
  35.3 0.0 collective-permute-done.11.dq_in
  35.3 0.7 %final.1 = (bf16[128,128]{1,0:T(8,128)(2,1)}, bf16[128,128]{1,0:T(8,128)(2,1)}, bf16[128,128]{1,0:T(8,128)(2,1)}, bf16[128,128]{1,0:T(8,128)(2,1)}, bf16[128,256]{1,0:T(8,128)(2,1)}) custom-call(f32[128,256]{1,0:T(8,128)S(1)} %slice.9.dq_ref, bf16[128,256]{1,0:T(8,128)(2,1)S(1)} %collective-permute-done.11.dq_in, f32[128,512]{1,0:T(8,128)S(1)} %get-tuple-element.18.own_ref, ...), custom_call_target="tpu_custom_call" | custom-call | tf_op jit(solution)/shard_map/final/pallas_call | solution.py:288
  (4 shorter events, 0.1 us)
Async XLA Ops:
  0.6 7.2 %collective-permute-start.3 = (bf16[2,32,2,256]{3,2,1,0:T(2,128)(2,1)}, bf16[2,32,2,256]{3,2,1,0:T(2,128)(2,1)S(1)}, u32[]{:S(2)}, u32[]{:S(2)}) collective-permute-start(bf16[2,32,2,256]{3,2,1,0:T(2,128)(2,1)} %own_ref.1), channel_id=1, source_target_pairs={{0,16},{16,0},{1,17},{17,1},{2,18},{18,2},{3,19},{19,3},{4,20},{20... | collective-permute-start | bytes 196616 | tf_op jit(solution)/shard_map/ppermute | solution.py:205
  3.7 4.2 %copy-start = (bf16[2,32,2,256]{3,2,1,0:T(2,128)(2,1)S(1)}, bf16[2,32,2,256]{3,2,1,0:T(2,128)(2,1)}, u32[]{:S(2)}) copy-start(bf16[2,32,2,256]{3,2,1,0:T(2,128)(2,1)} %own_ref.1) | copy-start | bytes 196612
  3.7 4.2 %copy-start.1 = (bf16[2,64,1,256]{3,1,2,0:T(8,128)(2,1)S(1)}, bf16[2,64,1,256]{3,1,2,0:T(8,128)(2,1)}, u32[]{:S(2)}) copy-start(bf16[2,64,1,256]{3,1,2,0:T(8,128)(2,1)} %param.17) | copy-start | bytes 196612
  4.5 6.7 %collective-permute-start = (bf16[128,256]{1,0:T(8,128)(2,1)S(1)}, bf16[128,256]{1,0:T(8,128)(2,1)S(1)}, u32[]{:S(2)}, u32[]{:S(2)}) collective-permute-start(bf16[128,256]{1,0:T(8,128)(2,1)S(1)} %pad_maximum_fusion.1.refs_0_), channel_id=1, source_target_pairs={{0,8},{1,9},{2,10},{3,11},{4,12},{5,13},{6,14},{7,15},{8,0},{9,1},... | collective-permute-start | bytes 196616 | tf_op jit(solution)/shard_map/ppermute | solution.py:37
  7.2 7.1 %collective-permute-start.1 = (bf16[128,256]{1,0:T(8,128)(2,1)S(1)}, bf16[128,256]{1,0:T(8,128)(2,1)S(1)}, u32[]{:S(2)}, u32[]{:S(2)}) collective-permute-start(bf16[128,256]{1,0:T(8,128)(2,1)S(1)} %pad_maximum_fusion.1.refs_0_), channel_id=1, source_target_pairs={{0,1},{1,0},{2,3},{3,2},{4,5},{5,4},{6,7},{7,6},{8,9},{9,8},{10,11... | collective-permute-start | bytes 196616 | tf_op jit(solution)/shard_map/ppermute | solution.py:37
  7.8 0.7 %copy-start.3 = (f32[1,2,2,64]{3,2,1,0:T(2,128)S(1)}, f32[1,2,2,64]{3,2,1,0:T(2,128)}, u32[]{:S(2)}) copy-start(f32[1,2,2,64]{3,2,1,0:T(2,128)} %param.19) | copy-start | bytes 3076
  7.8 0.7 %copy-start.4 = (f32[1,256]{1,0:T(1,128)S(1)}, f32[1,256]{1,0:T(1,128)}, u32[]{:S(2)}) copy-start(f32[1,256]{1,0:T(1,128)} %gain_ref.1) | copy-start | bytes 3076
  8.5 0.8 %copy-start.2 = (bf16[2,64,1,256]{3,1,2,0:T(8,128)(2,1)S(1)}, bf16[2,64,1,256]{3,1,2,0:T(8,128)(2,1)}, u32[]{:S(2)}) copy-start(bf16[2,64,1,256]{3,1,2,0:T(8,128)(2,1)} %param.18) | copy-start | bytes 196612
  9.4 1.9 %copy-start.6 = (bf16[2,64,1,256]{3,1,2,0:T(8,128)(2,1)S(1)}, bf16[2,64,1,256]{3,1,2,0:T(8,128)(2,1)}, u32[]{:S(2)}) copy-start(bf16[2,64,1,256]{3,1,2,0:T(8,128)(2,1)} %param.16) | copy-start | bytes 196612
  9.4 1.9 %copy-start.7 = (bf16[2,64,1,128]{3,1,2,0:T(8,128)(2,1)S(1)}, bf16[2,64,1,128]{3,1,2,0:T(8,128)(2,1)}, u32[]{:S(2)}) copy-start(bf16[2,64,1,128]{3,1,2,0:T(8,128)(2,1)} %param.15) | copy-start | bytes 98308
  9.4 1.9 %copy-start.8 = (bf16[2,64,1,128]{3,1,2,0:T(8,128)(2,1)S(1)}, bf16[2,64,1,128]{3,1,2,0:T(8,128)(2,1)}, u32[]{:S(2)}) copy-start(bf16[2,64,1,128]{3,1,2,0:T(8,128)(2,1)} %param.14) | copy-start | bytes 98308
  9.8 7.3 %collective-permute-start.4 = (bf16[144,256]{1,0:T(8,128)(2,1)S(1)}, bf16[144,256]{1,0:T(8,128)(2,1)S(1)}, u32[]{:S(2)}, u32[]{:S(2)}) collective-permute-start(bf16[144,256]{1,0:T(8,128)(2,1)S(1)} %grad_out.1.refs_4_), channel_id=1, source_target_pairs={{0,8},{1,9},{2,10},{3,11},{4,12},{5,13},{6,14},{7,15},{8,0},{9,1},... | collective-permute-start | bytes 221192 | tf_op jit(solution)/shard_map/ppermute | solution.py:37
  11.2 3.6 %collective-permute-start.2 = (bf16[128,256]{1,0:T(8,128)(2,1)S(1)}, bf16[128,256]{1,0:T(8,128)(2,1)S(1)}, u32[]{:S(2)}, u32[]{:S(2)}) collective-permute-start(bf16[128,256]{1,0:T(8,128)(2,1)S(1)} %collective-permute-done.refs_1_), channel_id=1, source_target_pairs={{0,1},{1,0},{2,3},{3,2},{4,5},{5,4},{6,7},{7,6},{8,9},{9,8},{10,11... | collective-permute-start | bytes 196616 | tf_op jit(solution)/shard_map/ppermute | solution.py:37
  11.3 7.9 %collective-permute-start.9 = (bf16[128,512]{1,0:T(8,128)(2,1)S(1)}, bf16[128,512]{1,0:T(8,128)(2,1)S(1)}, u32[]{:S(2)}, u32[]{:S(2)}) collective-permute-start(bf16[128,512]{1,0:T(8,128)(2,1)S(1)} %pad_maximum_fusion.refs_8_), channel_id=1, source_target_pairs={{0,6},{1,7},{2,4},{3,5},{4,2},{5,3},{6,0},{7,1},{8,14},{9,15},{10,... | collective-permute-start | bytes 393224 | tf_op jit(solution)/shard_map/ppermute | solution.py:37
  13.8 7.6 %collective-permute-start.8 = (bf16[128,512]{1,0:T(8,128)(2,1)S(1)}, bf16[128,512]{1,0:T(8,128)(2,1)S(1)}, u32[]{:S(2)}, u32[]{:S(2)}) collective-permute-start(bf16[128,512]{1,0:T(8,128)(2,1)S(1)} %pad_maximum_fusion.refs_8_), channel_id=1, source_target_pairs={{0,4},{1,5},{2,6},{3,7},{4,0},{5,1},{6,2},{7,3},{8,12},{9,13},{10,... | collective-permute-start | bytes 393224 | tf_op jit(solution)/shard_map/ppermute | solution.py:37
  14.3 7.2 %collective-permute-start.7 = (bf16[128,512]{1,0:T(8,128)(2,1)S(1)}, bf16[128,512]{1,0:T(8,128)(2,1)S(1)}, u32[]{:S(2)}, u32[]{:S(2)}) collective-permute-start(bf16[128,512]{1,0:T(8,128)(2,1)S(1)} %pad_maximum_fusion.refs_8_), channel_id=1, source_target_pairs={{0,2},{1,3},{2,0},{3,1},{4,6},{5,7},{6,4},{7,5},{8,10},{9,11},{10,... | collective-permute-start | bytes 393224 | tf_op jit(solution)/shard_map/ppermute | solution.py:37
  14.8 6.6 %collective-permute-start.5 = (bf16[144,256]{1,0:T(8,128)(2,1)S(1)}, bf16[144,256]{1,0:T(8,128)(2,1)S(1)}, u32[]{:S(2)}, u32[]{:S(2)}) collective-permute-start(bf16[144,256]{1,0:T(8,128)(2,1)S(1)} %grad_out.1.refs_4_), channel_id=1, source_target_pairs={{0,1},{1,0},{2,3},{3,2},{4,5},{5,4},{6,7},{7,6},{8,9},{9,8},{10,11... | collective-permute-start | bytes 221192 | tf_op jit(solution)/shard_map/ppermute | solution.py:37
  17.1 4.4 %collective-permute-start.6 = (bf16[144,256]{1,0:T(8,128)(2,1)S(1)}, bf16[144,256]{1,0:T(8,128)(2,1)S(1)}, u32[]{:S(2)}, u32[]{:S(2)}) collective-permute-start(bf16[144,256]{1,0:T(8,128)(2,1)S(1)} %collective-permute-done.4.refs_5_), channel_id=1, source_target_pairs={{0,1},{1,0},{2,3},{3,2},{4,5},{5,4},{6,7},{7,6},{8,9},{9,8},{10,11... | collective-permute-start | bytes 221192 | tf_op jit(solution)/shard_map/ppermute | solution.py:37
  17.1 4.4 %copy-start.5 = (s32[32]{0:T(128)S(1)}, s32[32]{0:T(128)}, u32[]{:S(2)}) copy-start(s32[32]{0:T(128)} %table.1) | copy-start | bytes 388
  23.9 3.6 %collective-permute-start.10 = (bf16[256,256]{1,0:T(8,128)(2,1)S(1)}, bf16[256,256]{1,0:T(8,128)(2,1)S(1)}, u32[]{:S(2)}, u32[]{:S(2)}) collective-permute-start(bf16[256,256]{1,0:T(8,128)(2,1)S(1)} %get-tuple-element.17), channel_id=1, source_target_pairs={{0,1},{1,0},{2,3},{3,2},{4,5},{5,4},{6,7},{7,6},{8,9},{9,8},{10,11... | collective-permute-start | bytes 393224 | tf_op jit(solution)/shard_map/ppermute | solution.py:37
  24.0 5.9 %collective-permute-start.12 = (bf16[128,512]{1,0:T(8,128)(2,1)S(1)}, bf16[128,512]{1,0:T(8,128)(2,1)S(1)}, u32[]{:S(2)}, u32[]{:S(2)}) collective-permute-start(bf16[128,512]{1,0:T(8,128)(2,1)S(1)} %get-tuple-element.19), channel_id=1, source_target_pairs={{0,2},{1,3},{2,0},{3,1},{4,6},{5,7},{6,4},{7,5},{8,10},{9,11},{10,... | collective-permute-start | bytes 393224 | tf_op jit(solution)/shard_map/ppermute | solution.py:37
  25.1 7.1 %collective-permute-start.13 = (bf16[128,512]{1,0:T(8,128)(2,1)S(1)}, bf16[128,512]{1,0:T(8,128)(2,1)S(1)}, u32[]{:S(2)}, u32[]{:S(2)}) collective-permute-start(bf16[128,512]{1,0:T(8,128)(2,1)S(1)} %get-tuple-element.20), channel_id=1, source_target_pairs={{0,4},{1,5},{2,6},{3,7},{4,0},{5,1},{6,2},{7,3},{8,12},{9,13},{10,... | collective-permute-start | bytes 393224 | tf_op jit(solution)/shard_map/ppermute | solution.py:37
  26.6 8.7 %collective-permute-start.14 = (bf16[128,512]{1,0:T(8,128)(2,1)S(1)}, bf16[128,512]{1,0:T(8,128)(2,1)S(1)}, u32[]{:S(2)}, u32[]{:S(2)}) collective-permute-start(bf16[128,512]{1,0:T(8,128)(2,1)S(1)} %get-tuple-element.21), channel_id=1, source_target_pairs={{0,6},{1,7},{2,4},{3,5},{4,2},{5,3},{6,0},{7,1},{8,14},{9,15},{10,... | collective-permute-start | bytes 393224 | tf_op jit(solution)/shard_map/ppermute | solution.py:37
  27.6 7.7 %collective-permute-start.11 = (bf16[128,256]{1,0:T(8,128)(2,1)S(1)}, bf16[128,256]{1,0:T(8,128)(2,1)S(1)}, u32[]{:S(2)}, u32[]{:S(2)}) collective-permute-start(bf16[128,256]{1,0:T(8,128)(2,1)S(1)} %slice.12), channel_id=1, source_target_pairs={{0,8},{1,9},{2,10},{3,11},{4,12},{5,13},{6,14},{7,15},{8,0},{9,1},... | collective-permute-start | bytes 196616 | tf_op jit(solution)/shard_map/ppermute | solution.py:37
where the time goes:
time: 36.3 us; the launch traced here: 36 us
  starting transfers between devices  16.5 us (45%)
  waiting for transfers between devices  12.2 us (34%)
  Pallas kernels  3.53 us (10%)
  local copies, waits for them, and re-layouts  1.54 us (4%)
  between operations  1.41 us (4%)
  other arithmetic  0.86 us (2%)
    ppermute x14, starting transfers between devices, send(): lax.ppermute(member, 'blk', [(place, place ^ mask) for place in range(sha...  13.4 us
    ppermute x14, waiting for transfers between devices, send(): lax.ppermute(member, 'blk', [(place, place ^ mask) for place in range(sha...  12.2 us
    ppermute x1, starting transfers between devices, one_device(): other_half = lax.ppermute(cotangent, 'ulysses', [(0, 1), (1, 0)])  3.06 us
    pallas_call x1, Pallas kernels, one_device(): pl.pallas_call(functools.partial(tile_kernel, scale, block_len, q_masks,...  2.42 us
    unnamed x18, local copies, waits for them, and re-layouts  1.52 us
    concatenate x1, other arithmetic, one_device(): jnp.concatenate([flat(query_first), flat(query_second)], axis=1)  0.82 us
  transfers between devices with their start and end apart: 15, of which 6 were waited for; matrix products, arithmetic and copies ran while one was open for 2% of the time, Pallas kernels for 1%

commit v1 on v0

v1 whole, which is shorter than its diff:
```python
import functools
import math

import jax
import jax.numpy as jnp
from jax import lax
from jax.experimental import pallas as pl
from jax.experimental.pallas import tpu as pltpu
from jax.sharding import PartitionSpec as P


norm_eps = 1e-05
VMEM = pltpu.VMEM
SMEM = pltpu.SMEM
f32 = jnp.float32
bf16 = jnp.bfloat16


def span(bits):
    masks = [0]
    for bit in bits:
        masks = masks + [mask ^ bit for mask in masks]
    return masks


def group_bits(shards):
    width = shards.bit_length() - 1
    bits = [1 << place for place in range(width)]
    middle = bits[1:-1]
    take = (width + 1) // 2
    key_bits = middle[:take]
    query_bits = [bit for bit in bits[::-1] if bit not in key_bits]
    return query_bits, key_bits


def send(member, mask, shards):
    return lax.ppermute(member, "blk", [(place, place ^ mask) for place in range(shards)])


def in_vmem(count):
    return [pl.BlockSpec(memory_space=VMEM)] * count


def in_smem(count):
    return [pl.BlockSpec(memory_space=SMEM)] * count


def three_parts(exact):
    high = exact.astype(bf16)
    rest = exact - high.astype(f32)
    middle = rest.astype(bf16)
    low = (rest - middle.astype(f32)).astype(bf16)
    return high, middle, low


def prepare_kernel(block_len, q_masks, k_masks, me, *refs):
    sources, (key_pack, query_pack, small, q_pos, k_pos) = refs[:8], refs[8:13]
    table, gain, logs, sems = refs[13:]
    rows, kw = sources[0].shape
    targets = [
        key_pack.at[:, :kw],
        key_pack.at[:, kw : 2 * kw],
        key_pack.at[:, 2 * kw :],
        query_pack.at[:, :kw],
        query_pack.at[:, kw:],
        gain,
        logs,
        table,
    ]
    copies = [
        pltpu.make_async_copy(source, target, sems.at[i])
        for i, (source, target) in enumerate(zip(sources, targets))
    ]
    for copy in copies[::-1]:
        copy.start()
    copies[7].wait()

    def places(mask, axis):
        shard = jnp.bitwise_xor(me[0], mask)
        low = table[2 * shard] * block_len
        high = (table[2 * shard + 1] - 1) * block_len
        shape = (rows, 1) if axis == 0 else (1, rows)
        offset = lax.broadcasted_iota(jnp.int32, shape, axis)
        return offset + jnp.where(offset < block_len, low, high)

    q_pos[...] = jnp.concatenate([places(mask, 1) for mask in q_masks], axis=1)
    for j, mask in enumerate(k_masks):
        k_pos[j * rows : (j + 1) * rows, :] = places(mask, 0)
    for copy in copies[:7]:
        copy.wait()
    width = gain.shape[1]
    wide_logs = jnp.concatenate(
        [logs[side, slot : slot + 1, :] for side in range(2) for slot in range(logs.shape[1])], axis=1
    )
    filler = jnp.zeros((small.shape[0] - 2, width), f32)
    small[...] = jnp.concatenate([gain[...], wide_logs, filler], axis=0)


def grad_out_kernel(place, lam, small, own_ref, other_ref, one_ref, two_ref, pack_ref):
    rows, width = one_ref.shape
    first = place[0] == 0
    own = jnp.where(first, own_ref[:, :, 0, :].astype(f32), own_ref[:, :, 1, :].astype(f32))
    other = jnp.where(first, other_ref[:, :, 0, :].astype(f32), other_ref[:, :, 1, :].astype(f32))
    upper = jnp.where(first, own, other)
    lower = jnp.where(first, other, own)
    grad_y = jnp.concatenate([upper, lower], axis=1).reshape(rows, width)
    one = one_ref[...].astype(f32)
    two = two_ref[...].astype(f32)
    combined = one - lam[0] * two
    inv_rms = lax.rsqrt(jnp.mean(combined * combined, axis=1, keepdims=True) + norm_eps)
    gained = small[0:1, :] * grad_y
    centre = jnp.mean(combined * gained, axis=1, keepdims=True)
    grad_out = (inv_rms * (gained - combined * inv_rms * inv_rms * centre)).astype(bf16)
    pack_ref[:rows, :] = grad_out
    wide = grad_out.astype(f32)

    def as_row(column):
        return jnp.transpose(jnp.broadcast_to(column, (rows, rows)))[:1, :]

    dot_one = as_row(jnp.sum(wide * one, axis=1, keepdims=True))
    dot_two = as_row(jnp.sum(wide * two, axis=1, keepdims=True))
    wide_dots = jnp.concatenate([dot_one, dot_two], axis=1)
    parts = three_parts(small[1:2, :]) + three_parts(wide_dots)
    filler = jnp.zeros((pack_ref.shape[0] - rows - len(parts), width), f32)
    pack_ref[rows:, :] = jnp.concatenate([part.astype(f32) for part in parts] + [filler], axis=0).astype(
        bf16
    )


def query_side(q_refs, do_refs, q_pos):
    rows, kw = q_refs[0].shape[0], q_refs[0].shape[1] // 2

    def stat(row, side):
        pieces = []
        for ref in do_refs:
            block = ref[rows:, side * rows : (side + 1) * rows].astype(f32)
            pieces.append(block[row : row + 1] + block[row + 1 : row + 2] + block[row + 2 : row + 3])
        return jnp.concatenate(pieces, axis=1)

    return (
        jnp.concatenate([ref[:, :kw] for ref in q_refs], axis=0),
        jnp.concatenate([ref[:, kw:] for ref in q_refs], axis=0),
        jnp.concatenate([ref[:rows, :] for ref in do_refs], axis=0),
        stat(0, 0),
        stat(0, 1),
        stat(3, 0),
        stat(3, 1),
        q_pos,
    )


def tile_terms(scale, lam, queries, k_ref, k_pos):
    q_one, q_two, grad, log_one, log_two, dot_one, dot_two, q_pos = queries
    kw = q_one.shape[1]
    contract = (((1,), (1,)), ((), ()))
    along_keys = (((0,), (0,)), ((), ()))
    k_one, k_two, val = k_ref[:, :kw], k_ref[:, kw : 2 * kw], k_ref[:, 2 * kw :]
    visible = k_pos <= q_pos
    s_one = lax.dot_general(k_one, q_one, contract, preferred_element_type=f32)
    s_two = lax.dot_general(k_two, q_two, contract, preferred_element_type=f32)
    d_attn = lax.dot_general(val, grad, contract, preferred_element_type=f32)
    p_one = jnp.exp(jnp.where(visible, s_one * scale - log_one, -jnp.inf))
    p_two = lam * jnp.exp(jnp.where(visible, s_two * scale - log_two, -jnp.inf))
    g_one = (p_one * (d_attn - dot_one)).astype(bf16)
    g_two = (p_two * (dot_two - d_attn)).astype(bf16)
    mix = (p_one - p_two).astype(bf16)
    return (
        jnp.dot(g_one, q_one, preferred_element_type=f32),
        jnp.dot(g_two, q_two, preferred_element_type=f32),
        jnp.dot(mix, grad, preferred_element_type=f32),
        lax.dot_general(g_one, k_one, along_keys, preferred_element_type=f32),
        lax.dot_general(g_two, k_two, along_keys, preferred_element_type=f32),
    )


def put_key_terms(out, terms, before=None):
    kw = terms[0].shape[1]
    for part, term in zip((slice(0, kw), slice(kw, 2 * kw), slice(2 * kw, None)), terms):
        out[:, part] = (term if before is None else term + before[:, part]).astype(out.dtype)


def added(sums, terms):
    return terms if sums is None else tuple(a + b for a, b in zip(sums, terms))


def key_rows(k_pos, place, rows):
    return k_pos[place * rows : (place + 1) * rows, :]


def tile_early_kernel(scale, half, places, lam, q_pos, k_pos, *refs):
    q_refs, do_refs, refs = refs[:half], refs[half : 2 * half], refs[2 * half :]
    k_refs, (dq_sum, *dkv) = refs[: len(places)], refs[len(places) :]
    rows = q_refs[0].shape[0]
    queries = query_side(q_refs, do_refs, q_pos[:, : half * rows])
    sums = None
    for ref, place, out in zip(k_refs, places, dkv):
        terms = tile_terms(scale, lam[0], queries, ref, key_rows(k_pos, place, rows))
        put_key_terms(out, terms[:3])
        sums = added(sums, terms[3:])
    kw = sums[0].shape[1]
    dq_sum[:, :kw], dq_sum[:, kw:] = sums


def tile_far_kernel(scale, half, places, whole_places, lam, q_pos, k_pos, *refs):
    count = len(places)
    q_refs, do_refs, refs = refs[: 2 * half], refs[2 * half : 4 * half], refs[4 * half :]
    k_refs, refs = refs[:count], refs[count:]
    whole_refs, refs = refs[: len(whole_places)], refs[len(whole_places) :]
    before, (dq_before, dq_sum, *dkv) = refs[:count], refs[count:]
    rows, kw = q_refs[0].shape[0], q_refs[0].shape[1] // 2
    edge = half * rows
    late = query_side(q_refs[half:], do_refs[half:], q_pos[:, edge:])
    late_sums = None
    for ref, place, old, out in zip(k_refs, places, before, dkv):
        terms = tile_terms(scale, lam[0], late, ref, key_rows(k_pos, place, rows))
        put_key_terms(out, terms[:3], old)
        late_sums = added(late_sums, terms[3:])
    whole = query_side(q_refs, do_refs, q_pos[...])
    sums = None
    for ref, place, out in zip(whole_refs, whole_places, dkv[count:]):
        terms = tile_terms(scale, lam[0], whole, ref, key_rows(k_pos, place, rows))
        put_key_terms(out, terms[:3])
        sums = added(sums, terms[3:])
    one, two = sums
    dq_sum[:edge, :kw] = dq_before[:, :kw] + one[:edge]
    dq_sum[:edge, kw:] = dq_before[:, kw:] + two[:edge]
    dq_sum[edge:, :kw] = late_sums[0] + one[edge:]
    dq_sum[edge:, kw:] = late_sums[1] + two[edge:]


def tile_near_kernel(scale, half, keep, sent, lam, q_pos, k_pos, *refs):
    q_refs, do_refs, refs = refs[:half], refs[half : 2 * half], refs[2 * half :]
    k_ref, before, dq_sum, dq_keep, dq_send, dkv = refs
    rows, kw = q_refs[0].shape[0], q_refs[0].shape[1] // 2
    edge = half * rows
    late = query_side(q_refs, do_refs, q_pos[:, edge:])
    terms = tile_terms(scale, lam[0], late, k_ref, key_rows(k_pos, 0, rows))
    put_key_terms(dkv, terms[:3], before)
    for out, order in ((dq_keep, keep), (dq_send, sent)):
        for slot, i in enumerate(order):
            here = slice(slot * rows, (slot + 1) * rows)
            from_sum = slice(i * rows, (i + 1) * rows)
            for side, term in ((slice(0, kw), terms[3]), (slice(kw, None), terms[4])):
                total = dq_sum[from_sum, side]
                if i >= half:
                    total = total + term[i * rows - edge : (i + 1) * rows - edge]
                out[here, side] = total.astype(out.dtype)


def final_kernel(scale, count, dq_ref, dq_in, own_ref, *refs):
    dkv_in, outs = refs[:count], refs[count:]
    kw = outs[0].shape[1]
    dq = (dq_ref[...] + dq_in[...].astype(f32)) * scale
    outs[0][...] = dq[:, :kw].astype(bf16)
    outs[1][...] = dq[:, kw:].astype(bf16)
    total = own_ref[...]
    for ref in dkv_in:
        total = total + ref[...].astype(f32)
    outs[2][...] = (total[:, :kw] * scale).astype(bf16)
    outs[3][...] = (total[:, kw : 2 * kw] * scale).astype(bf16)
    outs[4][...] = total[:, 2 * kw :].astype(bf16)


def one_device(
    shards,
    ranks,
    query_first,
    query_second,
    key_first,
    key_second,
    values,
    out_first,
    out_second,
    log_totals,
    lambdas,
    norm_gain,
    cotangent,
    block_of,
):
    slot_count, block_len, heads_here, value_width = values.shape
    key_width = query_first.shape[3]
    rows = slot_count * block_len
    scale = 1.0 / math.sqrt(key_width)
    assert heads_here == 1 and slot_count == 2 and shards == 1 << (shards.bit_length() - 1)
    q_bits, k_bits = group_bits(shards)
    top = q_bits[-1]
    early_masks = [mask for mask in span(q_bits) if not mask & q_bits[0]]
    q_masks = early_masks + [mask ^ q_bits[0] for mask in early_masks]
    k_masks = span(k_bits)
    nq, nk = len(q_masks), len(k_masks)
    width = 2 * key_width + value_width
    me = lax.axis_index("blk").reshape(1).astype(jnp.int32)
    rank = lax.axis_index("ulysses").reshape(1).astype(jnp.int32)
    limits = pltpu.CompilerParams(vmem_limit_bytes=16 << 20)

    def flat(member):
        return member.reshape(rows, member.shape[3])

    if ranks == 2:
        own_half = cotangent
        other_half = lax.ppermute(cotangent, "ulysses", [(0, 1), (1, 0)])
    else:
        whole = lax.all_to_all(cotangent, "ulysses", split_axis=2, concat_axis=1, tiled=True)
        whole = jnp.concatenate([whole, whole], axis=2)
        own_half, other_half = whole[:, : block_len // 2], whole[:, block_len // 2 :]
        rank = jnp.zeros((1,), jnp.int32)

    key_pack, query_pack, small, q_pos, k_pos = pl.pallas_call(
        functools.partial(prepare_kernel, block_len, q_masks, k_masks),
        out_shape=[
            jax.ShapeDtypeStruct((rows, width), bf16),
            jax.ShapeDtypeStruct((rows, 2 * key_width), bf16),
            jax.ShapeDtypeStruct((8, value_width), f32),
            jax.ShapeDtypeStruct((1, nq * rows), jnp.int32),
            jax.ShapeDtypeStruct((nk * rows, 1), jnp.int32),
        ],
        in_specs=in_smem(1) + [pl.BlockSpec(memory_space=pltpu.HBM)] * 8,
        out_specs=in_vmem(5),
        scratch_shapes=[
            SMEM(block_of.shape, jnp.int32),
            VMEM((1, value_width), f32),
            VMEM((2, slot_count, block_len), f32),
            pltpu.SemaphoreType.DMA((8,)),
        ],
        compiler_params=limits,
        name="prepare",
    )(
        me,
        *[
            pltpu.with_memory_space_constraint(member, pltpu.HBM)
            for member in (
                flat(key_first),
                flat(key_second),
                flat(values),
                flat(query_first),
                flat(query_second),
                norm_gain,
                log_totals.reshape(2, slot_count, block_len),
                block_of,
            )
        ],
    )

    def spread(member, bits):
        held = {0: member}
        for bit in bits:
            for mask in list(held):
                held[mask ^ bit] = send(held[mask], bit, shards)
        return held

    keys = spread(key_pack, k_bits[::-1])
    queries = spread(query_pack, q_bits)
    grad_pack = pl.pallas_call(
        grad_out_kernel,
        out_shape=jax.ShapeDtypeStruct((rows + 16, value_width), bf16),
        in_specs=in_smem(2) + in_vmem(5),
        out_specs=pl.BlockSpec(memory_space=VMEM),
        compiler_params=limits,
        name="grad_out",
    )(rank, lambdas, small, own_half, other_half, flat(out_first), flat(out_second))
    grads = spread(grad_pack, q_bits)

    half = nq // 2
    keep_masks = [mask for mask in span(q_bits) if not mask & top]
    keep = [q_masks.index(mask) for mask in keep_masks]
    sent = [q_masks.index(mask ^ top) for mask in keep_masks]

    def query_parts(masks):
        return [queries[mask] for mask in masks] + [grads[mask] for mask in masks]

    def shape(row_count, columns, dtype):
        return jax.ShapeDtypeStruct((row_count, columns), dtype)

    def tile(kernel, outs, *operands):
        return pl.pallas_call(
            kernel,
            out_shape=outs,
            in_specs=in_smem(1) + in_vmem(2 + len(operands)),
            out_specs=in_vmem(len(outs)),
            compiler_params=limits,
        )(lambdas, q_pos, k_pos, *operands)

    early = [0] + [k_masks.index(k_bits[-1])]
    whole = [j for j in range(nk) if j not in early]
    far = early[1:] + whole
    dq_early, *early_parts = tile(
        functools.partial(tile_early_kernel, scale, half, early),
        [shape(half * rows, 2 * key_width, f32)] + [shape(rows, width, f32)] * len(early),
        *query_parts(q_masks[:half]),
        *[keys[k_masks[j]] for j in early],
    )
    dq_sum, *far_parts = tile(
        functools.partial(tile_far_kernel, scale, half, early[1:], whole),
        [shape(nq * rows, 2 * key_width, f32)] + [shape(rows, width, bf16)] * (nk - 1),
        *query_parts(q_masks),
        *[keys[k_masks[j]] for j in far],
        *early_parts[1:],
        dq_early,
    )
    dq_keep, dq_send, dkv_own = tile(
        functools.partial(tile_near_kernel, scale, half, keep, sent),
        [
            shape(half * rows, 2 * key_width, f32),
            shape(half * rows, 2 * key_width, bf16),
            shape(rows, width, f32),
        ],
        *query_parts(q_masks[half:]),
        key_pack,
        early_parts[0],
        dq_sum,
    )
    held = dict(zip(far, far_parts))
    dkv_in = [send(held[j], k_masks[j], shards) for j in range(1, nk)]
    arrived = send(dq_send, top, shards)
    kept = dq_keep + arrived.astype(f32)
    for bit in q_bits[-2::-1]:
        size = kept.shape[0] // 2
        dq_in = send(kept[size:].astype(bf16), bit, shards)
        kept = kept[:size]
        if bit != q_bits[0]:
            kept = kept + dq_in.astype(f32)
    outs = pl.pallas_call(
        functools.partial(final_kernel, scale, nk - 1),
        out_shape=[jax.ShapeDtypeStruct((rows, key_width), bf16)] * 4
        + [jax.ShapeDtypeStruct((rows, value_width), bf16)],
        in_specs=in_vmem(3 + nk - 1),
        out_specs=in_vmem(5),
        compiler_params=limits,
        name="final",
    )(kept, dq_in, dkv_own, *dkv_in)
    return tuple(
        out.reshape(slot_count, block_len, heads_here, out.shape[1]) for out in outs
    )


def solution(mesh):
    rows_spec = P("blk", None, "ulysses", None)
    in_specs = (rows_spec,) * 7 + (
        P("ulysses", None, "blk", None),
        P("ulysses"),
        P("ulysses", None),
        P("blk", "ulysses", None, None),
        P(),
    )
    shards = mesh.shape["blk"]
    body = functools.partial(one_device, shards, mesh.shape["ulysses"])
    return jax.shard_map(
        body, mesh=mesh, in_specs=in_specs, out_specs=(rows_spec,) * 5, check_vma=False
    )
```

time: 36.3 us -> 35.2 us (0.970)
  local copies, waits for them, and re-layouts: 1.54 us -> 0.03 us
  Pallas kernels: 3.53 us -> 4.88 us
  other arithmetic: 0.86 us -> 0.03 us
  starting transfers between devices: 16.5 us -> 16 us
  waiting for transfers between devices: 12.2 us -> 12.7 us
    ppermute x1, waiting for transfers between devices: 0.01 us -> 2.09 us  [one_device(): other_half = lax.ppermute(cotangent, 'ulysses', [(0, 1), (1, 0)])]
    ppermute x14, waiting for transfers between devices: 12.2 us -> 10.6 us  [send(): lax.ppermute(member, 'blk', [(place, place ^ mask) for place in range(sha...]
    ppermute x1, starting transfers between devices: 3.06 us -> 1.52 us  [one_device(): other_half = lax.ppermute(cotangent, 'ulysses', [(0, 1), (1, 0)])]
    unnamed x18 -> x6, local copies, waits for them, and re-layouts: 1.52 us -> 0.01 us
    pallas_call x2 -> x5, Pallas kernels: 2.81 us -> 4.15 us  [the longest x3 2.65 us: tile(): pl.pallas_call(kernel, out_shape=outs, in_specs=in_smem(1) + in_vmem(2 +...]
    ppermute x14, starting transfers between devices: 13.4 us -> 14.5 us  [send(): lax.ppermute(member, 'blk', [(place, place ^ mask) for place in range(sha...]
    concatenate x2 -> x0, other arithmetic: 0.83 us -> none  [the longest x1 0.82 us: one_device(): jnp.concatenate([flat(query_first), flat(query_second)], axis=1)]
  transfers between devices with their start and end apart: 15 -> 15, of which waited for: 6 -> 7; matrix products, arithmetic and copies ran while one was open for 2% -> 0% of each run, Pallas kernels for 1% -> 3%
where the time goes in v1:
time: 35.2 us; the launch traced here: 35 us
  starting transfers between devices  16 us (45%)
  waiting for transfers between devices  12.7 us (36%)
  Pallas kernels  4.88 us (14%)
  between operations  1.39 us (4%)
    ppermute x14, starting transfers between devices, send(): lax.ppermute(member, 'blk', [(place, place ^ mask) for place in range(sha...  14.5 us
    ppermute x14, waiting for transfers between devices, send(): lax.ppermute(member, 'blk', [(place, place ^ mask) for place in range(sha...  10.6 us
    pallas_call x3, Pallas kernels, tile(): pl.pallas_call(kernel, out_shape=outs, in_specs=in_smem(1) + in_vmem(2 +...  2.65 us
    ppermute x1, waiting for transfers between devices, one_device(): other_half = lax.ppermute(cotangent, 'ulysses', [(0, 1), (1, 0)])  2.09 us
    ppermute x1, starting transfers between devices, one_device(): other_half = lax.ppermute(cotangent, 'ulysses', [(0, 1), (1, 0)])  1.52 us
    pallas_call x1, Pallas kernels, one_device(): pl.pallas_call(functools.partial(prepare_kernel, block_len, q_masks, k_ma...  1.1 us
    pallas_call x1, Pallas kernels, one_device(): pl.pallas_call(functools.partial(final_kernel, scale, nk - 1), out_shape=...  0.73 us
  transfers between devices with their start and end apart: 15, of which 7 were waited for; matrix products, arithmetic and copies ran while one was open for 0% of the time, Pallas kernels for 3%

profile of v1, /device:TPU:0, one launch (start us, length us, event | category | flops | bytes accessed | tf_op | source)
XLA Modules:
  0.0 35.0 jit_solution(15262596822637420760)
XLA Ops:
  0.6 0.0 copy-start
  0.6 0.0 copy-start.1
  0.7 0.0 copy-start.2
  0.7 1.1 %prepare.1 = (bf16[128,512]{1,0:T(8,128)(2,1)S(1)}, bf16[128,256]{1,0:T(8,128)(2,1)S(1)}, f32[8,256]{1,0:T(8,128)S(1)}, s32[1,512]{1,0:T(1,128)S(1)}, s32[512,1]{1,0:T(8,128)S(1)}) custom-call(s32[1]{0:T(128)} %bitcast.me, bf16[128,128]{1,0:T(8,128)(2,1)} %bitcast.28, bf16[128,128]{1,0:T(8,128)(2,1)} %bitcast.29, bf16[128,256]{1,0:T(8,128)(2,1)} %bitcast.27, ...), custom_call_target="tpu_custom_call" | custom-call | tf_op jit(solution)/shard_map/prepare/pallas_call | solution.py:308
  1.8 3.1 %collective-permute-start.7 = (bf16[128,512]{1,0:T(8,128)(2,1)S(1)}, bf16[128,512]{1,0:T(8,128)(2,1)S(1)}, u32[]{:S(2)}, u32[]{:S(2)}) collective-permute-start(bf16[128,512]{1,0:T(8,128)(2,1)S(1)} %get-tuple-element.29.refs_4_), channel_id=1, source_target_pairs={{0,4},{1,5},{2,6},{3,7},{4,0},{5,1},{6,2},{7,3},{8,12},{9,13},{10,... | collective-permute-start | bytes 393224 | tf_op jit(solution)/shard_map/ppermute | solution.py:37
  4.9 0.0 copy-done
  4.9 1.5 %collective-permute-start.2 = (bf16[2,32,2,256]{3,2,1,0:T(2,128)(2,1)S(1)}, bf16[2,32,2,256]{3,2,1,0:T(2,128)(2,1)S(1)}, u32[]{:S(2)}, u32[]{:S(2)}) collective-permute-start(bf16[2,32,2,256]{3,2,1,0:T(2,128)(2,1)S(1)} %copy-done), channel_id=1, source_target_pairs={{0,16},{16,0},{1,17},{17,1},{2,18},{18,2},{3,19},{19,3},{4,20},{20... | collective-permute-start | bytes 196616 | tf_op jit(solution)/shard_map/ppermute | solution.py:301
  7.1 2.1 %collective-permute-done.2.other_ref = bf16[2,32,2,256]{3,2,1,0:T(2,128)(2,1)S(1)} collective-permute-done((bf16[2,32,2,256]{3,2,1,0:T(2,128)(2,1)S(1)}, bf16[2,32,2,256]{3,2,1,0:T(2,128)(2,1)S(1)}, u32[]{:S(2)}, u32[]{:S(2)}) %collective-permute-start.2) | collective-permute-done | bytes 65568 | tf_op jit(solution)/shard_map/ppermute | solution.py:301
  9.2 0.0 copy-done.1
  9.2 0.0 copy-done.2
  9.2 0.4 %grad_out.1.refs_2_.refs_4_ = bf16[144,256]{1,0:T(8,128)(2,1)S(1)} custom-call(s32[1]{0:T(128)} %bitcast.7.place, f32[1]{0:T(128)S(6)} %copy.22.lam, f32[8,256]{1,0:T(8,128)S(1)} %get-tuple-element.28.small, bf16[2,32,2,256]{3,2,1,0:T(2,128)(2,1)S(1)} %copy-done, bf16[2,32,2,256]{3,2,1,0:T(2,128)(2,1)S(1)} %collective-permute-done.2.other_ref, ...), custom_call_target="tpu_custom_call" | custom-call | tf_op jit(solution)/shard_map/grad_out/pallas_call | solution.py:353
  9.6 2.6 %collective-permute-start.3 = (bf16[144,256]{1,0:T(8,128)(2,1)S(1)}, bf16[144,256]{1,0:T(8,128)(2,1)S(1)}, u32[]{:S(2)}, u32[]{:S(2)}) collective-permute-start(bf16[144,256]{1,0:T(8,128)(2,1)S(1)} %grad_out.1.refs_2_.refs_4_), channel_id=1, source_target_pairs={{0,8},{1,9},{2,10},{3,11},{4,12},{5,13},{6,14},{7,15},{8,0},{9,1},... | collective-permute-start | bytes 221192 | tf_op jit(solution)/shard_map/ppermute | solution.py:37
  12.2 0.0 collective-permute-start.5
  12.2 0.3 collective-permute-start
  12.5 1.5 %collective-permute-start.8 = (bf16[128,512]{1,0:T(8,128)(2,1)S(1)}, bf16[128,512]{1,0:T(8,128)(2,1)S(1)}, u32[]{:S(2)}, u32[]{:S(2)}) collective-permute-start(bf16[128,512]{1,0:T(8,128)(2,1)S(1)} %get-tuple-element.29.refs_4_), channel_id=1, source_target_pairs={{0,2},{1,3},{2,0},{3,1},{4,6},{5,7},{6,4},{7,5},{8,10},{9,11},{10,... | collective-permute-start | bytes 393224 | tf_op jit(solution)/shard_map/ppermute | solution.py:37
  14.0 0.0 collective-permute-done.7.refs_5_.refs_8_
  14.0 0.5 %collective-permute-start.9 = (bf16[128,512]{1,0:T(8,128)(2,1)S(1)}, bf16[128,512]{1,0:T(8,128)(2,1)S(1)}, u32[]{:S(2)}, u32[]{:S(2)}) collective-permute-start(bf16[128,512]{1,0:T(8,128)(2,1)S(1)} %collective-permute-done.7.refs_5_.refs_8_), channel_id=1, source_target_pairs={{0,2},{1,3},{2,0},{3,1},{4,6},{5,7},{6,4},{7,5},{8,10},{9,11},{10,... | collective-permute-start | bytes 393224 | tf_op jit(solution)/shard_map/ppermute | solution.py:37
  14.6 0.0 collective-permute-done.5.refs_1_
  14.6 0.0 collective-permute-start.6
  14.6 0.6 %collective-permute-done.3.refs_6_.refs_2_ = bf16[144,256]{1,0:T(8,128)(2,1)S(1)} collective-permute-done((bf16[144,256]{1,0:T(8,128)(2,1)S(1)}, bf16[144,256]{1,0:T(8,128)(2,1)S(1)}, u32[]{:S(2)}, u32[]{:S(2)}) %collective-permute-start.3) | collective-permute-done | bytes 73760 | tf_op jit(solution)/shard_map/ppermute | solution.py:37
  15.2 0.0 collective-permute-start.4
  15.2 3.7 %collective-permute-done.refs_2_.refs_0_ = bf16[128,256]{1,0:T(8,128)(2,1)S(1)} collective-permute-done((bf16[128,256]{1,0:T(8,128)(2,1)S(1)}, bf16[128,256]{1,0:T(8,128)(2,1)S(1)}, u32[]{:S(2)}, u32[]{:S(2)}) %collective-permute-start) | collective-permute-done | bytes 65568 | tf_op jit(solution)/shard_map/ppermute | solution.py:37
  18.9 0.1 collective-permute-start.1
  19.0 0.0 collective-permute-done.6.refs_3_.refs_5_
  19.0 0.8 %shard_map.155 = (f32[256,256]{1,0:T(8,128)S(1)}, f32[128,512]{1,0:T(8,128)S(1)}, f32[128,512]{1,0:T(8,128)S(1)}) custom-call(f32[1]{0:T(128)S(6)} %copy.22.lam, s32[1,512]{1,0:T(1,128)S(1)} %get-tuple-element.25.q_pos, s32[512,1]{1,0:T(8,128)S(1)} %get-tuple-element.26.k_pos, bf16[128,256]{1,0:T(8,128)(2,1)S(1)} %get-tuple-element.27.refs_0_, ...), custom_call_target="tpu_custom_call" | custom-call | tf_op jit(solution)/shard_map/pallas_call | solution.py:375
  19.7 0.4 %collective-permute-done.1.refs_3_.refs_1_ = bf16[128,256]{1,0:T(8,128)(2,1)S(1)} collective-permute-done((bf16[128,256]{1,0:T(8,128)(2,1)S(1)}, bf16[128,256]{1,0:T(8,128)(2,1)S(1)}, u32[]{:S(2)}, u32[]{:S(2)}) %collective-permute-start.1) | collective-permute-done | bytes 65568 | tf_op jit(solution)/shard_map/ppermute | solution.py:37
  20.2 0.0 collective-permute-done.8.refs_9_
  20.2 0.0 collective-permute-done.4.refs_7_.refs_3_
  20.2 0.8 %collective-permute-done.9.refs_10_ = bf16[128,512]{1,0:T(8,128)(2,1)S(1)} collective-permute-done((bf16[128,512]{1,0:T(8,128)(2,1)S(1)}, bf16[128,512]{1,0:T(8,128)(2,1)S(1)}, u32[]{:S(2)}, u32[]{:S(2)}) %collective-permute-start.9) | collective-permute-done | bytes 131104 | tf_op jit(solution)/shard_map/ppermute | solution.py:37
  21.0 1.3 %shard_map.156 = (f32[512,256]{1,0:T(8,128)S(1)}, bf16[128,512]{1,0:T(8,128)(2,1)S(1)}, bf16[128,512]{1,0:T(8,128)(2,1)S(1)}, bf16[128,512]{1,0:T(8,128)(2,1)S(1)}) custom-call(f32[1]{0:T(128)S(6)} %copy.22.lam, s32[1,512]{1,0:T(1,128)S(1)} %get-tuple-element.25.q_pos, s32[512,1]{1,0:T(8,128)S(1)} %get-tuple-element.26.k_pos, ...), custom_call_target="tpu_custom_call" | custom-call | tf_op jit(solution)/shard_map/pallas_call | solution.py:375
  22.3 0.6 %shard_map.157 = (f32[256,256]{1,0:T(8,128)S(1)}, bf16[256,256]{1,0:T(8,128)(2,1)S(1)}, f32[128,512]{1,0:T(8,128)S(1)}) custom-call(f32[1]{0:T(128)S(6)} %copy.22.lam, s32[1,512]{1,0:T(1,128)S(1)} %get-tuple-element.25.q_pos, s32[512,1]{1,0:T(8,128)S(1)} %get-tuple-element.26.k_pos, bf16[128,256]{1,0:T(8,128)(2,1)S(1)} %collective-permute-done.refs_2_.refs_0_, ...), custom_call_target="tpu_custom_call" | custom-call | tf_op jit(solution)/shard_map/pallas_call | solution.py:375
  22.9 0.1 collective-permute-start.10
  23.0 1.6 %collective-permute-start.12 = (bf16[128,512]{1,0:T(8,128)(2,1)S(1)}, bf16[128,512]{1,0:T(8,128)(2,1)S(1)}, u32[]{:S(2)}, u32[]{:S(2)}) collective-permute-start(bf16[128,512]{1,0:T(8,128)(2,1)S(1)} %get-tuple-element.37), channel_id=1, source_target_pairs={{0,2},{1,3},{2,0},{3,1},{4,6},{5,7},{6,4},{7,5},{8,10},{9,11},{10,... | collective-permute-start | bytes 393224 | tf_op jit(solution)/shard_map/ppermute | solution.py:37
  24.5 0.4 %collective-permute-start.13 = (bf16[128,512]{1,0:T(8,128)(2,1)S(1)}, bf16[128,512]{1,0:T(8,128)(2,1)S(1)}, u32[]{:S(2)}, u32[]{:S(2)}) collective-permute-start(bf16[128,512]{1,0:T(8,128)(2,1)S(1)} %get-tuple-element.38), channel_id=1, source_target_pairs={{0,4},{1,5},{2,6},{3,7},{4,0},{5,1},{6,2},{7,3},{8,12},{9,13},{10,... | collective-permute-start | bytes 393224 | tf_op jit(solution)/shard_map/ppermute | solution.py:37
  25.0 1.6 %collective-permute-start.14 = (bf16[128,512]{1,0:T(8,128)(2,1)S(1)}, bf16[128,512]{1,0:T(8,128)(2,1)S(1)}, u32[]{:S(2)}, u32[]{:S(2)}) collective-permute-start(bf16[128,512]{1,0:T(8,128)(2,1)S(1)} %get-tuple-element.39), channel_id=1, source_target_pairs={{0,6},{1,7},{2,4},{3,5},{4,2},{5,3},{6,0},{7,1},{8,14},{9,15},{10,... | collective-permute-start | bytes 393224 | tf_op jit(solution)/shard_map/ppermute | solution.py:37
  26.5 0.0 collective-permute-done.10
  26.6 2.7 %collective-permute-start.11 = (bf16[128,256]{1,0:T(8,128)(2,1)S(1)}, bf16[128,256]{1,0:T(8,128)(2,1)S(1)}, u32[]{:S(2)}, u32[]{:S(2)}) collective-permute-start(bf16[128,256]{1,0:T(8,128)(2,1)S(1)} %slice.12), channel_id=1, source_target_pairs={{0,8},{1,9},{2,10},{3,11},{4,12},{5,13},{6,14},{7,15},{8,0},{9,1},... | collective-permute-start | bytes 196616 | tf_op jit(solution)/shard_map/ppermute | solution.py:37
  29.2 0.0 collective-permute-done.12.refs_0_
  29.3 3.0 %collective-permute-done.13.refs_1_ = bf16[128,512]{1,0:T(8,128)(2,1)S(1)} collective-permute-done((bf16[128,512]{1,0:T(8,128)(2,1)S(1)}, bf16[128,512]{1,0:T(8,128)(2,1)S(1)}, u32[]{:S(2)}, u32[]{:S(2)}) %collective-permute-start.13) | collective-permute-done | bytes 131104 | tf_op jit(solution)/shard_map/ppermute | solution.py:37
  32.3 2.0 %collective-permute-done.14.refs_2_ = bf16[128,512]{1,0:T(8,128)(2,1)S(1)} collective-permute-done((bf16[128,512]{1,0:T(8,128)(2,1)S(1)}, bf16[128,512]{1,0:T(8,128)(2,1)S(1)}, u32[]{:S(2)}, u32[]{:S(2)}) %collective-permute-start.14) | collective-permute-done | bytes 131104 | tf_op jit(solution)/shard_map/ppermute | solution.py:37
  34.3 0.0 collective-permute-done.11.dq_in
  34.3 0.7 %final.1 = (bf16[128,128]{1,0:T(8,128)(2,1)}, bf16[128,128]{1,0:T(8,128)(2,1)}, bf16[128,128]{1,0:T(8,128)(2,1)}, bf16[128,128]{1,0:T(8,128)(2,1)}, bf16[128,256]{1,0:T(8,128)(2,1)}) custom-call(f32[128,256]{1,0:T(8,128)S(1)} %slice.9.dq_ref, bf16[128,256]{1,0:T(8,128)(2,1)S(1)} %collective-permute-done.11.dq_in, f32[128,512]{1,0:T(8,128)S(1)} %get-tuple-element.36.own_ref, ...), custom_call_target="tpu_custom_call" | custom-call | tf_op jit(solution)/shard_map/final/pallas_call | solution.py:422
  (3 shorter events, 0.1 us)
Async XLA Ops:
  0.6 4.3 %copy-start = (bf16[2,32,2,256]{3,2,1,0:T(2,128)(2,1)S(1)}, bf16[2,32,2,256]{3,2,1,0:T(2,128)(2,1)}, u32[]{:S(2)}) copy-start(bf16[2,32,2,256]{3,2,1,0:T(2,128)(2,1)} %own_ref.1) | copy-start | bytes 196612
  0.6 8.5 %copy-start.1 = (bf16[2,64,1,256]{3,1,2,0:T(8,128)(2,1)S(1)}, bf16[2,64,1,256]{3,1,2,0:T(8,128)(2,1)}, u32[]{:S(2)}) copy-start(bf16[2,64,1,256]{3,1,2,0:T(8,128)(2,1)} %param.17) | copy-start | bytes 196612
  0.7 8.5 %copy-start.2 = (bf16[2,64,1,256]{3,1,2,0:T(8,128)(2,1)S(1)}, bf16[2,64,1,256]{3,1,2,0:T(8,128)(2,1)}, u32[]{:S(2)}) copy-start(bf16[2,64,1,256]{3,1,2,0:T(8,128)(2,1)} %param.18) | copy-start | bytes 196612
  1.8 12.3 %collective-permute-start.7 = (bf16[128,512]{1,0:T(8,128)(2,1)S(1)}, bf16[128,512]{1,0:T(8,128)(2,1)S(1)}, u32[]{:S(2)}, u32[]{:S(2)}) collective-permute-start(bf16[128,512]{1,0:T(8,128)(2,1)S(1)} %get-tuple-element.29.refs_4_), channel_id=1, source_target_pairs={{0,4},{1,5},{2,6},{3,7},{4,0},{5,1},{6,2},{7,3},{8,12},{9,13},{10,... | collective-permute-start | bytes 393224 | tf_op jit(solution)/shard_map/ppermute | solution.py:37
  4.9 4.3 %collective-permute-start.2 = (bf16[2,32,2,256]{3,2,1,0:T(2,128)(2,1)S(1)}, bf16[2,32,2,256]{3,2,1,0:T(2,128)(2,1)S(1)}, u32[]{:S(2)}, u32[]{:S(2)}) collective-permute-start(bf16[2,32,2,256]{3,2,1,0:T(2,128)(2,1)S(1)} %copy-done), channel_id=1, source_target_pairs={{0,16},{16,0},{1,17},{17,1},{2,18},{18,2},{3,19},{19,3},{4,20},{20... | collective-permute-start | bytes 196616 | tf_op jit(solution)/shard_map/ppermute | solution.py:301
  9.6 5.7 %collective-permute-start.3 = (bf16[144,256]{1,0:T(8,128)(2,1)S(1)}, bf16[144,256]{1,0:T(8,128)(2,1)S(1)}, u32[]{:S(2)}, u32[]{:S(2)}) collective-permute-start(bf16[144,256]{1,0:T(8,128)(2,1)S(1)} %grad_out.1.refs_2_.refs_4_), channel_id=1, source_target_pairs={{0,8},{1,9},{2,10},{3,11},{4,12},{5,13},{6,14},{7,15},{8,0},{9,1},... | collective-permute-start | bytes 221192 | tf_op jit(solution)/shard_map/ppermute | solution.py:37
  12.2 2.4 %collective-permute-start.5 = (bf16[128,256]{1,0:T(8,128)(2,1)S(1)}, bf16[128,256]{1,0:T(8,128)(2,1)S(1)}, u32[]{:S(2)}, u32[]{:S(2)}) collective-permute-start(bf16[128,256]{1,0:T(8,128)(2,1)S(1)} %get-tuple-element.27.refs_0_), channel_id=1, source_target_pairs={{0,1},{1,0},{2,3},{3,2},{4,5},{5,4},{6,7},{7,6},{8,9},{9,8},{10,11... | collective-permute-start | bytes 196616 | tf_op jit(solution)/shard_map/ppermute | solution.py:37
  12.2 6.7 %collective-permute-start = (bf16[128,256]{1,0:T(8,128)(2,1)S(1)}, bf16[128,256]{1,0:T(8,128)(2,1)S(1)}, u32[]{:S(2)}, u32[]{:S(2)}) collective-permute-start(bf16[128,256]{1,0:T(8,128)(2,1)S(1)} %get-tuple-element.27.refs_0_), channel_id=1, source_target_pairs={{0,8},{1,9},{2,10},{3,11},{4,12},{5,13},{6,14},{7,15},{8,0},{9,1},... | collective-permute-start | bytes 196616 | tf_op jit(solution)/shard_map/ppermute | solution.py:37
  12.5 7.6 %collective-permute-start.8 = (bf16[128,512]{1,0:T(8,128)(2,1)S(1)}, bf16[128,512]{1,0:T(8,128)(2,1)S(1)}, u32[]{:S(2)}, u32[]{:S(2)}) collective-permute-start(bf16[128,512]{1,0:T(8,128)(2,1)S(1)} %get-tuple-element.29.refs_4_), channel_id=1, source_target_pairs={{0,2},{1,3},{2,0},{3,1},{4,6},{5,7},{6,4},{7,5},{8,10},{9,11},{10,... | collective-permute-start | bytes 393224 | tf_op jit(solution)/shard_map/ppermute | solution.py:37
  14.0 6.9 %collective-permute-start.9 = (bf16[128,512]{1,0:T(8,128)(2,1)S(1)}, bf16[128,512]{1,0:T(8,128)(2,1)S(1)}, u32[]{:S(2)}, u32[]{:S(2)}) collective-permute-start(bf16[128,512]{1,0:T(8,128)(2,1)S(1)} %collective-permute-done.7.refs_5_.refs_8_), channel_id=1, source_target_pairs={{0,2},{1,3},{2,0},{3,1},{4,6},{5,7},{6,4},{7,5},{8,10},{9,11},{10,... | collective-permute-start | bytes 393224 | tf_op jit(solution)/shard_map/ppermute | solution.py:37
  14.6 4.4 %collective-permute-start.6 = (bf16[144,256]{1,0:T(8,128)(2,1)S(1)}, bf16[144,256]{1,0:T(8,128)(2,1)S(1)}, u32[]{:S(2)}, u32[]{:S(2)}) collective-permute-start(bf16[144,256]{1,0:T(8,128)(2,1)S(1)} %grad_out.1.refs_2_.refs_4_), channel_id=1, source_target_pairs={{0,1},{1,0},{2,3},{3,2},{4,5},{5,4},{6,7},{7,6},{8,9},{9,8},{10,11... | collective-permute-start | bytes 221192 | tf_op jit(solution)/shard_map/ppermute | solution.py:37
  15.2 5.0 %collective-permute-start.4 = (bf16[144,256]{1,0:T(8,128)(2,1)S(1)}, bf16[144,256]{1,0:T(8,128)(2,1)S(1)}, u32[]{:S(2)}, u32[]{:S(2)}) collective-permute-start(bf16[144,256]{1,0:T(8,128)(2,1)S(1)} %collective-permute-done.3.refs_6_.refs_2_), channel_id=1, source_target_pairs={{0,1},{1,0},{2,3},{3,2},{4,5},{5,4},{6,7},{7,6},{8,9},{9,8},{10,11... | collective-permute-start | bytes 221192 | tf_op jit(solution)/shard_map/ppermute | solution.py:37
  18.9 1.3 %collective-permute-start.1 = (bf16[128,256]{1,0:T(8,128)(2,1)S(1)}, bf16[128,256]{1,0:T(8,128)(2,1)S(1)}, u32[]{:S(2)}, u32[]{:S(2)}) collective-permute-start(bf16[128,256]{1,0:T(8,128)(2,1)S(1)} %collective-permute-done.refs_2_.refs_0_), channel_id=1, source_target_pairs={{0,1},{1,0},{2,3},{3,2},{4,5},{5,4},{6,7},{7,6},{8,9},{9,8},{10,11... | collective-permute-start | bytes 196616 | tf_op jit(solution)/shard_map/ppermute | solution.py:37
  22.9 3.6 %collective-permute-start.10 = (bf16[256,256]{1,0:T(8,128)(2,1)S(1)}, bf16[256,256]{1,0:T(8,128)(2,1)S(1)}, u32[]{:S(2)}, u32[]{:S(2)}) collective-permute-start(bf16[256,256]{1,0:T(8,128)(2,1)S(1)} %get-tuple-element.35), channel_id=1, source_target_pairs={{0,1},{1,0},{2,3},{3,2},{4,5},{5,4},{6,7},{7,6},{8,9},{9,8},{10,11... | collective-permute-start | bytes 393224 | tf_op jit(solution)/shard_map/ppermute | solution.py:37
  23.0 6.3 %collective-permute-start.12 = (bf16[128,512]{1,0:T(8,128)(2,1)S(1)}, bf16[128,512]{1,0:T(8,128)(2,1)S(1)}, u32[]{:S(2)}, u32[]{:S(2)}) collective-permute-start(bf16[128,512]{1,0:T(8,128)(2,1)S(1)} %get-tuple-element.37), channel_id=1, source_target_pairs={{0,2},{1,3},{2,0},{3,1},{4,6},{5,7},{6,4},{7,5},{8,10},{9,11},{10,... | collective-permute-start | bytes 393224 | tf_op jit(solution)/shard_map/ppermute | solution.py:37
  24.5 7.8 %collective-permute-start.13 = (bf16[128,512]{1,0:T(8,128)(2,1)S(1)}, bf16[128,512]{1,0:T(8,128)(2,1)S(1)}, u32[]{:S(2)}, u32[]{:S(2)}) collective-permute-start(bf16[128,512]{1,0:T(8,128)(2,1)S(1)} %get-tuple-element.38), channel_id=1, source_target_pairs={{0,4},{1,5},{2,6},{3,7},{4,0},{5,1},{6,2},{7,3},{8,12},{9,13},{10,... | collective-permute-start | bytes 393224 | tf_op jit(solution)/shard_map/ppermute | solution.py:37
  25.0 9.3 %collective-permute-start.14 = (bf16[128,512]{1,0:T(8,128)(2,1)S(1)}, bf16[128,512]{1,0:T(8,128)(2,1)S(1)}, u32[]{:S(2)}, u32[]{:S(2)}) collective-permute-start(bf16[128,512]{1,0:T(8,128)(2,1)S(1)} %get-tuple-element.39), channel_id=1, source_target_pairs={{0,6},{1,7},{2,4},{3,5},{4,2},{5,3},{6,0},{7,1},{8,14},{9,15},{10,... | collective-permute-start | bytes 393224 | tf_op jit(solution)/shard_map/ppermute | solution.py:37
  26.6 7.7 %collective-permute-start.11 = (bf16[128,256]{1,0:T(8,128)(2,1)S(1)}, bf16[128,256]{1,0:T(8,128)(2,1)S(1)}, u32[]{:S(2)}, u32[]{:S(2)}) collective-permute-start(bf16[128,256]{1,0:T(8,128)(2,1)S(1)} %slice.12), channel_id=1, source_target_pairs={{0,8},{1,9},{2,10},{3,11},{4,12},{5,13},{6,14},{7,15},{8,0},{9,1},... | collective-permute-start | bytes 196616 | tf_op jit(solution)/shard_map/ppermute | solution.py:37

commit v2 on v1

--- a/solution.py
+++ b/solution.py
@@ -10,6 +10,7 @@
 
 
 norm_eps = 1e-05
+log2_e = math.log2(math.e)
 VMEM = pltpu.VMEM
 SMEM = pltpu.SMEM
 f32 = jnp.float32
@@ -127,7 +128,7 @@
     )
 
 
-def query_side(q_refs, do_refs, q_pos):
+def query_side(scale, lam, q_refs, do_refs, q_pos):
     rows, kw = q_refs[0].shape[0], q_refs[0].shape[1] // 2
 
     def stat(row, side):
@@ -137,30 +138,50 @@
             pieces.append(block[row : row + 1] + block[row + 1 : row + 2] + block[row + 2 : row + 3])
         return jnp.concatenate(pieces, axis=1)
 
+    log_one = stat(0, 0) * -log2_e
+    log_two = stat(0, 1) * -log2_e
     return (
         jnp.concatenate([ref[:, :kw] for ref in q_refs], axis=0),
         jnp.concatenate([ref[:, kw:] for ref in q_refs], axis=0),
         jnp.concatenate([ref[:rows, :] for ref in do_refs], axis=0),
-        stat(0, 0),
-        stat(0, 1),
+        scale * log2_e,
+        log_one,
+        log_two + jnp.log(jnp.full(log_two.shape, lam, f32)) * log2_e,
         stat(3, 0),
         stat(3, 1),
         q_pos,
     )
 
 
-def tile_terms(scale, lam, queries, k_ref, k_pos):
-    q_one, q_two, grad, log_one, log_two, dot_one, dot_two, q_pos = queries
+def tile_terms(queries, k_refs, k_poss, own=False):
+    q_one, q_two, grad, factor, log_one, log_two, dot_one, dot_two, q_pos = queries
     kw = q_one.shape[1]
+    rows = k_refs[0].shape[0]
     contract = (((1,), (1,)), ((), ()))
     along_keys = (((0,), (0,)), ((), ()))
-    k_one, k_two, val = k_ref[:, :kw], k_ref[:, kw : 2 * kw], k_ref[:, 2 * kw :]
-    visible = k_pos <= q_pos
+    k_one = jnp.concatenate([ref[:, :kw] for ref in k_refs], axis=0)
+    k_two = jnp.concatenate([ref[:, kw : 2 * kw] for ref in k_refs], axis=0)
+    val = jnp.concatenate([ref[:, 2 * kw :] for ref in k_refs], axis=0)
     s_one = lax.dot_general(k_one, q_one, contract, preferred_element_type=f32)
     s_two = lax.dot_general(k_two, q_two, contract, preferred_element_type=f32)
     d_attn = lax.dot_general(val, grad, contract, preferred_element_type=f32)
-    p_one = jnp.exp(jnp.where(visible, s_one * scale - log_one, -jnp.inf))
-    p_two = lam * jnp.exp(jnp.where(visible, s_two * scale - log_two, -jnp.inf))
+
+    def weights(score, log):
+        score = score * factor
+        parts = []
+        for i, k_pos in enumerate(k_poss):
+            if own and i == 0:
+                seen = jnp.where(k_pos <= q_pos, score[:rows] + log, -jnp.inf)
+                parts.append(jnp.exp2(seen))
+                continue
+            for first in (0, rows // 2):
+                block = score[i * rows + first : i * rows + first + rows // 2]
+                shift = jnp.where(k_pos[first : first + 1, :] <= q_pos, log, -jnp.inf)
+                parts.append(jnp.exp2(block + shift))
+        return jnp.concatenate(parts, axis=0)
+
+    p_one = weights(s_one, log_one)
+    p_two = weights(s_two, log_two)
     g_one = (p_one * (d_attn - dot_one)).astype(bf16)
     g_two = (p_two * (dot_two - d_attn)).astype(bf16)
     mix = (p_one - p_two).astype(bf16)
@@ -173,14 +194,12 @@
     )
 
 
-def put_key_terms(out, terms, before=None):
+def put_key_terms(outs, terms, befores=None):
     kw = terms[0].shape[1]
-    for part, term in zip((slice(0, kw), slice(kw, 2 * kw), slice(2 * kw, None)), terms):
-        out[:, part] = (term if before is None else term + before[:, part]).astype(out.dtype)
-
-
-def added(sums, terms):
-    return terms if sums is None else tuple(a + b for a, b in zip(sums, terms))
+    for part, stacked in zip((slice(0, kw), slice(kw, 2 * kw), slice(2 * kw, None)), terms):
+        for i, out in enumerate(outs):
+            term = stacked[i * out.shape[0] : (i + 1) * out.shape[0]]
+            out[:, part] = (term if befores is None else term + befores[i][:, part]).astype(out.dtype)
 
 
 def key_rows(k_pos, place, rows):
@@ -191,14 +210,11 @@
     q_refs, do_refs, refs = refs[:half], refs[half : 2 * half], refs[2 * half :]
     k_refs, (dq_sum, *dkv) = refs[: len(places)], refs[len(places) :]
     rows = q_refs[0].shape[0]
-    queries = query_side(q_refs, do_refs, q_pos[:, : half * rows])
-    sums = None
-    for ref, place, out in zip(k_refs, places, dkv):
-        terms = tile_terms(scale, lam[0], queries, ref, key_rows(k_pos, place, rows))
-        put_key_terms(out, terms[:3])
-        sums = added(sums, terms[3:])
-    kw = sums[0].shape[1]
-    dq_sum[:, :kw], dq_sum[:, kw:] = sums
+    queries = query_side(scale, lam[0], q_refs, do_refs, q_pos[:, : half * rows])
+    terms = tile_terms(queries, k_refs, [key_rows(k_pos, place, rows) for place in places], True)
+    put_key_terms(dkv, terms[:3])
+    kw = terms[3].shape[1]
+    dq_sum[:, :kw], dq_sum[:, kw:] = terms[3:]
 
 
 def tile_far_kernel(scale, half, places, whole_places, lam, q_pos, k_pos, *refs):
@@ -209,19 +225,14 @@
     before, (dq_before, dq_sum, *dkv) = refs[:count], refs[count:]
     rows, kw = q_refs[0].shape[0], q_refs[0].shape[1] // 2
     edge = half * rows
-    late = query_side(q_refs[half:], do_refs[half:], q_pos[:, edge:])
-    late_sums = None
-    for ref, place, old, out in zip(k_refs, places, before, dkv):
-        terms = tile_terms(scale, lam[0], late, ref, key_rows(k_pos, place, rows))
-        put_key_terms(out, terms[:3], old)
-        late_sums = added(late_sums, terms[3:])
-    whole = query_side(q_refs, do_refs, q_pos[...])
-    sums = None
-    for ref, place, out in zip(whole_refs, whole_places, dkv[count:]):
-        terms = tile_terms(scale, lam[0], whole, ref, key_rows(k_pos, place, rows))
-        put_key_terms(out, terms[:3])
-        sums = added(sums, terms[3:])
-    one, two = sums
+    late = query_side(scale, lam[0], q_refs[half:], do_refs[half:], q_pos[:, edge:])
+    terms = tile_terms(late, k_refs, [key_rows(k_pos, place, rows) for place in places])
+    put_key_terms(dkv[:count], terms[:3], before)
+    late_sums = terms[3:]
+    whole = query_side(scale, lam[0], q_refs, do_refs, q_pos[...])
+    terms = tile_terms(whole, whole_refs, [key_rows(k_pos, place, rows) for place in whole_places])
+    put_key_terms(dkv[count:], terms[:3])
+    one, two = terms[3:]
     dq_sum[:edge, :kw] = dq_before[:, :kw] + one[:edge]
     dq_sum[:edge, kw:] = dq_before[:, kw:] + two[:edge]
     dq_sum[edge:, :kw] = late_sums[0] + one[edge:]
@@ -233,9 +244,9 @@
     k_ref, before, dq_sum, dq_keep, dq_send, dkv = refs
     rows, kw = q_refs[0].shape[0], q_refs[0].shape[1] // 2
     edge = half * rows
-    late = query_side(q_refs, do_refs, q_pos[:, edge:])
-    terms = tile_terms(scale, lam[0], late, k_ref, key_rows(k_pos, 0, rows))
-    put_key_terms(dkv, terms[:3], before)
+    late = query_side(scale, lam[0], q_refs, do_refs, q_pos[:, edge:])
+    terms = tile_terms(late, [k_ref], [key_rows(k_pos, 0, rows)])
+    put_key_terms([dkv], terms[:3], [before])
     for out, order in ((dq_keep, keep), (dq_send, sent)):
         for slot, i in enumerate(order):
             here = slice(slot * rows, (slot + 1) * rows)

time: 35.2 us -> 35 us (level)
  Pallas kernels: 4.88 us -> 4.49 us
    pallas_call x3, Pallas kernels: 2.65 us -> 2.27 us  [tile(): pl.pallas_call(kernel, out_shape=outs, in_specs=in_smem(1) + in_vmem(2 +...]
where the time goes in v2:
time: 35 us; the launch traced here: 34.8 us
  starting transfers between devices  16 us (46%)
  waiting for transfers between devices  12.8 us (37%)
  Pallas kernels  4.49 us (13%)
  between operations  1.39 us (4%)
    ppermute x14, starting transfers between devices, send(): lax.ppermute(member, 'blk', [(place, place ^ mask) for place in range(sha...  14.5 us
    ppermute x14, waiting for transfers between devices, send(): lax.ppermute(member, 'blk', [(place, place ^ mask) for place in range(sha...  10.8 us
    pallas_call x3, Pallas kernels, tile(): pl.pallas_call(kernel, out_shape=outs, in_specs=in_smem(1) + in_vmem(2 +...  2.27 us
    ppermute x1, waiting for transfers between devices, one_device(): other_half = lax.ppermute(cotangent, 'ulysses', [(0, 1), (1, 0)])  2.09 us
    ppermute x1, starting transfers between devices, one_device(): other_half = lax.ppermute(cotangent, 'ulysses', [(0, 1), (1, 0)])  1.52 us
    pallas_call x1, Pallas kernels, one_device(): pl.pallas_call(functools.partial(prepare_kernel, block_len, q_masks, k_ma...  1.1 us
    pallas_call x1, Pallas kernels, one_device(): pl.pallas_call(functools.partial(final_kernel, scale, nk - 1), out_shape=...  0.73 us
  transfers between devices with their start and end apart: 15, of which 7 were waited for; matrix products, arithmetic and copies ran while one was open for 0% of the time, Pallas kernels for 3%

profile of v2, /device:TPU:0, one launch (start us, length us, event | category | flops | bytes accessed | tf_op | source)
XLA Modules:
  0.0 34.8 jit_solution(9241338576756776041)
XLA Ops:
  0.6 0.0 copy-start
  0.6 0.0 copy-start.1
  0.7 0.0 copy-start.2
  0.7 1.1 %prepare.1 = (bf16[128,512]{1,0:T(8,128)(2,1)S(1)}, bf16[128,256]{1,0:T(8,128)(2,1)S(1)}, f32[8,256]{1,0:T(8,128)S(1)}, s32[1,512]{1,0:T(1,128)S(1)}, s32[512,1]{1,0:T(8,128)S(1)}) custom-call(s32[1]{0:T(128)} %bitcast.me, bf16[128,128]{1,0:T(8,128)(2,1)} %bitcast.28, bf16[128,128]{1,0:T(8,128)(2,1)} %bitcast.29, bf16[128,256]{1,0:T(8,128)(2,1)} %bitcast.27, ...), custom_call_target="tpu_custom_call" | custom-call | tf_op jit(solution)/shard_map/prepare/pallas_call | solution.py:319
  1.8 3.1 %collective-permute-start.7 = (bf16[128,512]{1,0:T(8,128)(2,1)S(1)}, bf16[128,512]{1,0:T(8,128)(2,1)S(1)}, u32[]{:S(2)}, u32[]{:S(2)}) collective-permute-start(bf16[128,512]{1,0:T(8,128)(2,1)S(1)} %get-tuple-element.29.refs_4_), channel_id=1, source_target_pairs={{0,4},{1,5},{2,6},{3,7},{4,0},{5,1},{6,2},{7,3},{8,12},{9,13},{10,... | collective-permute-start | bytes 393224 | tf_op jit(solution)/shard_map/ppermute | solution.py:38
  4.9 0.0 copy-done
  4.9 1.5 %collective-permute-start.2 = (bf16[2,32,2,256]{3,2,1,0:T(2,128)(2,1)S(1)}, bf16[2,32,2,256]{3,2,1,0:T(2,128)(2,1)S(1)}, u32[]{:S(2)}, u32[]{:S(2)}) collective-permute-start(bf16[2,32,2,256]{3,2,1,0:T(2,128)(2,1)S(1)} %copy-done), channel_id=1, source_target_pairs={{0,16},{16,0},{1,17},{17,1},{2,18},{18,2},{3,19},{19,3},{4,20},{20... | collective-permute-start | bytes 196616 | tf_op jit(solution)/shard_map/ppermute | solution.py:312
  7.1 2.1 %collective-permute-done.2.other_ref = bf16[2,32,2,256]{3,2,1,0:T(2,128)(2,1)S(1)} collective-permute-done((bf16[2,32,2,256]{3,2,1,0:T(2,128)(2,1)S(1)}, bf16[2,32,2,256]{3,2,1,0:T(2,128)(2,1)S(1)}, u32[]{:S(2)}, u32[]{:S(2)}) %collective-permute-start.2) | collective-permute-done | bytes 65568 | tf_op jit(solution)/shard_map/ppermute | solution.py:312
  9.2 0.0 copy-done.1
  9.2 0.0 copy-done.2
  9.2 0.4 %grad_out.1.refs_2_.refs_4_ = bf16[144,256]{1,0:T(8,128)(2,1)S(1)} custom-call(s32[1]{0:T(128)} %bitcast.7.place, f32[1]{0:T(128)S(6)} %copy.22.lam, f32[8,256]{1,0:T(8,128)S(1)} %get-tuple-element.28.small, bf16[2,32,2,256]{3,2,1,0:T(2,128)(2,1)S(1)} %copy-done, bf16[2,32,2,256]{3,2,1,0:T(2,128)(2,1)S(1)} %collective-permute-done.2.other_ref, ...), custom_call_target="tpu_custom_call" | custom-call | tf_op jit(solution)/shard_map/grad_out/pallas_call | solution.py:364
  9.6 2.6 %collective-permute-start.3 = (bf16[144,256]{1,0:T(8,128)(2,1)S(1)}, bf16[144,256]{1,0:T(8,128)(2,1)S(1)}, u32[]{:S(2)}, u32[]{:S(2)}) collective-permute-start(bf16[144,256]{1,0:T(8,128)(2,1)S(1)} %grad_out.1.refs_2_.refs_4_), channel_id=1, source_target_pairs={{0,8},{1,9},{2,10},{3,11},{4,12},{5,13},{6,14},{7,15},{8,0},{9,1},... | collective-permute-start | bytes 221192 | tf_op jit(solution)/shard_map/ppermute | solution.py:38
  12.2 0.0 collective-permute-start.5
  12.2 0.3 collective-permute-start
  12.5 1.5 %collective-permute-start.8 = (bf16[128,512]{1,0:T(8,128)(2,1)S(1)}, bf16[128,512]{1,0:T(8,128)(2,1)S(1)}, u32[]{:S(2)}, u32[]{:S(2)}) collective-permute-start(bf16[128,512]{1,0:T(8,128)(2,1)S(1)} %get-tuple-element.29.refs_4_), channel_id=1, source_target_pairs={{0,2},{1,3},{2,0},{3,1},{4,6},{5,7},{6,4},{7,5},{8,10},{9,11},{10,... | collective-permute-start | bytes 393224 | tf_op jit(solution)/shard_map/ppermute | solution.py:38
  14.0 0.0 collective-permute-done.7.refs_5_.refs_8_
  14.0 0.5 %collective-permute-start.9 = (bf16[128,512]{1,0:T(8,128)(2,1)S(1)}, bf16[128,512]{1,0:T(8,128)(2,1)S(1)}, u32[]{:S(2)}, u32[]{:S(2)}) collective-permute-start(bf16[128,512]{1,0:T(8,128)(2,1)S(1)} %collective-permute-done.7.refs_5_.refs_8_), channel_id=1, source_target_pairs={{0,2},{1,3},{2,0},{3,1},{4,6},{5,7},{6,4},{7,5},{8,10},{9,11},{10,... | collective-permute-start | bytes 393224 | tf_op jit(solution)/shard_map/ppermute | solution.py:38
  14.6 0.0 collective-permute-done.5.refs_1_
  14.6 0.0 collective-permute-start.6
  14.6 0.6 %collective-permute-done.3.refs_6_.refs_2_ = bf16[144,256]{1,0:T(8,128)(2,1)S(1)} collective-permute-done((bf16[144,256]{1,0:T(8,128)(2,1)S(1)}, bf16[144,256]{1,0:T(8,128)(2,1)S(1)}, u32[]{:S(2)}, u32[]{:S(2)}) %collective-permute-start.3) | collective-permute-done | bytes 73760 | tf_op jit(solution)/shard_map/ppermute | solution.py:38
  15.2 0.0 collective-permute-start.4
  15.2 3.7 %collective-permute-done.refs_2_.refs_0_ = bf16[128,256]{1,0:T(8,128)(2,1)S(1)} collective-permute-done((bf16[128,256]{1,0:T(8,128)(2,1)S(1)}, bf16[128,256]{1,0:T(8,128)(2,1)S(1)}, u32[]{:S(2)}, u32[]{:S(2)}) %collective-permute-start) | collective-permute-done | bytes 65568 | tf_op jit(solution)/shard_map/ppermute | solution.py:38
  18.9 0.1 collective-permute-start.1
  19.0 0.0 collective-permute-done.6.refs_3_.refs_5_
  19.0 0.6 %shard_map.155 = (f32[256,256]{1,0:T(8,128)S(1)}, f32[128,512]{1,0:T(8,128)S(1)}, f32[128,512]{1,0:T(8,128)S(1)}) custom-call(f32[1]{0:T(128)S(6)} %copy.22.lam, s32[1,512]{1,0:T(1,128)S(1)} %get-tuple-element.25.q_pos, s32[512,1]{1,0:T(8,128)S(1)} %get-tuple-element.26.k_pos, bf16[128,256]{1,0:T(8,128)(2,1)S(1)} %get-tuple-element.27.refs_0_, ...), custom_call_target="tpu_custom_call" | custom-call | tf_op jit(solution)/shard_map/pallas_call | solution.py:386
  19.6 0.6 %collective-permute-done.1.refs_3_.refs_1_ = bf16[128,256]{1,0:T(8,128)(2,1)S(1)} collective-permute-done((bf16[128,256]{1,0:T(8,128)(2,1)S(1)}, bf16[128,256]{1,0:T(8,128)(2,1)S(1)}, u32[]{:S(2)}, u32[]{:S(2)}) %collective-permute-start.1) | collective-permute-done | bytes 65568 | tf_op jit(solution)/shard_map/ppermute | solution.py:38
  20.2 0.0 collective-permute-done.8.refs_9_
  20.2 0.0 collective-permute-done.4.refs_7_.refs_3_
  20.2 0.8 %collective-permute-done.9.refs_10_ = bf16[128,512]{1,0:T(8,128)(2,1)S(1)} collective-permute-done((bf16[128,512]{1,0:T(8,128)(2,1)S(1)}, bf16[128,512]{1,0:T(8,128)(2,1)S(1)}, u32[]{:S(2)}, u32[]{:S(2)}) %collective-permute-start.9) | collective-permute-done | bytes 131104 | tf_op jit(solution)/shard_map/ppermute | solution.py:38
  21.0 1.1 %shard_map.156 = (f32[512,256]{1,0:T(8,128)S(1)}, bf16[128,512]{1,0:T(8,128)(2,1)S(1)}, bf16[128,512]{1,0:T(8,128)(2,1)S(1)}, bf16[128,512]{1,0:T(8,128)(2,1)S(1)}) custom-call(f32[1]{0:T(128)S(6)} %copy.22.lam, s32[1,512]{1,0:T(1,128)S(1)} %get-tuple-element.25.q_pos, s32[512,1]{1,0:T(8,128)S(1)} %get-tuple-element.26.k_pos, ...), custom_call_target="tpu_custom_call" | custom-call | tf_op jit(solution)/shard_map/pallas_call | solution.py:386
  22.1 0.6 %shard_map.157 = (f32[256,256]{1,0:T(8,128)S(1)}, bf16[256,256]{1,0:T(8,128)(2,1)S(1)}, f32[128,512]{1,0:T(8,128)S(1)}) custom-call(f32[1]{0:T(128)S(6)} %copy.22.lam, s32[1,512]{1,0:T(1,128)S(1)} %get-tuple-element.25.q_pos, s32[512,1]{1,0:T(8,128)S(1)} %get-tuple-element.26.k_pos, bf16[128,256]{1,0:T(8,128)(2,1)S(1)} %collective-permute-done.refs_2_.refs_0_, ...), custom_call_target="tpu_custom_call" | custom-call | tf_op jit(solution)/shard_map/pallas_call | solution.py:386
  22.7 0.1 collective-permute-start.10
  22.8 1.6 %collective-permute-start.12 = (bf16[128,512]{1,0:T(8,128)(2,1)S(1)}, bf16[128,512]{1,0:T(8,128)(2,1)S(1)}, u32[]{:S(2)}, u32[]{:S(2)}) collective-permute-start(bf16[128,512]{1,0:T(8,128)(2,1)S(1)} %get-tuple-element.37), channel_id=1, source_target_pairs={{0,2},{1,3},{2,0},{3,1},{4,6},{5,7},{6,4},{7,5},{8,10},{9,11},{10,... | collective-permute-start | bytes 393224 | tf_op jit(solution)/shard_map/ppermute | solution.py:38
  24.3 0.4 %collective-permute-start.13 = (bf16[128,512]{1,0:T(8,128)(2,1)S(1)}, bf16[128,512]{1,0:T(8,128)(2,1)S(1)}, u32[]{:S(2)}, u32[]{:S(2)}) collective-permute-start(bf16[128,512]{1,0:T(8,128)(2,1)S(1)} %get-tuple-element.38), channel_id=1, source_target_pairs={{0,4},{1,5},{2,6},{3,7},{4,0},{5,1},{6,2},{7,3},{8,12},{9,13},{10,... | collective-permute-start | bytes 393224 | tf_op jit(solution)/shard_map/ppermute | solution.py:38
  24.8 1.6 %collective-permute-start.14 = (bf16[128,512]{1,0:T(8,128)(2,1)S(1)}, bf16[128,512]{1,0:T(8,128)(2,1)S(1)}, u32[]{:S(2)}, u32[]{:S(2)}) collective-permute-start(bf16[128,512]{1,0:T(8,128)(2,1)S(1)} %get-tuple-element.39), channel_id=1, source_target_pairs={{0,6},{1,7},{2,4},{3,5},{4,2},{5,3},{6,0},{7,1},{8,14},{9,15},{10,... | collective-permute-start | bytes 393224 | tf_op jit(solution)/shard_map/ppermute | solution.py:38
  26.3 0.0 collective-permute-done.10
  26.4 2.7 %collective-permute-start.11 = (bf16[128,256]{1,0:T(8,128)(2,1)S(1)}, bf16[128,256]{1,0:T(8,128)(2,1)S(1)}, u32[]{:S(2)}, u32[]{:S(2)}) collective-permute-start(bf16[128,256]{1,0:T(8,128)(2,1)S(1)} %slice.12), channel_id=1, source_target_pairs={{0,8},{1,9},{2,10},{3,11},{4,12},{5,13},{6,14},{7,15},{8,0},{9,1},... | collective-permute-start | bytes 196616 | tf_op jit(solution)/shard_map/ppermute | solution.py:38
  29.0 0.0 collective-permute-done.12.refs_0_
  29.0 3.0 %collective-permute-done.13.refs_1_ = bf16[128,512]{1,0:T(8,128)(2,1)S(1)} collective-permute-done((bf16[128,512]{1,0:T(8,128)(2,1)S(1)}, bf16[128,512]{1,0:T(8,128)(2,1)S(1)}, u32[]{:S(2)}, u32[]{:S(2)}) %collective-permute-start.13) | collective-permute-done | bytes 131104 | tf_op jit(solution)/shard_map/ppermute | solution.py:38
  32.1 2.0 %collective-permute-done.14.refs_2_ = bf16[128,512]{1,0:T(8,128)(2,1)S(1)} collective-permute-done((bf16[128,512]{1,0:T(8,128)(2,1)S(1)}, bf16[128,512]{1,0:T(8,128)(2,1)S(1)}, u32[]{:S(2)}, u32[]{:S(2)}) %collective-permute-start.14) | collective-permute-done | bytes 131104 | tf_op jit(solution)/shard_map/ppermute | solution.py:38
  34.1 0.0 collective-permute-done.11.dq_in
  34.1 0.7 %final.1 = (bf16[128,128]{1,0:T(8,128)(2,1)}, bf16[128,128]{1,0:T(8,128)(2,1)}, bf16[128,128]{1,0:T(8,128)(2,1)}, bf16[128,128]{1,0:T(8,128)(2,1)}, bf16[128,256]{1,0:T(8,128)(2,1)}) custom-call(f32[128,256]{1,0:T(8,128)S(1)} %slice.9.dq_ref, bf16[128,256]{1,0:T(8,128)(2,1)S(1)} %collective-permute-done.11.dq_in, f32[128,512]{1,0:T(8,128)S(1)} %get-tuple-element.36.own_ref, ...), custom_call_target="tpu_custom_call" | custom-call | tf_op jit(solution)/shard_map/final/pallas_call | solution.py:433
  (3 shorter events, 0.1 us)
Async XLA Ops:
  0.6 4.3 %copy-start = (bf16[2,32,2,256]{3,2,1,0:T(2,128)(2,1)S(1)}, bf16[2,32,2,256]{3,2,1,0:T(2,128)(2,1)}, u32[]{:S(2)}) copy-start(bf16[2,32,2,256]{3,2,1,0:T(2,128)(2,1)} %own_ref.1) | copy-start | bytes 196612
  0.6 8.5 %copy-start.1 = (bf16[2,64,1,256]{3,1,2,0:T(8,128)(2,1)S(1)}, bf16[2,64,1,256]{3,1,2,0:T(8,128)(2,1)}, u32[]{:S(2)}) copy-start(bf16[2,64,1,256]{3,1,2,0:T(8,128)(2,1)} %param.17) | copy-start | bytes 196612
  0.7 8.5 %copy-start.2 = (bf16[2,64,1,256]{3,1,2,0:T(8,128)(2,1)S(1)}, bf16[2,64,1,256]{3,1,2,0:T(8,128)(2,1)}, u32[]{:S(2)}) copy-start(bf16[2,64,1,256]{3,1,2,0:T(8,128)(2,1)} %param.18) | copy-start | bytes 196612
  1.8 12.3 %collective-permute-start.7 = (bf16[128,512]{1,0:T(8,128)(2,1)S(1)}, bf16[128,512]{1,0:T(8,128)(2,1)S(1)}, u32[]{:S(2)}, u32[]{:S(2)}) collective-permute-start(bf16[128,512]{1,0:T(8,128)(2,1)S(1)} %get-tuple-element.29.refs_4_), channel_id=1, source_target_pairs={{0,4},{1,5},{2,6},{3,7},{4,0},{5,1},{6,2},{7,3},{8,12},{9,13},{10,... | collective-permute-start | bytes 393224 | tf_op jit(solution)/shard_map/ppermute | solution.py:38
  4.9 4.3 %collective-permute-start.2 = (bf16[2,32,2,256]{3,2,1,0:T(2,128)(2,1)S(1)}, bf16[2,32,2,256]{3,2,1,0:T(2,128)(2,1)S(1)}, u32[]{:S(2)}, u32[]{:S(2)}) collective-permute-start(bf16[2,32,2,256]{3,2,1,0:T(2,128)(2,1)S(1)} %copy-done), channel_id=1, source_target_pairs={{0,16},{16,0},{1,17},{17,1},{2,18},{18,2},{3,19},{19,3},{4,20},{20... | collective-permute-start | bytes 196616 | tf_op jit(solution)/shard_map/ppermute | solution.py:312
  9.6 5.7 %collective-permute-start.3 = (bf16[144,256]{1,0:T(8,128)(2,1)S(1)}, bf16[144,256]{1,0:T(8,128)(2,1)S(1)}, u32[]{:S(2)}, u32[]{:S(2)}) collective-permute-start(bf16[144,256]{1,0:T(8,128)(2,1)S(1)} %grad_out.1.refs_2_.refs_4_), channel_id=1, source_target_pairs={{0,8},{1,9},{2,10},{3,11},{4,12},{5,13},{6,14},{7,15},{8,0},{9,1},... | collective-permute-start | bytes 221192 | tf_op jit(solution)/shard_map/ppermute | solution.py:38
  12.2 2.4 %collective-permute-start.5 = (bf16[128,256]{1,0:T(8,128)(2,1)S(1)}, bf16[128,256]{1,0:T(8,128)(2,1)S(1)}, u32[]{:S(2)}, u32[]{:S(2)}) collective-permute-start(bf16[128,256]{1,0:T(8,128)(2,1)S(1)} %get-tuple-element.27.refs_0_), channel_id=1, source_target_pairs={{0,1},{1,0},{2,3},{3,2},{4,5},{5,4},{6,7},{7,6},{8,9},{9,8},{10,11... | collective-permute-start | bytes 196616 | tf_op jit(solution)/shard_map/ppermute | solution.py:38
  12.2 6.7 %collective-permute-start = (bf16[128,256]{1,0:T(8,128)(2,1)S(1)}, bf16[128,256]{1,0:T(8,128)(2,1)S(1)}, u32[]{:S(2)}, u32[]{:S(2)}) collective-permute-start(bf16[128,256]{1,0:T(8,128)(2,1)S(1)} %get-tuple-element.27.refs_0_), channel_id=1, source_target_pairs={{0,8},{1,9},{2,10},{3,11},{4,12},{5,13},{6,14},{7,15},{8,0},{9,1},... | collective-permute-start | bytes 196616 | tf_op jit(solution)/shard_map/ppermute | solution.py:38
  12.5 7.6 %collective-permute-start.8 = (bf16[128,512]{1,0:T(8,128)(2,1)S(1)}, bf16[128,512]{1,0:T(8,128)(2,1)S(1)}, u32[]{:S(2)}, u32[]{:S(2)}) collective-permute-start(bf16[128,512]{1,0:T(8,128)(2,1)S(1)} %get-tuple-element.29.refs_4_), channel_id=1, source_target_pairs={{0,2},{1,3},{2,0},{3,1},{4,6},{5,7},{6,4},{7,5},{8,10},{9,11},{10,... | collective-permute-start | bytes 393224 | tf_op jit(solution)/shard_map/ppermute | solution.py:38
  14.0 6.9 %collective-permute-start.9 = (bf16[128,512]{1,0:T(8,128)(2,1)S(1)}, bf16[128,512]{1,0:T(8,128)(2,1)S(1)}, u32[]{:S(2)}, u32[]{:S(2)}) collective-permute-start(bf16[128,512]{1,0:T(8,128)(2,1)S(1)} %collective-permute-done.7.refs_5_.refs_8_), channel_id=1, source_target_pairs={{0,2},{1,3},{2,0},{3,1},{4,6},{5,7},{6,4},{7,5},{8,10},{9,11},{10,... | collective-permute-start | bytes 393224 | tf_op jit(solution)/shard_map/ppermute | solution.py:38
  14.6 4.4 %collective-permute-start.6 = (bf16[144,256]{1,0:T(8,128)(2,1)S(1)}, bf16[144,256]{1,0:T(8,128)(2,1)S(1)}, u32[]{:S(2)}, u32[]{:S(2)}) collective-permute-start(bf16[144,256]{1,0:T(8,128)(2,1)S(1)} %grad_out.1.refs_2_.refs_4_), channel_id=1, source_target_pairs={{0,1},{1,0},{2,3},{3,2},{4,5},{5,4},{6,7},{7,6},{8,9},{9,8},{10,11... | collective-permute-start | bytes 221192 | tf_op jit(solution)/shard_map/ppermute | solution.py:38
  15.2 5.0 %collective-permute-start.4 = (bf16[144,256]{1,0:T(8,128)(2,1)S(1)}, bf16[144,256]{1,0:T(8,128)(2,1)S(1)}, u32[]{:S(2)}, u32[]{:S(2)}) collective-permute-start(bf16[144,256]{1,0:T(8,128)(2,1)S(1)} %collective-permute-done.3.refs_6_.refs_2_), channel_id=1, source_target_pairs={{0,1},{1,0},{2,3},{3,2},{4,5},{5,4},{6,7},{7,6},{8,9},{9,8},{10,11... | collective-permute-start | bytes 221192 | tf_op jit(solution)/shard_map/ppermute | solution.py:38
  18.9 1.3 %collective-permute-start.1 = (bf16[128,256]{1,0:T(8,128)(2,1)S(1)}, bf16[128,256]{1,0:T(8,128)(2,1)S(1)}, u32[]{:S(2)}, u32[]{:S(2)}) collective-permute-start(bf16[128,256]{1,0:T(8,128)(2,1)S(1)} %collective-permute-done.refs_2_.refs_0_), channel_id=1, source_target_pairs={{0,1},{1,0},{2,3},{3,2},{4,5},{5,4},{6,7},{7,6},{8,9},{9,8},{10,11... | collective-permute-start | bytes 196616 | tf_op jit(solution)/shard_map/ppermute | solution.py:38
  22.7 3.6 %collective-permute-start.10 = (bf16[256,256]{1,0:T(8,128)(2,1)S(1)}, bf16[256,256]{1,0:T(8,128)(2,1)S(1)}, u32[]{:S(2)}, u32[]{:S(2)}) collective-permute-start(bf16[256,256]{1,0:T(8,128)(2,1)S(1)} %get-tuple-element.35), channel_id=1, source_target_pairs={{0,1},{1,0},{2,3},{3,2},{4,5},{5,4},{6,7},{7,6},{8,9},{9,8},{10,11... | collective-permute-start | bytes 393224 | tf_op jit(solution)/shard_map/ppermute | solution.py:38
  22.8 6.3 %collective-permute-start.12 = (bf16[128,512]{1,0:T(8,128)(2,1)S(1)}, bf16[128,512]{1,0:T(8,128)(2,1)S(1)}, u32[]{:S(2)}, u32[]{:S(2)}) collective-permute-start(bf16[128,512]{1,0:T(8,128)(2,1)S(1)} %get-tuple-element.37), channel_id=1, source_target_pairs={{0,2},{1,3},{2,0},{3,1},{4,6},{5,7},{6,4},{7,5},{8,10},{9,11},{10,... | collective-permute-start | bytes 393224 | tf_op jit(solution)/shard_map/ppermute | solution.py:38
  24.3 7.8 %collective-permute-start.13 = (bf16[128,512]{1,0:T(8,128)(2,1)S(1)}, bf16[128,512]{1,0:T(8,128)(2,1)S(1)}, u32[]{:S(2)}, u32[]{:S(2)}) collective-permute-start(bf16[128,512]{1,0:T(8,128)(2,1)S(1)} %get-tuple-element.38), channel_id=1, source_target_pairs={{0,4},{1,5},{2,6},{3,7},{4,0},{5,1},{6,2},{7,3},{8,12},{9,13},{10,... | collective-permute-start | bytes 393224 | tf_op jit(solution)/shard_map/ppermute | solution.py:38
  24.8 9.3 %collective-permute-start.14 = (bf16[128,512]{1,0:T(8,128)(2,1)S(1)}, bf16[128,512]{1,0:T(8,128)(2,1)S(1)}, u32[]{:S(2)}, u32[]{:S(2)}) collective-permute-start(bf16[128,512]{1,0:T(8,128)(2,1)S(1)} %get-tuple-element.39), channel_id=1, source_target_pairs={{0,6},{1,7},{2,4},{3,5},{4,2},{5,3},{6,0},{7,1},{8,14},{9,15},{10,... | collective-permute-start | bytes 393224 | tf_op jit(solution)/shard_map/ppermute | solution.py:38
  26.4 7.7 %collective-permute-start.11 = (bf16[128,256]{1,0:T(8,128)(2,1)S(1)}, bf16[128,256]{1,0:T(8,128)(2,1)S(1)}, u32[]{:S(2)}, u32[]{:S(2)}) collective-permute-start(bf16[128,256]{1,0:T(8,128)(2,1)S(1)} %slice.12), channel_id=1, source_target_pairs={{0,8},{1,9},{2,10},{3,11},{4,12},{5,13},{6,14},{7,15},{8,0},{9,1},... | collective-permute-start | bytes 196616 | tf_op jit(solution)/shard_map/ppermute | solution.py:38

commit v3 on v2

--- a/solution.py
+++ b/solution.py
@@ -217,12 +217,12 @@
     dq_sum[:, :kw], dq_sum[:, kw:] = terms[3:]
 
 
-def tile_far_kernel(scale, half, places, whole_places, lam, q_pos, k_pos, *refs):
+def tile_late_kernel(scale, half, places, whole_places, keep, sent, lam, q_pos, k_pos, *refs):
     count = len(places)
     q_refs, do_refs, refs = refs[: 2 * half], refs[2 * half : 4 * half], refs[4 * half :]
     k_refs, refs = refs[:count], refs[count:]
     whole_refs, refs = refs[: len(whole_places)], refs[len(whole_places) :]
-    before, (dq_before, dq_sum, *dkv) = refs[:count], refs[count:]
+    before, (dq_before, dq_keep, dq_send, *dkv) = refs[:count], refs[count:]
     rows, kw = q_refs[0].shape[0], q_refs[0].shape[1] // 2
     edge = half * rows
     late = query_side(scale, lam[0], q_refs[half:], do_refs[half:], q_pos[:, edge:])
@@ -232,29 +232,15 @@
     whole = query_side(scale, lam[0], q_refs, do_refs, q_pos[...])
     terms = tile_terms(whole, whole_refs, [key_rows(k_pos, place, rows) for place in whole_places])
     put_key_terms(dkv[count:], terms[:3])
-    one, two = terms[3:]
-    dq_sum[:edge, :kw] = dq_before[:, :kw] + one[:edge]
-    dq_sum[:edge, kw:] = dq_before[:, kw:] + two[:edge]
-    dq_sum[edge:, :kw] = late_sums[0] + one[edge:]
-    dq_sum[edge:, kw:] = late_sums[1] + two[edge:]
-
-
-def tile_near_kernel(scale, half, keep, sent, lam, q_pos, k_pos, *refs):
-    q_refs, do_refs, refs = refs[:half], refs[half : 2 * half], refs[2 * half :]
-    k_ref, before, dq_sum, dq_keep, dq_send, dkv = refs
-    rows, kw = q_refs[0].shape[0], q_refs[0].shape[1] // 2
-    edge = half * rows
-    late = query_side(scale, lam[0], q_refs, do_refs, q_pos[:, edge:])
-    terms = tile_terms(late, [k_ref], [key_rows(k_pos, 0, rows)])
-    put_key_terms([dkv], terms[:3], [before])
     for out, order in ((dq_keep, keep), (dq_send, sent)):
         for slot, i in enumerate(order):
             here = slice(slot * rows, (slot + 1) * rows)
-            from_sum = slice(i * rows, (i + 1) * rows)
-            for side, term in ((slice(0, kw), terms[3]), (slice(kw, None), terms[4])):
-                total = dq_sum[from_sum, side]
-                if i >= half:
-                    total = total + term[i * rows - edge : (i + 1) * rows - edge]
+            for n, side in enumerate((slice(0, kw), slice(kw, None))):
+                total = terms[3 + n][i * rows : (i + 1) * rows]
+                if i < half:
+                    total = total + dq_before[i * rows : (i + 1) * rows, side]
+                else:
+                    total = total + late_sums[n][i * rows - edge : (i + 1) * rows - edge]
                 out[here, side] = total.astype(out.dtype)
 
 
@@ -363,7 +349,7 @@
     queries = spread(query_pack, q_bits)
     grad_pack = pl.pallas_call(
         grad_out_kernel,
-        out_shape=jax.ShapeDtypeStruct((rows + 16, value_width), bf16),
+        out_shape=jax.ShapeDtypeStruct((rows + 8, value_width), bf16),
         in_specs=in_smem(2) + in_vmem(5),
         out_specs=pl.BlockSpec(memory_space=VMEM),
         compiler_params=limits,
@@ -400,25 +386,18 @@
         *query_parts(q_masks[:half]),
         *[keys[k_masks[j]] for j in early],
     )
-    dq_sum, *far_parts = tile(
-        functools.partial(tile_far_kernel, scale, half, early[1:], whole),
-        [shape(nq * rows, 2 * key_width, f32)] + [shape(rows, width, bf16)] * (nk - 1),
-        *query_parts(q_masks),
-        *[keys[k_masks[j]] for j in far],
-        *early_parts[1:],
-        dq_early,
-    )
-    dq_keep, dq_send, dkv_own = tile(
-        functools.partial(tile_near_kernel, scale, half, keep, sent),
+    dq_keep, dq_send, dkv_own, *far_parts = tile(
+        functools.partial(tile_late_kernel, scale, half, early, whole, keep, sent),
         [
             shape(half * rows, 2 * key_width, f32),
             shape(half * rows, 2 * key_width, bf16),
             shape(rows, width, f32),
-        ],
-        *query_parts(q_masks[half:]),
-        key_pack,
-        early_parts[0],
-        dq_sum,
+        ]
+        + [shape(rows, width, bf16)] * (nk - 1),
+        *query_parts(q_masks),
+        *[keys[k_masks[j]] for j in early + whole],
+        *early_parts,
+        dq_early,
     )
     held = dict(zip(far, far_parts))
     dkv_in = [send(held[j], k_masks[j], shards) for j in range(1, nk)]

time: 35 us -> 34.8 us (level)
  starting transfers between devices: 16 us -> 16.5 us
  Pallas kernels: 4.49 us -> 4.09 us
    ppermute x14, starting transfers between devices: 14.5 us -> 15 us  [send(): lax.ppermute(member, 'blk', [(place, place ^ mask) for place in range(sha...]
    pallas_call x3 -> x2, Pallas kernels: 2.27 us -> 1.87 us  [tile(): pl.pallas_call(kernel, out_shape=outs, in_specs=in_smem(1) + in_vmem(2 +...]
  transfers between devices with their start and end apart: 15 -> 15, of which waited for: 7 -> 6; matrix products, arithmetic and copies ran while one was open for 0% -> 0% of each run, Pallas kernels for 3% -> 3%
where the time goes in v3:
time: 34.8 us; the launch traced here: 34.7 us
  starting transfers between devices  16.5 us (47%)
  waiting for transfers between devices  12.6 us (36%)
  Pallas kernels  4.09 us (12%)
  between operations  1.4 us (4%)
    ppermute x14, starting transfers between devices, send(): lax.ppermute(member, 'blk', [(place, place ^ mask) for place in range(sha...  15 us
    ppermute x14, waiting for transfers between devices, send(): lax.ppermute(member, 'blk', [(place, place ^ mask) for place in range(sha...  10.5 us
    ppermute x1, waiting for transfers between devices, one_device(): other_half = lax.ppermute(cotangent, 'ulysses', [(0, 1), (1, 0)])  2.09 us
    pallas_call x2, Pallas kernels, tile(): pl.pallas_call(kernel, out_shape=outs, in_specs=in_smem(1) + in_vmem(2 +...  1.87 us
    ppermute x1, starting transfers between devices, one_device(): other_half = lax.ppermute(cotangent, 'ulysses', [(0, 1), (1, 0)])  1.52 us
    pallas_call x1, Pallas kernels, one_device(): pl.pallas_call(functools.partial(prepare_kernel, block_len, q_masks, k_ma...  1.1 us
    pallas_call x1, Pallas kernels, one_device(): pl.pallas_call(functools.partial(final_kernel, scale, nk - 1), out_shape=...  0.72 us
  transfers between devices with their start and end apart: 15, of which 6 were waited for; matrix products, arithmetic and copies ran while one was open for 0% of the time, Pallas kernels for 3%

profile of v3, /device:TPU:0, one launch (start us, length us, event | category | flops | bytes accessed | tf_op | source)
XLA Modules:
  0.0 34.7 jit_solution(7706525614331498521)
XLA Ops:
  0.6 0.0 copy-start
  0.6 0.0 copy-start.1
  0.7 0.0 copy-start.2
  0.7 1.1 %prepare.1 = (bf16[128,512]{1,0:T(8,128)(2,1)S(1)}, bf16[128,256]{1,0:T(8,128)(2,1)S(1)}, f32[8,256]{1,0:T(8,128)S(1)}, s32[1,512]{1,0:T(1,128)S(1)}, s32[512,1]{1,0:T(8,128)S(1)}) custom-call(s32[1]{0:T(128)} %bitcast.me, bf16[128,128]{1,0:T(8,128)(2,1)} %bitcast.28, bf16[128,128]{1,0:T(8,128)(2,1)} %bitcast.29, bf16[128,256]{1,0:T(8,128)(2,1)} %bitcast.27, ...), custom_call_target="tpu_custom_call" | custom-call | tf_op jit(solution)/shard_map/prepare/pallas_call | solution.py:305
  1.8 3.1 %collective-permute-start.7 = (bf16[128,512]{1,0:T(8,128)(2,1)S(1)}, bf16[128,512]{1,0:T(8,128)(2,1)S(1)}, u32[]{:S(2)}, u32[]{:S(2)}) collective-permute-start(bf16[128,512]{1,0:T(8,128)(2,1)S(1)} %get-tuple-element.28.refs_4_.refs_8_), channel_id=1, source_target_pairs={{0,4},{1,5},{2,6},{3,7},{4,0},{5,1},{6,2},{7,3},{8,12},{9,13},{10,... | collective-permute-start | bytes 393224 | tf_op jit(solution)/shard_map/ppermute | solution.py:38
  4.9 0.0 copy-done
  4.9 1.5 %collective-permute-start.3 = (bf16[2,32,2,256]{3,2,1,0:T(2,128)(2,1)S(1)}, bf16[2,32,2,256]{3,2,1,0:T(2,128)(2,1)S(1)}, u32[]{:S(2)}, u32[]{:S(2)}) collective-permute-start(bf16[2,32,2,256]{3,2,1,0:T(2,128)(2,1)S(1)} %copy-done), channel_id=1, source_target_pairs={{0,16},{16,0},{1,17},{17,1},{2,18},{18,2},{3,19},{19,3},{4,20},{20... | collective-permute-start | bytes 196616 | tf_op jit(solution)/shard_map/ppermute | solution.py:298
  7.1 2.1 %collective-permute-done.3.other_ref = bf16[2,32,2,256]{3,2,1,0:T(2,128)(2,1)S(1)} collective-permute-done((bf16[2,32,2,256]{3,2,1,0:T(2,128)(2,1)S(1)}, bf16[2,32,2,256]{3,2,1,0:T(2,128)(2,1)S(1)}, u32[]{:S(2)}, u32[]{:S(2)}) %collective-permute-start.3) | collective-permute-done | bytes 65568 | tf_op jit(solution)/shard_map/ppermute | solution.py:298
  9.2 0.0 copy-done.1
  9.2 0.0 copy-done.2
  9.2 0.4 %grad_out.1.refs_2_.refs_4_ = bf16[136,256]{1,0:T(8,128)(2,1)S(1)} custom-call(s32[1]{0:T(128)} %bitcast.7.place, f32[1]{0:T(128)S(6)} %copy.22.lam, f32[8,256]{1,0:T(8,128)S(1)} %get-tuple-element.27.small, bf16[2,32,2,256]{3,2,1,0:T(2,128)(2,1)S(1)} %copy-done, bf16[2,32,2,256]{3,2,1,0:T(2,128)(2,1)S(1)} %collective-permute-done.3.other_ref, ...), custom_call_target="tpu_custom_call" | custom-call | tf_op jit(solution)/shard_map/grad_out/pallas_call | solution.py:350
  9.6 2.6 %collective-permute-start.5 = (bf16[136,256]{1,0:T(8,128)(2,1)S(1)}, bf16[136,256]{1,0:T(8,128)(2,1)S(1)}, u32[]{:S(2)}, u32[]{:S(2)}) collective-permute-start(bf16[136,256]{1,0:T(8,128)(2,1)S(1)} %grad_out.1.refs_2_.refs_4_), channel_id=1, source_target_pairs={{0,8},{1,9},{2,10},{3,11},{4,12},{5,13},{6,14},{7,15},{8,0},{9,1},... | collective-permute-start | bytes 208904 | tf_op jit(solution)/shard_map/ppermute | solution.py:38
  12.2 0.3 collective-permute-start.1
  12.5 0.0 collective-permute-start
  12.5 1.5 %collective-permute-start.8 = (bf16[128,512]{1,0:T(8,128)(2,1)S(1)}, bf16[128,512]{1,0:T(8,128)(2,1)S(1)}, u32[]{:S(2)}, u32[]{:S(2)}) collective-permute-start(bf16[128,512]{1,0:T(8,128)(2,1)S(1)} %get-tuple-element.28.refs_4_.refs_8_), channel_id=1, source_target_pairs={{0,2},{1,3},{2,0},{3,1},{4,6},{5,7},{6,4},{7,5},{8,10},{9,11},{10,... | collective-permute-start | bytes 393224 | tf_op jit(solution)/shard_map/ppermute | solution.py:38
  14.0 0.0 collective-permute-done.7.refs_5_.refs_9_
  14.0 0.5 %collective-permute-start.9 = (bf16[128,512]{1,0:T(8,128)(2,1)S(1)}, bf16[128,512]{1,0:T(8,128)(2,1)S(1)}, u32[]{:S(2)}, u32[]{:S(2)}) collective-permute-start(bf16[128,512]{1,0:T(8,128)(2,1)S(1)} %collective-permute-done.7.refs_5_.refs_9_), channel_id=1, source_target_pairs={{0,2},{1,3},{2,0},{3,1},{4,6},{5,7},{6,4},{7,5},{8,10},{9,11},{10,... | collective-permute-start | bytes 393224 | tf_op jit(solution)/shard_map/ppermute | solution.py:38
  14.6 3.4 %collective-permute-done.1.refs_2_ = bf16[128,256]{1,0:T(8,128)(2,1)S(1)} collective-permute-done((bf16[128,256]{1,0:T(8,128)(2,1)S(1)}, bf16[128,256]{1,0:T(8,128)(2,1)S(1)}, u32[]{:S(2)}, u32[]{:S(2)}) %collective-permute-start.1) | collective-permute-done | bytes 65568 | tf_op jit(solution)/shard_map/ppermute | solution.py:38
  18.0 0.0 collective-permute-start.4
  18.0 0.0 collective-permute-done.5.refs_6_
  18.0 0.5 %collective-permute-start.6 = (bf16[136,256]{1,0:T(8,128)(2,1)S(1)}, bf16[136,256]{1,0:T(8,128)(2,1)S(1)}, u32[]{:S(2)}, u32[]{:S(2)}) collective-permute-start(bf16[136,256]{1,0:T(8,128)(2,1)S(1)} %collective-permute-done.5.refs_6_), channel_id=1, source_target_pairs={{0,1},{1,0},{2,3},{3,2},{4,5},{5,4},{6,7},{7,6},{8,9},{9,8},{10,11... | collective-permute-start | bytes 208904 | tf_op jit(solution)/shard_map/ppermute | solution.py:38
  18.5 0.0 collective-permute-done.refs_1_
  18.5 0.1 collective-permute-start.2
  18.6 0.7 %collective-permute-done.4.refs_3_.refs_5_ = bf16[136,256]{1,0:T(8,128)(2,1)S(1)} collective-permute-done((bf16[136,256]{1,0:T(8,128)(2,1)S(1)}, bf16[136,256]{1,0:T(8,128)(2,1)S(1)}, u32[]{:S(2)}, u32[]{:S(2)}) %collective-permute-start.4) | collective-permute-done | bytes 69664 | tf_op jit(solution)/shard_map/ppermute | solution.py:38
  19.2 0.6 %shard_map.155 = (f32[256,256]{1,0:T(8,128)S(1)}, f32[128,512]{1,0:T(8,128)S(1)}, f32[128,512]{1,0:T(8,128)S(1)}) custom-call(f32[1]{0:T(128)S(6)} %copy.22.lam, s32[1,512]{1,0:T(1,128)S(1)} %get-tuple-element.24.q_pos, s32[512,1]{1,0:T(8,128)S(1)} %get-tuple-element.25.k_pos, bf16[128,256]{1,0:T(8,128)(2,1)S(1)} %get-tuple-element.26.refs_0_, ...), custom_call_target="tpu_custom_call" | custom-call | tf_op jit(solution)/shard_map/pallas_call | solution.py:372
  19.8 0.0 collective-permute-done.2.refs_3_
  19.8 0.0 collective-permute-done.8.refs_10_
  19.8 0.0 collective-permute-done.6.refs_7_
  19.8 1.4 %collective-permute-done.9.refs_11_ = bf16[128,512]{1,0:T(8,128)(2,1)S(1)} collective-permute-done((bf16[128,512]{1,0:T(8,128)(2,1)S(1)}, bf16[128,512]{1,0:T(8,128)(2,1)S(1)}, u32[]{:S(2)}, u32[]{:S(2)}) %collective-permute-start.9) | collective-permute-done | bytes 131104 | tf_op jit(solution)/shard_map/ppermute | solution.py:38
  21.3 1.3 %shard_map.156 = (f32[256,256]{1,0:T(8,128)S(1)}, bf16[256,256]{1,0:T(8,128)(2,1)S(1)}, f32[128,512]{1,0:T(8,128)S(1)}, bf16[128,512]{1,0:T(8,128)(2,1)S(1)}, bf...) custom-call(f32[1]{0:T(128)S(6)} %copy.22.lam, s32[1,512]{1,0:T(1,128)S(1)} %get-tuple-element.24.q_pos, ...), custom_call_target="tpu_custom_call" | custom-call | tf_op jit(solution)/shard_map/pallas_call | solution.py:372
  22.6 0.1 collective-permute-start.10
  22.6 1.6 %collective-permute-start.12 = (bf16[128,512]{1,0:T(8,128)(2,1)S(1)}, bf16[128,512]{1,0:T(8,128)(2,1)S(1)}, u32[]{:S(2)}, u32[]{:S(2)}) collective-permute-start(bf16[128,512]{1,0:T(8,128)(2,1)S(1)} %get-tuple-element.35), channel_id=1, source_target_pairs={{0,2},{1,3},{2,0},{3,1},{4,6},{5,7},{6,4},{7,5},{8,10},{9,11},{10,... | collective-permute-start | bytes 393224 | tf_op jit(solution)/shard_map/ppermute | solution.py:38
  24.2 0.4 %collective-permute-start.13 = (bf16[128,512]{1,0:T(8,128)(2,1)S(1)}, bf16[128,512]{1,0:T(8,128)(2,1)S(1)}, u32[]{:S(2)}, u32[]{:S(2)}) collective-permute-start(bf16[128,512]{1,0:T(8,128)(2,1)S(1)} %get-tuple-element.36), channel_id=1, source_target_pairs={{0,4},{1,5},{2,6},{3,7},{4,0},{5,1},{6,2},{7,3},{8,12},{9,13},{10,... | collective-permute-start | bytes 393224 | tf_op jit(solution)/shard_map/ppermute | solution.py:38
  24.6 1.6 %collective-permute-start.14 = (bf16[128,512]{1,0:T(8,128)(2,1)S(1)}, bf16[128,512]{1,0:T(8,128)(2,1)S(1)}, u32[]{:S(2)}, u32[]{:S(2)}) collective-permute-start(bf16[128,512]{1,0:T(8,128)(2,1)S(1)} %get-tuple-element.37), channel_id=1, source_target_pairs={{0,6},{1,7},{2,4},{3,5},{4,2},{5,3},{6,0},{7,1},{8,14},{9,15},{10,... | collective-permute-start | bytes 393224 | tf_op jit(solution)/shard_map/ppermute | solution.py:38
  26.2 0.0 collective-permute-done.10
  26.2 2.7 %collective-permute-start.11 = (bf16[128,256]{1,0:T(8,128)(2,1)S(1)}, bf16[128,256]{1,0:T(8,128)(2,1)S(1)}, u32[]{:S(2)}, u32[]{:S(2)}) collective-permute-start(bf16[128,256]{1,0:T(8,128)(2,1)S(1)} %slice.12), channel_id=1, source_target_pairs={{0,8},{1,9},{2,10},{3,11},{4,12},{5,13},{6,14},{7,15},{8,0},{9,1},... | collective-permute-start | bytes 196616 | tf_op jit(solution)/shard_map/ppermute | solution.py:38
  28.9 0.0 collective-permute-done.12.refs_0_
  28.9 3.0 %collective-permute-done.13.refs_1_ = bf16[128,512]{1,0:T(8,128)(2,1)S(1)} collective-permute-done((bf16[128,512]{1,0:T(8,128)(2,1)S(1)}, bf16[128,512]{1,0:T(8,128)(2,1)S(1)}, u32[]{:S(2)}, u32[]{:S(2)}) %collective-permute-start.13) | collective-permute-done | bytes 131104 | tf_op jit(solution)/shard_map/ppermute | solution.py:38
  32.0 2.0 %collective-permute-done.14.refs_2_ = bf16[128,512]{1,0:T(8,128)(2,1)S(1)} collective-permute-done((bf16[128,512]{1,0:T(8,128)(2,1)S(1)}, bf16[128,512]{1,0:T(8,128)(2,1)S(1)}, u32[]{:S(2)}, u32[]{:S(2)}) %collective-permute-start.14) | collective-permute-done | bytes 131104 | tf_op jit(solution)/shard_map/ppermute | solution.py:38
  33.9 0.0 collective-permute-done.11.dq_in
  33.9 0.7 %final.1 = (bf16[128,128]{1,0:T(8,128)(2,1)}, bf16[128,128]{1,0:T(8,128)(2,1)}, bf16[128,128]{1,0:T(8,128)(2,1)}, bf16[128,128]{1,0:T(8,128)(2,1)}, bf16[128,256]{1,0:T(8,128)(2,1)}) custom-call(f32[128,256]{1,0:T(8,128)S(1)} %slice.9.dq_ref, bf16[128,256]{1,0:T(8,128)(2,1)S(1)} %collective-permute-done.11.dq_in, f32[128,512]{1,0:T(8,128)S(1)} %get-tuple-element.34.own_ref, ...), custom_call_target="tpu_custom_call" | custom-call | tf_op jit(solution)/shard_map/final/pallas_call | solution.py:412
  (3 shorter events, 0.0 us)
Async XLA Ops:
  0.6 4.3 %copy-start = (bf16[2,32,2,256]{3,2,1,0:T(2,128)(2,1)S(1)}, bf16[2,32,2,256]{3,2,1,0:T(2,128)(2,1)}, u32[]{:S(2)}) copy-start(bf16[2,32,2,256]{3,2,1,0:T(2,128)(2,1)} %own_ref.1) | copy-start | bytes 196612
  0.6 8.5 %copy-start.1 = (bf16[2,64,1,256]{3,1,2,0:T(8,128)(2,1)S(1)}, bf16[2,64,1,256]{3,1,2,0:T(8,128)(2,1)}, u32[]{:S(2)}) copy-start(bf16[2,64,1,256]{3,1,2,0:T(8,128)(2,1)} %param.17) | copy-start | bytes 196612
  0.7 8.5 %copy-start.2 = (bf16[2,64,1,256]{3,1,2,0:T(8,128)(2,1)S(1)}, bf16[2,64,1,256]{3,1,2,0:T(8,128)(2,1)}, u32[]{:S(2)}) copy-start(bf16[2,64,1,256]{3,1,2,0:T(8,128)(2,1)} %param.18) | copy-start | bytes 196612
  1.8 12.3 %collective-permute-start.7 = (bf16[128,512]{1,0:T(8,128)(2,1)S(1)}, bf16[128,512]{1,0:T(8,128)(2,1)S(1)}, u32[]{:S(2)}, u32[]{:S(2)}) collective-permute-start(bf16[128,512]{1,0:T(8,128)(2,1)S(1)} %get-tuple-element.28.refs_4_.refs_8_), channel_id=1, source_target_pairs={{0,4},{1,5},{2,6},{3,7},{4,0},{5,1},{6,2},{7,3},{8,12},{9,13},{10,... | collective-permute-start | bytes 393224 | tf_op jit(solution)/shard_map/ppermute | solution.py:38
  4.9 4.3 %collective-permute-start.3 = (bf16[2,32,2,256]{3,2,1,0:T(2,128)(2,1)S(1)}, bf16[2,32,2,256]{3,2,1,0:T(2,128)(2,1)S(1)}, u32[]{:S(2)}, u32[]{:S(2)}) collective-permute-start(bf16[2,32,2,256]{3,2,1,0:T(2,128)(2,1)S(1)} %copy-done), channel_id=1, source_target_pairs={{0,16},{16,0},{1,17},{17,1},{2,18},{18,2},{3,19},{19,3},{4,20},{20... | collective-permute-start | bytes 196616 | tf_op jit(solution)/shard_map/ppermute | solution.py:298
  9.6 8.4 %collective-permute-start.5 = (bf16[136,256]{1,0:T(8,128)(2,1)S(1)}, bf16[136,256]{1,0:T(8,128)(2,1)S(1)}, u32[]{:S(2)}, u32[]{:S(2)}) collective-permute-start(bf16[136,256]{1,0:T(8,128)(2,1)S(1)} %grad_out.1.refs_2_.refs_4_), channel_id=1, source_target_pairs={{0,8},{1,9},{2,10},{3,11},{4,12},{5,13},{6,14},{7,15},{8,0},{9,1},... | collective-permute-start | bytes 208904 | tf_op jit(solution)/shard_map/ppermute | solution.py:38
  12.2 5.8 %collective-permute-start.1 = (bf16[128,256]{1,0:T(8,128)(2,1)S(1)}, bf16[128,256]{1,0:T(8,128)(2,1)S(1)}, u32[]{:S(2)}, u32[]{:S(2)}) collective-permute-start(bf16[128,256]{1,0:T(8,128)(2,1)S(1)} %get-tuple-element.26.refs_0_), channel_id=1, source_target_pairs={{0,8},{1,9},{2,10},{3,11},{4,12},{5,13},{6,14},{7,15},{8,0},{9,1},... | collective-permute-start | bytes 196616 | tf_op jit(solution)/shard_map/ppermute | solution.py:38
  12.5 5.9 %collective-permute-start = (bf16[128,256]{1,0:T(8,128)(2,1)S(1)}, bf16[128,256]{1,0:T(8,128)(2,1)S(1)}, u32[]{:S(2)}, u32[]{:S(2)}) collective-permute-start(bf16[128,256]{1,0:T(8,128)(2,1)S(1)} %get-tuple-element.26.refs_0_), channel_id=1, source_target_pairs={{0,1},{1,0},{2,3},{3,2},{4,5},{5,4},{6,7},{7,6},{8,9},{9,8},{10,11... | collective-permute-start | bytes 196616 | tf_op jit(solution)/shard_map/ppermute | solution.py:38
  12.5 7.3 %collective-permute-start.8 = (bf16[128,512]{1,0:T(8,128)(2,1)S(1)}, bf16[128,512]{1,0:T(8,128)(2,1)S(1)}, u32[]{:S(2)}, u32[]{:S(2)}) collective-permute-start(bf16[128,512]{1,0:T(8,128)(2,1)S(1)} %get-tuple-element.28.refs_4_.refs_8_), channel_id=1, source_target_pairs={{0,2},{1,3},{2,0},{3,1},{4,6},{5,7},{6,4},{7,5},{8,10},{9,11},{10,... | collective-permute-start | bytes 393224 | tf_op jit(solution)/shard_map/ppermute | solution.py:38
  14.0 7.2 %collective-permute-start.9 = (bf16[128,512]{1,0:T(8,128)(2,1)S(1)}, bf16[128,512]{1,0:T(8,128)(2,1)S(1)}, u32[]{:S(2)}, u32[]{:S(2)}) collective-permute-start(bf16[128,512]{1,0:T(8,128)(2,1)S(1)} %collective-permute-done.7.refs_5_.refs_9_), channel_id=1, source_target_pairs={{0,2},{1,3},{2,0},{3,1},{4,6},{5,7},{6,4},{7,5},{8,10},{9,11},{10,... | collective-permute-start | bytes 393224 | tf_op jit(solution)/shard_map/ppermute | solution.py:38
  18.0 1.3 %collective-permute-start.4 = (bf16[136,256]{1,0:T(8,128)(2,1)S(1)}, bf16[136,256]{1,0:T(8,128)(2,1)S(1)}, u32[]{:S(2)}, u32[]{:S(2)}) collective-permute-start(bf16[136,256]{1,0:T(8,128)(2,1)S(1)} %grad_out.1.refs_2_.refs_4_), channel_id=1, source_target_pairs={{0,1},{1,0},{2,3},{3,2},{4,5},{5,4},{6,7},{7,6},{8,9},{9,8},{10,11... | collective-permute-start | bytes 208904 | tf_op jit(solution)/shard_map/ppermute | solution.py:38
  18.0 1.9 %collective-permute-start.6 = (bf16[136,256]{1,0:T(8,128)(2,1)S(1)}, bf16[136,256]{1,0:T(8,128)(2,1)S(1)}, u32[]{:S(2)}, u32[]{:S(2)}) collective-permute-start(bf16[136,256]{1,0:T(8,128)(2,1)S(1)} %collective-permute-done.5.refs_6_), channel_id=1, source_target_pairs={{0,1},{1,0},{2,3},{3,2},{4,5},{5,4},{6,7},{7,6},{8,9},{9,8},{10,11... | collective-permute-start | bytes 208904 | tf_op jit(solution)/shard_map/ppermute | solution.py:38
  18.5 1.3 %collective-permute-start.2 = (bf16[128,256]{1,0:T(8,128)(2,1)S(1)}, bf16[128,256]{1,0:T(8,128)(2,1)S(1)}, u32[]{:S(2)}, u32[]{:S(2)}) collective-permute-start(bf16[128,256]{1,0:T(8,128)(2,1)S(1)} %collective-permute-done.1.refs_2_), channel_id=1, source_target_pairs={{0,1},{1,0},{2,3},{3,2},{4,5},{5,4},{6,7},{7,6},{8,9},{9,8},{10,11... | collective-permute-start | bytes 196616 | tf_op jit(solution)/shard_map/ppermute | solution.py:38
  22.6 3.6 %collective-permute-start.10 = (bf16[256,256]{1,0:T(8,128)(2,1)S(1)}, bf16[256,256]{1,0:T(8,128)(2,1)S(1)}, u32[]{:S(2)}, u32[]{:S(2)}) collective-permute-start(bf16[256,256]{1,0:T(8,128)(2,1)S(1)} %get-tuple-element.33), channel_id=1, source_target_pairs={{0,1},{1,0},{2,3},{3,2},{4,5},{5,4},{6,7},{7,6},{8,9},{9,8},{10,11... | collective-permute-start | bytes 393224 | tf_op jit(solution)/shard_map/ppermute | solution.py:38
  22.6 6.3 %collective-permute-start.12 = (bf16[128,512]{1,0:T(8,128)(2,1)S(1)}, bf16[128,512]{1,0:T(8,128)(2,1)S(1)}, u32[]{:S(2)}, u32[]{:S(2)}) collective-permute-start(bf16[128,512]{1,0:T(8,128)(2,1)S(1)} %get-tuple-element.35), channel_id=1, source_target_pairs={{0,2},{1,3},{2,0},{3,1},{4,6},{5,7},{6,4},{7,5},{8,10},{9,11},{10,... | collective-permute-start | bytes 393224 | tf_op jit(solution)/shard_map/ppermute | solution.py:38
  24.2 7.8 %collective-permute-start.13 = (bf16[128,512]{1,0:T(8,128)(2,1)S(1)}, bf16[128,512]{1,0:T(8,128)(2,1)S(1)}, u32[]{:S(2)}, u32[]{:S(2)}) collective-permute-start(bf16[128,512]{1,0:T(8,128)(2,1)S(1)} %get-tuple-element.36), channel_id=1, source_target_pairs={{0,4},{1,5},{2,6},{3,7},{4,0},{5,1},{6,2},{7,3},{8,12},{9,13},{10,... | collective-permute-start | bytes 393224 | tf_op jit(solution)/shard_map/ppermute | solution.py:38
  24.6 9.3 %collective-permute-start.14 = (bf16[128,512]{1,0:T(8,128)(2,1)S(1)}, bf16[128,512]{1,0:T(8,128)(2,1)S(1)}, u32[]{:S(2)}, u32[]{:S(2)}) collective-permute-start(bf16[128,512]{1,0:T(8,128)(2,1)S(1)} %get-tuple-element.37), channel_id=1, source_target_pairs={{0,6},{1,7},{2,4},{3,5},{4,2},{5,3},{6,0},{7,1},{8,14},{9,15},{10,... | collective-permute-start | bytes 393224 | tf_op jit(solution)/shard_map/ppermute | solution.py:38
  26.2 7.7 %collective-permute-start.11 = (bf16[128,256]{1,0:T(8,128)(2,1)S(1)}, bf16[128,256]{1,0:T(8,128)(2,1)S(1)}, u32[]{:S(2)}, u32[]{:S(2)}) collective-permute-start(bf16[128,256]{1,0:T(8,128)(2,1)S(1)} %slice.12), channel_id=1, source_target_pairs={{0,8},{1,9},{2,10},{3,11},{4,12},{5,13},{6,14},{7,15},{8,0},{9,1},... | collective-permute-start | bytes 196616 | tf_op jit(solution)/shard_map/ppermute | solution.py:38

commit v4 on v3

--- a/solution.py
+++ b/solution.py
@@ -346,7 +346,11 @@
         return held
 
     keys = spread(key_pack, k_bits[::-1])
-    queries = spread(query_pack, q_bits)
+    queries = spread(query_pack, q_bits[:-1])
+    held_masks = list(queries)
+    both = send(jnp.concatenate([queries[mask] for mask in held_masks]), top, shards)
+    for i, mask in enumerate(held_masks):
+        queries[mask ^ top] = both[i * rows : (i + 1) * rows]
     grad_pack = pl.pallas_call(
         grad_out_kernel,
         out_shape=jax.ShapeDtypeStruct((rows + 8, value_width), bf16),

time: 34.8 us -> 35.1 us (level)
  waiting for transfers between devices: 12.6 us -> 13.4 us
  starting transfers between devices: 16.5 us -> 16 us
    ppermute x14 -> x13, waiting for transfers between devices: 10.5 us -> 13.2 us  [send(): lax.ppermute(member, 'blk', [(place, place ^ mask) for place in range(sha...]
    ppermute x1, waiting for transfers between devices: 2.09 us -> 0.21 us  [one_device(): other_half = lax.ppermute(cotangent, 'ulysses', [(0, 1), (1, 0)])]
    ppermute x14 -> x13, starting transfers between devices: 15 us -> 14.5 us  [send(): lax.ppermute(member, 'blk', [(place, place ^ mask) for place in range(sha...]
  transfers between devices with their start and end apart: 15 -> 14, of which waited for: 6 -> 8; matrix products, arithmetic and copies ran while one was open for 0% -> 0% of each run, Pallas kernels for 3% -> 3%
where the time goes in v4:
time: 35.1 us; the launch traced here: 34.9 us
  starting transfers between devices  16 us (46%)
  waiting for transfers between devices  13.4 us (38%)
  Pallas kernels  4.07 us (12%)
  between operations  1.38 us (4%)
    ppermute x13, starting transfers between devices, send(): lax.ppermute(member, 'blk', [(place, place ^ mask) for place in range(sha...  14.5 us
    ppermute x13, waiting for transfers between devices, send(): lax.ppermute(member, 'blk', [(place, place ^ mask) for place in range(sha...  13.2 us
    pallas_call x2, Pallas kernels, tile(): pl.pallas_call(kernel, out_shape=outs, in_specs=in_smem(1) + in_vmem(2 +...  1.87 us
    ppermute x1, starting transfers between devices, one_device(): other_half = lax.ppermute(cotangent, 'ulysses', [(0, 1), (1, 0)])  1.52 us
    pallas_call x1, Pallas kernels, one_device(): pl.pallas_call(functools.partial(prepare_kernel, block_len, q_masks, k_ma...  1.09 us
    pallas_call x1, Pallas kernels, one_device(): pl.pallas_call(functools.partial(final_kernel, scale, nk - 1), out_shape=...  0.72 us
  transfers between devices with their start and end apart: 14, of which 8 were waited for; matrix products, arithmetic and copies ran while one was open for 0% of the time, Pallas kernels for 3%

profile of v4, /device:TPU:0, one launch (start us, length us, event | category | flops | bytes accessed | tf_op | source)
XLA Modules:
  0.0 34.9 jit_solution(2701045647493026396)
XLA Ops:
  0.6 0.0 copy-start
  0.6 1.1 %prepare.1 = (bf16[128,512]{1,0:T(8,128)(2,1)S(1)}, bf16[128,256]{1,0:T(8,128)(2,1)S(1)}, f32[8,256]{1,0:T(8,128)S(1)}, s32[1,512]{1,0:T(1,128)S(1)}, s32[512,1]{1,0:T(8,128)S(1)}) custom-call(s32[1]{0:T(128)} %bitcast.me, bf16[128,128]{1,0:T(8,128)(2,1)} %bitcast.28, bf16[128,128]{1,0:T(8,128)(2,1)} %bitcast.29, bf16[128,256]{1,0:T(8,128)(2,1)} %bitcast.27, ...), custom_call_target="tpu_custom_call" | custom-call | tf_op jit(solution)/shard_map/prepare/pallas_call | solution.py:305
  1.7 4.1 %collective-permute-start = (bf16[128,256]{1,0:T(8,128)(2,1)S(1)}, bf16[128,256]{1,0:T(8,128)(2,1)S(1)}, u32[]{:S(2)}, u32[]{:S(2)}) collective-permute-start(bf16[128,256]{1,0:T(8,128)(2,1)S(1)} %get-tuple-element.26.refs_0_), channel_id=1, source_target_pairs={{0,8},{1,9},{2,10},{3,11},{4,12},{5,13},{6,14},{7,15},{8,0},{9,1},... | collective-permute-start | bytes 196616 | tf_op jit(solution)/shard_map/ppermute | solution.py:38
  5.9 0.0 copy-done
  5.9 1.5 %collective-permute-start.2 = (bf16[2,32,2,256]{3,2,1,0:T(2,128)(2,1)S(1)}, bf16[2,32,2,256]{3,2,1,0:T(2,128)(2,1)S(1)}, u32[]{:S(2)}, u32[]{:S(2)}) collective-permute-start(bf16[2,32,2,256]{3,2,1,0:T(2,128)(2,1)S(1)} %copy-done), channel_id=1, source_target_pairs={{0,16},{16,0},{1,17},{17,1},{2,18},{18,2},{3,19},{19,3},{4,20},{20... | collective-permute-start | bytes 196616 | tf_op jit(solution)/shard_map/ppermute | solution.py:298
  7.4 0.0 copy-start.1
  7.4 0.0 copy-start.2
  7.4 1.6 %collective-permute-start.6 = (bf16[128,512]{1,0:T(8,128)(2,1)S(1)}, bf16[128,512]{1,0:T(8,128)(2,1)S(1)}, u32[]{:S(2)}, u32[]{:S(2)}) collective-permute-start(bf16[128,512]{1,0:T(8,128)(2,1)S(1)} %get-tuple-element.28.refs_4_.refs_8_), channel_id=1, source_target_pairs={{0,4},{1,5},{2,6},{3,7},{4,0},{5,1},{6,2},{7,3},{8,12},{9,13},{10,... | collective-permute-start | bytes 393224 | tf_op jit(solution)/shard_map/ppermute | solution.py:38
  9.0 0.2 collective-permute-done.refs_2_
  9.2 0.1 collective-permute-start.1
  9.9 0.2 collective-permute-done.2.other_ref
  10.1 0.0 copy-done.1
  10.1 0.0 copy-done.2
  10.2 0.4 %grad_out.1.refs_2_.refs_4_ = bf16[136,256]{1,0:T(8,128)(2,1)S(1)} custom-call(s32[1]{0:T(128)} %bitcast.7.place, f32[1]{0:T(128)S(6)} %copy.22.lam, f32[8,256]{1,0:T(8,128)S(1)} %get-tuple-element.27.small, bf16[2,32,2,256]{3,2,1,0:T(2,128)(2,1)S(1)} %copy-done, bf16[2,32,2,256]{3,2,1,0:T(2,128)(2,1)S(1)} %collective-permute-done.2.other_ref, ...), custom_call_target="tpu_custom_call" | custom-call | tf_op jit(solution)/shard_map/grad_out/pallas_call | solution.py:354
  10.5 1.7 %collective-permute-start.4 = (bf16[136,256]{1,0:T(8,128)(2,1)S(1)}, bf16[136,256]{1,0:T(8,128)(2,1)S(1)}, u32[]{:S(2)}, u32[]{:S(2)}) collective-permute-start(bf16[136,256]{1,0:T(8,128)(2,1)S(1)} %grad_out.1.refs_2_.refs_4_), channel_id=1, source_target_pairs={{0,8},{1,9},{2,10},{3,11},{4,12},{5,13},{6,14},{7,15},{8,0},{9,1},... | collective-permute-start | bytes 208904 | tf_op jit(solution)/shard_map/ppermute | solution.py:38
  12.3 1.5 %collective-permute-start.7 = (bf16[128,512]{1,0:T(8,128)(2,1)S(1)}, bf16[128,512]{1,0:T(8,128)(2,1)S(1)}, u32[]{:S(2)}, u32[]{:S(2)}) collective-permute-start(bf16[128,512]{1,0:T(8,128)(2,1)S(1)} %get-tuple-element.28.refs_4_.refs_8_), channel_id=1, source_target_pairs={{0,2},{1,3},{2,0},{3,1},{4,6},{5,7},{6,4},{7,5},{8,10},{9,11},{10,... | collective-permute-start | bytes 393224 | tf_op jit(solution)/shard_map/ppermute | solution.py:38
  13.8 0.0 collective-permute-start.3
  13.8 0.0 collective-permute-done.6.refs_5_.refs_9_
  13.8 0.5 %collective-permute-start.8 = (bf16[128,512]{1,0:T(8,128)(2,1)S(1)}, bf16[128,512]{1,0:T(8,128)(2,1)S(1)}, u32[]{:S(2)}, u32[]{:S(2)}) collective-permute-start(bf16[128,512]{1,0:T(8,128)(2,1)S(1)} %collective-permute-done.6.refs_5_.refs_9_), channel_id=1, source_target_pairs={{0,2},{1,3},{2,0},{3,1},{4,6},{5,7},{6,4},{7,5},{8,10},{9,11},{10,... | collective-permute-start | bytes 393224 | tf_op jit(solution)/shard_map/ppermute | solution.py:38
  14.3 3.1 %collective-permute-done.4.refs_6_ = bf16[136,256]{1,0:T(8,128)(2,1)S(1)} collective-permute-done((bf16[136,256]{1,0:T(8,128)(2,1)S(1)}, bf16[136,256]{1,0:T(8,128)(2,1)S(1)}, u32[]{:S(2)}, u32[]{:S(2)}) %collective-permute-start.4) | collective-permute-done | bytes 69664 | tf_op jit(solution)/shard_map/ppermute | solution.py:38
  17.4 0.0 collective-permute-start.5
  17.4 0.0 collective-permute-done.1
  17.4 0.0 collective-permute-done.3.refs_3_.refs_5_
  17.4 0.6 %shard_map.155 = (f32[256,256]{1,0:T(8,128)S(1)}, f32[128,512]{1,0:T(8,128)S(1)}, f32[128,512]{1,0:T(8,128)S(1)}) custom-call(f32[1]{0:T(128)S(6)} %copy.22.lam, s32[1,512]{1,0:T(1,128)S(1)} %get-tuple-element.24.q_pos, s32[512,1]{1,0:T(8,128)S(1)} %get-tuple-element.25.k_pos, bf16[128,256]{1,0:T(8,128)(2,1)S(1)} %get-tuple-element.26.refs_0_, ...), custom_call_target="tpu_custom_call" | custom-call | tf_op jit(solution)/shard_map/pallas_call | solution.py:376
  18.0 0.6 %collective-permute-done.7.refs_10_ = bf16[128,512]{1,0:T(8,128)(2,1)S(1)} collective-permute-done((bf16[128,512]{1,0:T(8,128)(2,1)S(1)}, bf16[128,512]{1,0:T(8,128)(2,1)S(1)}, u32[]{:S(2)}, u32[]{:S(2)}) %collective-permute-start.7) | collective-permute-done | bytes 131104 | tf_op jit(solution)/shard_map/ppermute | solution.py:38
  18.6 0.0 collective-permute-done.5.refs_7_
  18.6 2.0 %collective-permute-done.8.refs_11_ = bf16[128,512]{1,0:T(8,128)(2,1)S(1)} collective-permute-done((bf16[128,512]{1,0:T(8,128)(2,1)S(1)}, bf16[128,512]{1,0:T(8,128)(2,1)S(1)}, u32[]{:S(2)}, u32[]{:S(2)}) %collective-permute-start.8) | collective-permute-done | bytes 131104 | tf_op jit(solution)/shard_map/ppermute | solution.py:38
  20.7 1.3 %shard_map.156 = (f32[256,256]{1,0:T(8,128)S(1)}, bf16[256,256]{1,0:T(8,128)(2,1)S(1)}, f32[128,512]{1,0:T(8,128)S(1)}, bf16[128,512]{1,0:T(8,128)(2,1)S(1)}, bf...) custom-call(f32[1]{0:T(128)S(6)} %copy.22.lam, s32[1,512]{1,0:T(1,128)S(1)} %get-tuple-element.24.q_pos, ...), custom_call_target="tpu_custom_call" | custom-call | tf_op jit(solution)/shard_map/pallas_call | solution.py:376
  22.0 0.1 collective-permute-start.9
  22.1 1.6 %collective-permute-start.11 = (bf16[128,512]{1,0:T(8,128)(2,1)S(1)}, bf16[128,512]{1,0:T(8,128)(2,1)S(1)}, u32[]{:S(2)}, u32[]{:S(2)}) collective-permute-start(bf16[128,512]{1,0:T(8,128)(2,1)S(1)} %get-tuple-element.35), channel_id=1, source_target_pairs={{0,2},{1,3},{2,0},{3,1},{4,6},{5,7},{6,4},{7,5},{8,10},{9,11},{10,... | collective-permute-start | bytes 393224 | tf_op jit(solution)/shard_map/ppermute | solution.py:38
  23.6 2.5 %collective-permute-start.12 = (bf16[128,512]{1,0:T(8,128)(2,1)S(1)}, bf16[128,512]{1,0:T(8,128)(2,1)S(1)}, u32[]{:S(2)}, u32[]{:S(2)}) collective-permute-start(bf16[128,512]{1,0:T(8,128)(2,1)S(1)} %get-tuple-element.36), channel_id=1, source_target_pairs={{0,4},{1,5},{2,6},{3,7},{4,0},{5,1},{6,2},{7,3},{8,12},{9,13},{10,... | collective-permute-start | bytes 393224 | tf_op jit(solution)/shard_map/ppermute | solution.py:38
  26.2 0.0 collective-permute-start.13
  26.2 0.0 collective-permute-done.9
  26.2 0.8 %collective-permute-start.10 = (bf16[128,256]{1,0:T(8,128)(2,1)S(1)}, bf16[128,256]{1,0:T(8,128)(2,1)S(1)}, u32[]{:S(2)}, u32[]{:S(2)}) collective-permute-start(bf16[128,256]{1,0:T(8,128)(2,1)S(1)} %slice.22), channel_id=1, source_target_pairs={{0,8},{1,9},{2,10},{3,11},{4,12},{5,13},{6,14},{7,15},{8,0},{9,1},... | collective-permute-start | bytes 196616 | tf_op jit(solution)/shard_map/ppermute | solution.py:38
  27.0 1.0 %collective-permute-done.11.refs_0_ = bf16[128,512]{1,0:T(8,128)(2,1)S(1)} collective-permute-done((bf16[128,512]{1,0:T(8,128)(2,1)S(1)}, bf16[128,512]{1,0:T(8,128)(2,1)S(1)}, u32[]{:S(2)}, u32[]{:S(2)}) %collective-permute-start.11) | collective-permute-done | bytes 131104 | tf_op jit(solution)/shard_map/ppermute | solution.py:38
  28.0 3.9 %collective-permute-done.12.refs_1_ = bf16[128,512]{1,0:T(8,128)(2,1)S(1)} collective-permute-done((bf16[128,512]{1,0:T(8,128)(2,1)S(1)}, bf16[128,512]{1,0:T(8,128)(2,1)S(1)}, u32[]{:S(2)}, u32[]{:S(2)}) %collective-permute-start.12) | collective-permute-done | bytes 131104 | tf_op jit(solution)/shard_map/ppermute | solution.py:38
  31.9 2.2 %collective-permute-done.13.refs_2_ = bf16[128,512]{1,0:T(8,128)(2,1)S(1)} collective-permute-done((bf16[128,512]{1,0:T(8,128)(2,1)S(1)}, bf16[128,512]{1,0:T(8,128)(2,1)S(1)}, u32[]{:S(2)}, u32[]{:S(2)}) %collective-permute-start.13) | collective-permute-done | bytes 131104 | tf_op jit(solution)/shard_map/ppermute | solution.py:38
  34.1 0.0 collective-permute-done.10.dq_in
  34.2 0.7 %final.1 = (bf16[128,128]{1,0:T(8,128)(2,1)}, bf16[128,128]{1,0:T(8,128)(2,1)}, bf16[128,128]{1,0:T(8,128)(2,1)}, bf16[128,128]{1,0:T(8,128)(2,1)}, bf16[128,256]{1,0:T(8,128)(2,1)}) custom-call(f32[128,256]{1,0:T(8,128)S(1)} %slice.19.dq_ref, bf16[128,256]{1,0:T(8,128)(2,1)S(1)} %collective-permute-done.10.dq_in, f32[128,512]{1,0:T(8,128)S(1)} %get-tuple-element.34.own_ref, ...), custom_call_target="tpu_custom_call" | custom-call | tf_op jit(solution)/shard_map/final/pallas_call | solution.py:416
  (5 shorter events, 0.1 us)
Async XLA Ops:
  0.6 5.2 %copy-start = (bf16[2,32,2,256]{3,2,1,0:T(2,128)(2,1)S(1)}, bf16[2,32,2,256]{3,2,1,0:T(2,128)(2,1)}, u32[]{:S(2)}) copy-start(bf16[2,32,2,256]{3,2,1,0:T(2,128)(2,1)} %own_ref.1) | copy-start | bytes 196612
  1.7 7.4 %collective-permute-start = (bf16[128,256]{1,0:T(8,128)(2,1)S(1)}, bf16[128,256]{1,0:T(8,128)(2,1)S(1)}, u32[]{:S(2)}, u32[]{:S(2)}) collective-permute-start(bf16[128,256]{1,0:T(8,128)(2,1)S(1)} %get-tuple-element.26.refs_0_), channel_id=1, source_target_pairs={{0,8},{1,9},{2,10},{3,11},{4,12},{5,13},{6,14},{7,15},{8,0},{9,1},... | collective-permute-start | bytes 196616 | tf_op jit(solution)/shard_map/ppermute | solution.py:38
  5.9 4.3 %collective-permute-start.2 = (bf16[2,32,2,256]{3,2,1,0:T(2,128)(2,1)S(1)}, bf16[2,32,2,256]{3,2,1,0:T(2,128)(2,1)S(1)}, u32[]{:S(2)}, u32[]{:S(2)}) collective-permute-start(bf16[2,32,2,256]{3,2,1,0:T(2,128)(2,1)S(1)} %copy-done), channel_id=1, source_target_pairs={{0,16},{16,0},{1,17},{17,1},{2,18},{18,2},{3,19},{19,3},{4,20},{20... | collective-permute-start | bytes 196616 | tf_op jit(solution)/shard_map/ppermute | solution.py:298
  7.4 2.7 %copy-start.1 = (bf16[2,64,1,256]{3,1,2,0:T(8,128)(2,1)S(1)}, bf16[2,64,1,256]{3,1,2,0:T(8,128)(2,1)}, u32[]{:S(2)}) copy-start(bf16[2,64,1,256]{3,1,2,0:T(8,128)(2,1)} %param.17) | copy-start | bytes 196612
  7.4 2.7 %copy-start.2 = (bf16[2,64,1,256]{3,1,2,0:T(8,128)(2,1)S(1)}, bf16[2,64,1,256]{3,1,2,0:T(8,128)(2,1)}, u32[]{:S(2)}) copy-start(bf16[2,64,1,256]{3,1,2,0:T(8,128)(2,1)} %param.18) | copy-start | bytes 196612
  7.4 6.4 %collective-permute-start.6 = (bf16[128,512]{1,0:T(8,128)(2,1)S(1)}, bf16[128,512]{1,0:T(8,128)(2,1)S(1)}, u32[]{:S(2)}, u32[]{:S(2)}) collective-permute-start(bf16[128,512]{1,0:T(8,128)(2,1)S(1)} %get-tuple-element.28.refs_4_.refs_8_), channel_id=1, source_target_pairs={{0,4},{1,5},{2,6},{3,7},{4,0},{5,1},{6,2},{7,3},{8,12},{9,13},{10,... | collective-permute-start | bytes 393224 | tf_op jit(solution)/shard_map/ppermute | solution.py:38
  9.2 8.2 %collective-permute-start.1 = (bf16[256,256]{1,0:T(8,128)(2,1)S(1)}, bf16[256,256]{1,0:T(8,128)(2,1)S(1)}, u32[]{:S(2)}, u32[]{:S(2)}) collective-permute-start(bf16[256,256]{1,0:T(8,128)(2,1)S(1)} %pad_maximum_fusion), channel_id=1, source_target_pairs={{0,1},{1,0},{2,3},{3,2},{4,5},{5,4},{6,7},{7,6},{8,9},{9,8},{10,11... | collective-permute-start | bytes 393224 | tf_op jit(solution)/shard_map/ppermute | solution.py:38
  10.5 6.8 %collective-permute-start.4 = (bf16[136,256]{1,0:T(8,128)(2,1)S(1)}, bf16[136,256]{1,0:T(8,128)(2,1)S(1)}, u32[]{:S(2)}, u32[]{:S(2)}) collective-permute-start(bf16[136,256]{1,0:T(8,128)(2,1)S(1)} %grad_out.1.refs_2_.refs_4_), channel_id=1, source_target_pairs={{0,8},{1,9},{2,10},{3,11},{4,12},{5,13},{6,14},{7,15},{8,0},{9,1},... | collective-permute-start | bytes 208904 | tf_op jit(solution)/shard_map/ppermute | solution.py:38
  12.3 6.4 %collective-permute-start.7 = (bf16[128,512]{1,0:T(8,128)(2,1)S(1)}, bf16[128,512]{1,0:T(8,128)(2,1)S(1)}, u32[]{:S(2)}, u32[]{:S(2)}) collective-permute-start(bf16[128,512]{1,0:T(8,128)(2,1)S(1)} %get-tuple-element.28.refs_4_.refs_8_), channel_id=1, source_target_pairs={{0,2},{1,3},{2,0},{3,1},{4,6},{5,7},{6,4},{7,5},{8,10},{9,11},{10,... | collective-permute-start | bytes 393224 | tf_op jit(solution)/shard_map/ppermute | solution.py:38
  13.8 3.7 %collective-permute-start.3 = (bf16[136,256]{1,0:T(8,128)(2,1)S(1)}, bf16[136,256]{1,0:T(8,128)(2,1)S(1)}, u32[]{:S(2)}, u32[]{:S(2)}) collective-permute-start(bf16[136,256]{1,0:T(8,128)(2,1)S(1)} %grad_out.1.refs_2_.refs_4_), channel_id=1, source_target_pairs={{0,1},{1,0},{2,3},{3,2},{4,5},{5,4},{6,7},{7,6},{8,9},{9,8},{10,11... | collective-permute-start | bytes 208904 | tf_op jit(solution)/shard_map/ppermute | solution.py:38
  13.8 6.9 %collective-permute-start.8 = (bf16[128,512]{1,0:T(8,128)(2,1)S(1)}, bf16[128,512]{1,0:T(8,128)(2,1)S(1)}, u32[]{:S(2)}, u32[]{:S(2)}) collective-permute-start(bf16[128,512]{1,0:T(8,128)(2,1)S(1)} %collective-permute-done.6.refs_5_.refs_9_), channel_id=1, source_target_pairs={{0,2},{1,3},{2,0},{3,1},{4,6},{5,7},{6,4},{7,5},{8,10},{9,11},{10,... | collective-permute-start | bytes 393224 | tf_op jit(solution)/shard_map/ppermute | solution.py:38
  17.4 1.3 %collective-permute-start.5 = (bf16[136,256]{1,0:T(8,128)(2,1)S(1)}, bf16[136,256]{1,0:T(8,128)(2,1)S(1)}, u32[]{:S(2)}, u32[]{:S(2)}) collective-permute-start(bf16[136,256]{1,0:T(8,128)(2,1)S(1)} %collective-permute-done.4.refs_6_), channel_id=1, source_target_pairs={{0,1},{1,0},{2,3},{3,2},{4,5},{5,4},{6,7},{7,6},{8,9},{9,8},{10,11... | collective-permute-start | bytes 208904 | tf_op jit(solution)/shard_map/ppermute | solution.py:38
  22.0 4.2 %collective-permute-start.9 = (bf16[256,256]{1,0:T(8,128)(2,1)S(1)}, bf16[256,256]{1,0:T(8,128)(2,1)S(1)}, u32[]{:S(2)}, u32[]{:S(2)}) collective-permute-start(bf16[256,256]{1,0:T(8,128)(2,1)S(1)} %get-tuple-element.33), channel_id=1, source_target_pairs={{0,1},{1,0},{2,3},{3,2},{4,5},{5,4},{6,7},{7,6},{8,9},{9,8},{10,11... | collective-permute-start | bytes 393224 | tf_op jit(solution)/shard_map/ppermute | solution.py:38
  22.1 5.9 %collective-permute-start.11 = (bf16[128,512]{1,0:T(8,128)(2,1)S(1)}, bf16[128,512]{1,0:T(8,128)(2,1)S(1)}, u32[]{:S(2)}, u32[]{:S(2)}) collective-permute-start(bf16[128,512]{1,0:T(8,128)(2,1)S(1)} %get-tuple-element.35), channel_id=1, source_target_pairs={{0,2},{1,3},{2,0},{3,1},{4,6},{5,7},{6,4},{7,5},{8,10},{9,11},{10,... | collective-permute-start | bytes 393224 | tf_op jit(solution)/shard_map/ppermute | solution.py:38
  23.6 8.3 %collective-permute-start.12 = (bf16[128,512]{1,0:T(8,128)(2,1)S(1)}, bf16[128,512]{1,0:T(8,128)(2,1)S(1)}, u32[]{:S(2)}, u32[]{:S(2)}) collective-permute-start(bf16[128,512]{1,0:T(8,128)(2,1)S(1)} %get-tuple-element.36), channel_id=1, source_target_pairs={{0,4},{1,5},{2,6},{3,7},{4,0},{5,1},{6,2},{7,3},{8,12},{9,13},{10,... | collective-permute-start | bytes 393224 | tf_op jit(solution)/shard_map/ppermute | solution.py:38
  26.2 8.0 %collective-permute-start.13 = (bf16[128,512]{1,0:T(8,128)(2,1)S(1)}, bf16[128,512]{1,0:T(8,128)(2,1)S(1)}, u32[]{:S(2)}, u32[]{:S(2)}) collective-permute-start(bf16[128,512]{1,0:T(8,128)(2,1)S(1)} %get-tuple-element.37), channel_id=1, source_target_pairs={{0,6},{1,7},{2,4},{3,5},{4,2},{5,3},{6,0},{7,1},{8,14},{9,15},{10,... | collective-permute-start | bytes 393224 | tf_op jit(solution)/shard_map/ppermute | solution.py:38
  26.2 7.9 %collective-permute-start.10 = (bf16[128,256]{1,0:T(8,128)(2,1)S(1)}, bf16[128,256]{1,0:T(8,128)(2,1)S(1)}, u32[]{:S(2)}, u32[]{:S(2)}) collective-permute-start(bf16[128,256]{1,0:T(8,128)(2,1)S(1)} %slice.22), channel_id=1, source_target_pairs={{0,8},{1,9},{2,10},{3,11},{4,12},{5,13},{6,14},{7,15},{8,0},{9,1},... | collective-permute-start | bytes 196616 | tf_op jit(solution)/shard_map/ppermute | solution.py:38

commit v5 on v4

--- a/solution.py
+++ b/solution.py
@@ -226,21 +226,26 @@
     rows, kw = q_refs[0].shape[0], q_refs[0].shape[1] // 2
     edge = half * rows
     late = query_side(scale, lam[0], q_refs[half:], do_refs[half:], q_pos[:, edge:])
-    terms = tile_terms(late, k_refs, [key_rows(k_pos, place, rows) for place in places])
-    put_key_terms(dkv[:count], terms[:3], before)
-    late_sums = terms[3:]
-    whole = query_side(scale, lam[0], q_refs, do_refs, q_pos[...])
-    terms = tile_terms(whole, whole_refs, [key_rows(k_pos, place, rows) for place in whole_places])
-    put_key_terms(dkv[count:], terms[:3])
+    near = query_side(scale, lam[0], q_refs[:half], do_refs[:half], q_pos[:, :edge])
+    near_terms = tile_terms(near, whole_refs, [key_rows(k_pos, place, rows) for place in whole_places])
+    every = list(places) + list(whole_places)
+    terms = tile_terms(
+        late, list(k_refs) + list(whole_refs), [key_rows(k_pos, place, rows) for place in every]
+    )
+    put_key_terms(dkv[:count], [term[: count * rows] for term in terms[:3]], before)
+    put_key_terms(
+        dkv[count:], [term[count * rows :] + old for term, old in zip(terms[:3], near_terms[:3])]
+    )
+    late_sums, near_sums = terms[3:], near_terms[3:]
     for out, order in ((dq_keep, keep), (dq_send, sent)):
         for slot, i in enumerate(order):
             here = slice(slot * rows, (slot + 1) * rows)
             for n, side in enumerate((slice(0, kw), slice(kw, None))):
-                total = terms[3 + n][i * rows : (i + 1) * rows]
                 if i < half:
-                    total = total + dq_before[i * rows : (i + 1) * rows, side]
+                    mine = slice(i * rows, (i + 1) * rows)
+                    total = near_sums[n][mine] + dq_before[mine, side]
                 else:
-                    total = total + late_sums[n][i * rows - edge : (i + 1) * rows - edge]
+                    total = late_sums[n][i * rows - edge : (i + 1) * rows - edge]
                 out[here, side] = total.astype(out.dtype)
 
 

time: 35.1 us -> 35 us (level)
  no operation moved by 1% of the time
where the time goes in v5:
time: 35 us; the launch traced here: 34.8 us
  starting transfers between devices  16 us (46%)
  waiting for transfers between devices  13.4 us (38%)
  Pallas kernels  4.04 us (12%)
  between operations  1.38 us (4%)
    ppermute x13, starting transfers between devices, send(): lax.ppermute(member, 'blk', [(place, place ^ mask) for place in range(sha...  14.5 us
    ppermute x13, waiting for transfers between devices, send(): lax.ppermute(member, 'blk', [(place, place ^ mask) for place in range(sha...  13.2 us
    pallas_call x2, Pallas kernels, tile(): pl.pallas_call(kernel, out_shape=outs, in_specs=in_smem(1) + in_vmem(2 +...  1.83 us
    ppermute x1, starting transfers between devices, one_device(): other_half = lax.ppermute(cotangent, 'ulysses', [(0, 1), (1, 0)])  1.52 us
    pallas_call x1, Pallas kernels, one_device(): pl.pallas_call(functools.partial(prepare_kernel, block_len, q_masks, k_ma...  1.09 us
    pallas_call x1, Pallas kernels, one_device(): pl.pallas_call(functools.partial(final_kernel, scale, nk - 1), out_shape=...  0.72 us
  transfers between devices with their start and end apart: 14, of which 8 were waited for; matrix products, arithmetic and copies ran while one was open for 0% of the time, Pallas kernels for 3%

profile of v5, /device:TPU:0, one launch (start us, length us, event | category | flops | bytes accessed | tf_op | source)
XLA Modules:
  0.0 34.8 jit_solution(11195803027223473128)
XLA Ops:
  0.6 0.0 copy-start
  0.6 1.1 %prepare.1 = (bf16[128,512]{1,0:T(8,128)(2,1)S(1)}, bf16[128,256]{1,0:T(8,128)(2,1)S(1)}, f32[8,256]{1,0:T(8,128)S(1)}, s32[1,512]{1,0:T(1,128)S(1)}, s32[512,1]{1,0:T(8,128)S(1)}) custom-call(s32[1]{0:T(128)} %bitcast.me, bf16[128,128]{1,0:T(8,128)(2,1)} %bitcast.28, bf16[128,128]{1,0:T(8,128)(2,1)} %bitcast.29, bf16[128,256]{1,0:T(8,128)(2,1)} %bitcast.27, ...), custom_call_target="tpu_custom_call" | custom-call | tf_op jit(solution)/shard_map/prepare/pallas_call | solution.py:310
  1.7 4.1 %collective-permute-start = (bf16[128,256]{1,0:T(8,128)(2,1)S(1)}, bf16[128,256]{1,0:T(8,128)(2,1)S(1)}, u32[]{:S(2)}, u32[]{:S(2)}) collective-permute-start(bf16[128,256]{1,0:T(8,128)(2,1)S(1)} %get-tuple-element.26.refs_0_), channel_id=1, source_target_pairs={{0,8},{1,9},{2,10},{3,11},{4,12},{5,13},{6,14},{7,15},{8,0},{9,1},... | collective-permute-start | bytes 196616 | tf_op jit(solution)/shard_map/ppermute | solution.py:38
  5.9 0.0 copy-done
  5.9 1.5 %collective-permute-start.2 = (bf16[2,32,2,256]{3,2,1,0:T(2,128)(2,1)S(1)}, bf16[2,32,2,256]{3,2,1,0:T(2,128)(2,1)S(1)}, u32[]{:S(2)}, u32[]{:S(2)}) collective-permute-start(bf16[2,32,2,256]{3,2,1,0:T(2,128)(2,1)S(1)} %copy-done), channel_id=1, source_target_pairs={{0,16},{16,0},{1,17},{17,1},{2,18},{18,2},{3,19},{19,3},{4,20},{20... | collective-permute-start | bytes 196616 | tf_op jit(solution)/shard_map/ppermute | solution.py:303
  7.4 0.0 copy-start.1
  7.4 0.0 copy-start.2
  7.4 1.6 %collective-permute-start.6 = (bf16[128,512]{1,0:T(8,128)(2,1)S(1)}, bf16[128,512]{1,0:T(8,128)(2,1)S(1)}, u32[]{:S(2)}, u32[]{:S(2)}) collective-permute-start(bf16[128,512]{1,0:T(8,128)(2,1)S(1)} %get-tuple-element.28.refs_4_.refs_8_), channel_id=1, source_target_pairs={{0,4},{1,5},{2,6},{3,7},{4,0},{5,1},{6,2},{7,3},{8,12},{9,13},{10,... | collective-permute-start | bytes 393224 | tf_op jit(solution)/shard_map/ppermute | solution.py:38
  9.0 0.2 collective-permute-done.refs_2_
  9.2 0.1 collective-permute-start.1
  9.9 0.2 collective-permute-done.2.other_ref
  10.1 0.0 copy-done.1
  10.1 0.0 copy-done.2
  10.2 0.4 %grad_out.1.refs_2_.refs_4_ = bf16[136,256]{1,0:T(8,128)(2,1)S(1)} custom-call(s32[1]{0:T(128)} %bitcast.7.place, f32[1]{0:T(128)S(6)} %copy.22.lam, f32[8,256]{1,0:T(8,128)S(1)} %get-tuple-element.27.small, bf16[2,32,2,256]{3,2,1,0:T(2,128)(2,1)S(1)} %copy-done, bf16[2,32,2,256]{3,2,1,0:T(2,128)(2,1)S(1)} %collective-permute-done.2.other_ref, ...), custom_call_target="tpu_custom_call" | custom-call | tf_op jit(solution)/shard_map/grad_out/pallas_call | solution.py:359
  10.5 1.7 %collective-permute-start.4 = (bf16[136,256]{1,0:T(8,128)(2,1)S(1)}, bf16[136,256]{1,0:T(8,128)(2,1)S(1)}, u32[]{:S(2)}, u32[]{:S(2)}) collective-permute-start(bf16[136,256]{1,0:T(8,128)(2,1)S(1)} %grad_out.1.refs_2_.refs_4_), channel_id=1, source_target_pairs={{0,8},{1,9},{2,10},{3,11},{4,12},{5,13},{6,14},{7,15},{8,0},{9,1},... | collective-permute-start | bytes 208904 | tf_op jit(solution)/shard_map/ppermute | solution.py:38
  12.3 1.5 %collective-permute-start.7 = (bf16[128,512]{1,0:T(8,128)(2,1)S(1)}, bf16[128,512]{1,0:T(8,128)(2,1)S(1)}, u32[]{:S(2)}, u32[]{:S(2)}) collective-permute-start(bf16[128,512]{1,0:T(8,128)(2,1)S(1)} %get-tuple-element.28.refs_4_.refs_8_), channel_id=1, source_target_pairs={{0,2},{1,3},{2,0},{3,1},{4,6},{5,7},{6,4},{7,5},{8,10},{9,11},{10,... | collective-permute-start | bytes 393224 | tf_op jit(solution)/shard_map/ppermute | solution.py:38
  13.8 0.0 collective-permute-start.3
  13.8 0.0 collective-permute-done.6.refs_5_.refs_9_
  13.8 0.5 %collective-permute-start.8 = (bf16[128,512]{1,0:T(8,128)(2,1)S(1)}, bf16[128,512]{1,0:T(8,128)(2,1)S(1)}, u32[]{:S(2)}, u32[]{:S(2)}) collective-permute-start(bf16[128,512]{1,0:T(8,128)(2,1)S(1)} %collective-permute-done.6.refs_5_.refs_9_), channel_id=1, source_target_pairs={{0,2},{1,3},{2,0},{3,1},{4,6},{5,7},{6,4},{7,5},{8,10},{9,11},{10,... | collective-permute-start | bytes 393224 | tf_op jit(solution)/shard_map/ppermute | solution.py:38
  14.3 3.1 %collective-permute-done.4.refs_6_ = bf16[136,256]{1,0:T(8,128)(2,1)S(1)} collective-permute-done((bf16[136,256]{1,0:T(8,128)(2,1)S(1)}, bf16[136,256]{1,0:T(8,128)(2,1)S(1)}, u32[]{:S(2)}, u32[]{:S(2)}) %collective-permute-start.4) | collective-permute-done | bytes 69664 | tf_op jit(solution)/shard_map/ppermute | solution.py:38
  17.4 0.0 collective-permute-start.5
  17.4 0.0 collective-permute-done.1
  17.4 0.0 collective-permute-done.3.refs_3_.refs_5_
  17.4 0.6 %shard_map.155 = (f32[256,256]{1,0:T(8,128)S(1)}, f32[128,512]{1,0:T(8,128)S(1)}, f32[128,512]{1,0:T(8,128)S(1)}) custom-call(f32[1]{0:T(128)S(6)} %copy.22.lam, s32[1,512]{1,0:T(1,128)S(1)} %get-tuple-element.24.q_pos, s32[512,1]{1,0:T(8,128)S(1)} %get-tuple-element.25.k_pos, bf16[128,256]{1,0:T(8,128)(2,1)S(1)} %get-tuple-element.26.refs_0_, ...), custom_call_target="tpu_custom_call" | custom-call | tf_op jit(solution)/shard_map/pallas_call | solution.py:381
  18.0 0.6 %collective-permute-done.7.refs_10_ = bf16[128,512]{1,0:T(8,128)(2,1)S(1)} collective-permute-done((bf16[128,512]{1,0:T(8,128)(2,1)S(1)}, bf16[128,512]{1,0:T(8,128)(2,1)S(1)}, u32[]{:S(2)}, u32[]{:S(2)}) %collective-permute-start.7) | collective-permute-done | bytes 131104 | tf_op jit(solution)/shard_map/ppermute | solution.py:38
  18.6 0.0 collective-permute-done.5.refs_7_
  18.6 2.0 %collective-permute-done.8.refs_11_ = bf16[128,512]{1,0:T(8,128)(2,1)S(1)} collective-permute-done((bf16[128,512]{1,0:T(8,128)(2,1)S(1)}, bf16[128,512]{1,0:T(8,128)(2,1)S(1)}, u32[]{:S(2)}, u32[]{:S(2)}) %collective-permute-start.8) | collective-permute-done | bytes 131104 | tf_op jit(solution)/shard_map/ppermute | solution.py:38
  20.7 1.2 %shard_map.156 = (f32[256,256]{1,0:T(8,128)S(1)}, bf16[256,256]{1,0:T(8,128)(2,1)S(1)}, f32[128,512]{1,0:T(8,128)S(1)}, bf16[128,512]{1,0:T(8,128)(2,1)S(1)}, bf...) custom-call(f32[1]{0:T(128)S(6)} %copy.22.lam, s32[1,512]{1,0:T(1,128)S(1)} %get-tuple-element.24.q_pos, ...), custom_call_target="tpu_custom_call" | custom-call | tf_op jit(solution)/shard_map/pallas_call | solution.py:381
  21.9 0.1 collective-permute-start.9
  22.0 1.6 %collective-permute-start.11 = (bf16[128,512]{1,0:T(8,128)(2,1)S(1)}, bf16[128,512]{1,0:T(8,128)(2,1)S(1)}, u32[]{:S(2)}, u32[]{:S(2)}) collective-permute-start(bf16[128,512]{1,0:T(8,128)(2,1)S(1)} %get-tuple-element.35), channel_id=1, source_target_pairs={{0,2},{1,3},{2,0},{3,1},{4,6},{5,7},{6,4},{7,5},{8,10},{9,11},{10,... | collective-permute-start | bytes 393224 | tf_op jit(solution)/shard_map/ppermute | solution.py:38
  23.6 2.5 %collective-permute-start.12 = (bf16[128,512]{1,0:T(8,128)(2,1)S(1)}, bf16[128,512]{1,0:T(8,128)(2,1)S(1)}, u32[]{:S(2)}, u32[]{:S(2)}) collective-permute-start(bf16[128,512]{1,0:T(8,128)(2,1)S(1)} %get-tuple-element.36), channel_id=1, source_target_pairs={{0,4},{1,5},{2,6},{3,7},{4,0},{5,1},{6,2},{7,3},{8,12},{9,13},{10,... | collective-permute-start | bytes 393224 | tf_op jit(solution)/shard_map/ppermute | solution.py:38
  26.1 0.0 collective-permute-start.13
  26.1 0.0 collective-permute-done.9
  26.2 0.8 %collective-permute-start.10 = (bf16[128,256]{1,0:T(8,128)(2,1)S(1)}, bf16[128,256]{1,0:T(8,128)(2,1)S(1)}, u32[]{:S(2)}, u32[]{:S(2)}) collective-permute-start(bf16[128,256]{1,0:T(8,128)(2,1)S(1)} %slice.22), channel_id=1, source_target_pairs={{0,8},{1,9},{2,10},{3,11},{4,12},{5,13},{6,14},{7,15},{8,0},{9,1},... | collective-permute-start | bytes 196616 | tf_op jit(solution)/shard_map/ppermute | solution.py:38
  27.0 1.0 %collective-permute-done.11.refs_0_ = bf16[128,512]{1,0:T(8,128)(2,1)S(1)} collective-permute-done((bf16[128,512]{1,0:T(8,128)(2,1)S(1)}, bf16[128,512]{1,0:T(8,128)(2,1)S(1)}, u32[]{:S(2)}, u32[]{:S(2)}) %collective-permute-start.11) | collective-permute-done | bytes 131104 | tf_op jit(solution)/shard_map/ppermute | solution.py:38
  27.9 3.9 %collective-permute-done.12.refs_1_ = bf16[128,512]{1,0:T(8,128)(2,1)S(1)} collective-permute-done((bf16[128,512]{1,0:T(8,128)(2,1)S(1)}, bf16[128,512]{1,0:T(8,128)(2,1)S(1)}, u32[]{:S(2)}, u32[]{:S(2)}) %collective-permute-start.12) | collective-permute-done | bytes 131104 | tf_op jit(solution)/shard_map/ppermute | solution.py:38
  31.9 2.2 %collective-permute-done.13.refs_2_ = bf16[128,512]{1,0:T(8,128)(2,1)S(1)} collective-permute-done((bf16[128,512]{1,0:T(8,128)(2,1)S(1)}, bf16[128,512]{1,0:T(8,128)(2,1)S(1)}, u32[]{:S(2)}, u32[]{:S(2)}) %collective-permute-start.13) | collective-permute-done | bytes 131104 | tf_op jit(solution)/shard_map/ppermute | solution.py:38
  34.1 0.0 collective-permute-done.10.dq_in
  34.1 0.7 %final.1 = (bf16[128,128]{1,0:T(8,128)(2,1)}, bf16[128,128]{1,0:T(8,128)(2,1)}, bf16[128,128]{1,0:T(8,128)(2,1)}, bf16[128,128]{1,0:T(8,128)(2,1)}, bf16[128,256]{1,0:T(8,128)(2,1)}) custom-call(f32[128,256]{1,0:T(8,128)S(1)} %slice.19.dq_ref, bf16[128,256]{1,0:T(8,128)(2,1)S(1)} %collective-permute-done.10.dq_in, f32[128,512]{1,0:T(8,128)S(1)} %get-tuple-element.34.own_ref, ...), custom_call_target="tpu_custom_call" | custom-call | tf_op jit(solution)/shard_map/final/pallas_call | solution.py:421
  (5 shorter events, 0.1 us)
Async XLA Ops:
  0.6 5.2 %copy-start = (bf16[2,32,2,256]{3,2,1,0:T(2,128)(2,1)S(1)}, bf16[2,32,2,256]{3,2,1,0:T(2,128)(2,1)}, u32[]{:S(2)}) copy-start(bf16[2,32,2,256]{3,2,1,0:T(2,128)(2,1)} %own_ref.1) | copy-start | bytes 196612
  1.7 7.4 %collective-permute-start = (bf16[128,256]{1,0:T(8,128)(2,1)S(1)}, bf16[128,256]{1,0:T(8,128)(2,1)S(1)}, u32[]{:S(2)}, u32[]{:S(2)}) collective-permute-start(bf16[128,256]{1,0:T(8,128)(2,1)S(1)} %get-tuple-element.26.refs_0_), channel_id=1, source_target_pairs={{0,8},{1,9},{2,10},{3,11},{4,12},{5,13},{6,14},{7,15},{8,0},{9,1},... | collective-permute-start | bytes 196616 | tf_op jit(solution)/shard_map/ppermute | solution.py:38
  5.9 4.3 %collective-permute-start.2 = (bf16[2,32,2,256]{3,2,1,0:T(2,128)(2,1)S(1)}, bf16[2,32,2,256]{3,2,1,0:T(2,128)(2,1)S(1)}, u32[]{:S(2)}, u32[]{:S(2)}) collective-permute-start(bf16[2,32,2,256]{3,2,1,0:T(2,128)(2,1)S(1)} %copy-done), channel_id=1, source_target_pairs={{0,16},{16,0},{1,17},{17,1},{2,18},{18,2},{3,19},{19,3},{4,20},{20... | collective-permute-start | bytes 196616 | tf_op jit(solution)/shard_map/ppermute | solution.py:303
  7.4 2.7 %copy-start.1 = (bf16[2,64,1,256]{3,1,2,0:T(8,128)(2,1)S(1)}, bf16[2,64,1,256]{3,1,2,0:T(8,128)(2,1)}, u32[]{:S(2)}) copy-start(bf16[2,64,1,256]{3,1,2,0:T(8,128)(2,1)} %param.17) | copy-start | bytes 196612
  7.4 2.7 %copy-start.2 = (bf16[2,64,1,256]{3,1,2,0:T(8,128)(2,1)S(1)}, bf16[2,64,1,256]{3,1,2,0:T(8,128)(2,1)}, u32[]{:S(2)}) copy-start(bf16[2,64,1,256]{3,1,2,0:T(8,128)(2,1)} %param.18) | copy-start | bytes 196612
  7.4 6.4 %collective-permute-start.6 = (bf16[128,512]{1,0:T(8,128)(2,1)S(1)}, bf16[128,512]{1,0:T(8,128)(2,1)S(1)}, u32[]{:S(2)}, u32[]{:S(2)}) collective-permute-start(bf16[128,512]{1,0:T(8,128)(2,1)S(1)} %get-tuple-element.28.refs_4_.refs_8_), channel_id=1, source_target_pairs={{0,4},{1,5},{2,6},{3,7},{4,0},{5,1},{6,2},{7,3},{8,12},{9,13},{10,... | collective-permute-start | bytes 393224 | tf_op jit(solution)/shard_map/ppermute | solution.py:38
  9.2 8.2 %collective-permute-start.1 = (bf16[256,256]{1,0:T(8,128)(2,1)S(1)}, bf16[256,256]{1,0:T(8,128)(2,1)S(1)}, u32[]{:S(2)}, u32[]{:S(2)}) collective-permute-start(bf16[256,256]{1,0:T(8,128)(2,1)S(1)} %pad_maximum_fusion), channel_id=1, source_target_pairs={{0,1},{1,0},{2,3},{3,2},{4,5},{5,4},{6,7},{7,6},{8,9},{9,8},{10,11... | collective-permute-start | bytes 393224 | tf_op jit(solution)/shard_map/ppermute | solution.py:38
  10.5 6.8 %collective-permute-start.4 = (bf16[136,256]{1,0:T(8,128)(2,1)S(1)}, bf16[136,256]{1,0:T(8,128)(2,1)S(1)}, u32[]{:S(2)}, u32[]{:S(2)}) collective-permute-start(bf16[136,256]{1,0:T(8,128)(2,1)S(1)} %grad_out.1.refs_2_.refs_4_), channel_id=1, source_target_pairs={{0,8},{1,9},{2,10},{3,11},{4,12},{5,13},{6,14},{7,15},{8,0},{9,1},... | collective-permute-start | bytes 208904 | tf_op jit(solution)/shard_map/ppermute | solution.py:38
  12.3 6.4 %collective-permute-start.7 = (bf16[128,512]{1,0:T(8,128)(2,1)S(1)}, bf16[128,512]{1,0:T(8,128)(2,1)S(1)}, u32[]{:S(2)}, u32[]{:S(2)}) collective-permute-start(bf16[128,512]{1,0:T(8,128)(2,1)S(1)} %get-tuple-element.28.refs_4_.refs_8_), channel_id=1, source_target_pairs={{0,2},{1,3},{2,0},{3,1},{4,6},{5,7},{6,4},{7,5},{8,10},{9,11},{10,... | collective-permute-start | bytes 393224 | tf_op jit(solution)/shard_map/ppermute | solution.py:38
  13.8 3.7 %collective-permute-start.3 = (bf16[136,256]{1,0:T(8,128)(2,1)S(1)}, bf16[136,256]{1,0:T(8,128)(2,1)S(1)}, u32[]{:S(2)}, u32[]{:S(2)}) collective-permute-start(bf16[136,256]{1,0:T(8,128)(2,1)S(1)} %grad_out.1.refs_2_.refs_4_), channel_id=1, source_target_pairs={{0,1},{1,0},{2,3},{3,2},{4,5},{5,4},{6,7},{7,6},{8,9},{9,8},{10,11... | collective-permute-start | bytes 208904 | tf_op jit(solution)/shard_map/ppermute | solution.py:38
  13.8 6.9 %collective-permute-start.8 = (bf16[128,512]{1,0:T(8,128)(2,1)S(1)}, bf16[128,512]{1,0:T(8,128)(2,1)S(1)}, u32[]{:S(2)}, u32[]{:S(2)}) collective-permute-start(bf16[128,512]{1,0:T(8,128)(2,1)S(1)} %collective-permute-done.6.refs_5_.refs_9_), channel_id=1, source_target_pairs={{0,2},{1,3},{2,0},{3,1},{4,6},{5,7},{6,4},{7,5},{8,10},{9,11},{10,... | collective-permute-start | bytes 393224 | tf_op jit(solution)/shard_map/ppermute | solution.py:38
  17.4 1.3 %collective-permute-start.5 = (bf16[136,256]{1,0:T(8,128)(2,1)S(1)}, bf16[136,256]{1,0:T(8,128)(2,1)S(1)}, u32[]{:S(2)}, u32[]{:S(2)}) collective-permute-start(bf16[136,256]{1,0:T(8,128)(2,1)S(1)} %collective-permute-done.4.refs_6_), channel_id=1, source_target_pairs={{0,1},{1,0},{2,3},{3,2},{4,5},{5,4},{6,7},{7,6},{8,9},{9,8},{10,11... | collective-permute-start | bytes 208904 | tf_op jit(solution)/shard_map/ppermute | solution.py:38
  21.9 4.2 %collective-permute-start.9 = (bf16[256,256]{1,0:T(8,128)(2,1)S(1)}, bf16[256,256]{1,0:T(8,128)(2,1)S(1)}, u32[]{:S(2)}, u32[]{:S(2)}) collective-permute-start(bf16[256,256]{1,0:T(8,128)(2,1)S(1)} %get-tuple-element.33), channel_id=1, source_target_pairs={{0,1},{1,0},{2,3},{3,2},{4,5},{5,4},{6,7},{7,6},{8,9},{9,8},{10,11... | collective-permute-start | bytes 393224 | tf_op jit(solution)/shard_map/ppermute | solution.py:38
  22.0 5.9 %collective-permute-start.11 = (bf16[128,512]{1,0:T(8,128)(2,1)S(1)}, bf16[128,512]{1,0:T(8,128)(2,1)S(1)}, u32[]{:S(2)}, u32[]{:S(2)}) collective-permute-start(bf16[128,512]{1,0:T(8,128)(2,1)S(1)} %get-tuple-element.35), channel_id=1, source_target_pairs={{0,2},{1,3},{2,0},{3,1},{4,6},{5,7},{6,4},{7,5},{8,10},{9,11},{10,... | collective-permute-start | bytes 393224 | tf_op jit(solution)/shard_map/ppermute | solution.py:38
  23.6 8.3 %collective-permute-start.12 = (bf16[128,512]{1,0:T(8,128)(2,1)S(1)}, bf16[128,512]{1,0:T(8,128)(2,1)S(1)}, u32[]{:S(2)}, u32[]{:S(2)}) collective-permute-start(bf16[128,512]{1,0:T(8,128)(2,1)S(1)} %get-tuple-element.36), channel_id=1, source_target_pairs={{0,4},{1,5},{2,6},{3,7},{4,0},{5,1},{6,2},{7,3},{8,12},{9,13},{10,... | collective-permute-start | bytes 393224 | tf_op jit(solution)/shard_map/ppermute | solution.py:38
  26.1 8.0 %collective-permute-start.13 = (bf16[128,512]{1,0:T(8,128)(2,1)S(1)}, bf16[128,512]{1,0:T(8,128)(2,1)S(1)}, u32[]{:S(2)}, u32[]{:S(2)}) collective-permute-start(bf16[128,512]{1,0:T(8,128)(2,1)S(1)} %get-tuple-element.37), channel_id=1, source_target_pairs={{0,6},{1,7},{2,4},{3,5},{4,2},{5,3},{6,0},{7,1},{8,14},{9,15},{10,... | collective-permute-start | bytes 393224 | tf_op jit(solution)/shard_map/ppermute | solution.py:38
  26.2 7.9 %collective-permute-start.10 = (bf16[128,256]{1,0:T(8,128)(2,1)S(1)}, bf16[128,256]{1,0:T(8,128)(2,1)S(1)}, u32[]{:S(2)}, u32[]{:S(2)}) collective-permute-start(bf16[128,256]{1,0:T(8,128)(2,1)S(1)} %slice.22), channel_id=1, source_target_pairs={{0,8},{1,9},{2,10},{3,11},{4,12},{5,13},{6,14},{7,15},{8,0},{9,1},... | collective-permute-start | bytes 196616 | tf_op jit(solution)/shard_map/ppermute | solution.py:38
